TPU v7x, 256 devices: a whole 4x4x8 slice. The times are simulated.
256 devices in a mesh: ctx: 16 (over y, x), tp: 16 (over z, core).
Axes of the slice: x: 4, y: 4, z: 8, core: 2. Of those that a mesh axis runs over, the one named last changes fastest.
Arguments:
- queries: bfloat16 [3584, 8192], P('ctx', 'tp'), may hold values from -8 to 8
- keys: bfloat16 [3584, 1024], P('ctx'), may hold values from -8 to 8
- values: bfloat16 [3584, 1024], P('ctx'), may hold values from -32 to 32
- out_weight: bfloat16 [8192, 8192], P('tp'), may hold values from -0.09375 to 0.09375
- signs: int32 [8192], replicated, may hold values from 0 to 1
Outputs:
- rotated_payload: bfloat16 [3584, 8192], P('ctx')
- block_scales: float32 [3584, 64], P('ctx')
All inputs are finite; a program needn't handle non-finite values. Where the computation divides by a largest or mean magnitude, that divisor is 1e-20 or more.
Results may differ from a plain program's by a relative error of at most 0.0095.
Values may be sent and summed in bfloat16 or wider, within the bound.
No kernel may reach another device: no remote copies, remote signals or barrier semaphores. Data moves between devices by JAX's collectives and lax.ppermute only.
A program may use at most 128 MiB of HBM per device.

v0:
```python
import functools
import math

import jax
import jax.numpy as jnp
import numpy as np
from jax import lax
from jax.experimental import pallas as pl
from jax.experimental.pallas import tpu as pltpu
from jax.sharding import PartitionSpec as P


D = 8192
HEAD = 128
BLOCK = 128
CHIPS = 8
TOKENS = 224
HEADS = 4
WIDTH = HEADS * HEAD
KEYS = 3584
KEY_BLOCK = 896
CHUNK = D // CHIPS
SHARE = CHUNK // 2
COLS = SHARE // 2
SUB = COLS // BLOCK
ROWS = SUB * TOKENS
MSG = ROWS + 16

UP = [(t, (t + 2) % 16) for t in range(16)]
DOWN = [(t, (t - 2) % 16) for t in range(16)]
PAIR = [(t, t ^ 1) for t in range(16)]

SIDE = 4


def torus_pairs(axis_of_core, step):
    pairs = []
    for c in range(SIDE * SIDE):
        for t in range(16):
            y, x = divmod(c, SIDE)
            if axis_of_core[t % 2] == "x":
                x = (x + step) % SIDE
            else:
                y = (y + step) % SIDE
            pairs.append((c * 16 + t, (y * SIDE + x) * 16 + t))
    return pairs


FIRST = torus_pairs("xy", 1), torus_pairs("xy", -1)
SECOND = torus_pairs("yx", 1), torus_pairs("yx", -1)


def turn_matrix():
    common = np.arange(BLOCK)[:, None] & np.arange(BLOCK)[None, :]
    parity = np.zeros((BLOCK, BLOCK), np.int64)
    for bit in range(BLOCK.bit_length() - 1):
        parity += (common >> bit) & 1
    return np.kron(np.eye(2), 1 - 2 * (parity % 2)).astype(np.float32)


def spread_matrix():
    row, column = np.arange(BLOCK)[:, None], np.arange(COLS)[None, :]
    return ((row % SUB == column // BLOCK) & (row < 2 * SUB)).astype(np.float32)


def clipped_partial(pairs, signs, turn_ref, spread_ref):
    flat = jnp.concatenate(
        [
            (jnp.dot(rows, weight, preferred_element_type=jnp.float32) * signs).astype(jnp.bfloat16)
            for rows, weight in pairs
        ],
        0,
    )
    squares = lax.dot_general(
        flat * flat, spread_ref[...], (((1,), (1,)), ((), ())), preferred_element_type=jnp.float32
    )
    limit = 2.0 * jnp.sqrt(squares + BLOCK * 1e-06)
    upper = limit.astype(jnp.bfloat16).astype(jnp.float32)
    lane = lax.broadcasted_iota(jnp.int32, limit.shape, 1)
    limit = jnp.where(lane < SUB, upper, limit - upper).astype(jnp.bfloat16)
    limit = jnp.dot(limit, spread_ref[...], preferred_element_type=jnp.float32)
    turned = jnp.dot(flat, turn_ref[...], preferred_element_type=jnp.float32)
    clipped = jnp.minimum(jnp.maximum(turned, -limit), limit)
    return clipped[:TOKENS] + clipped[TOKENS:]


GROUP = HEADS // 2 * TOKENS
LANES = KEY_BLOCK // 128


def attention_kernel(place_ref, query_hbm, held_ref, swapped_ref, o_ref, key, wide, scores, query_ref, sem):
    first, core, y, x = place_ref[0], place_ref[1], place_ref[3], place_ref[4]
    fetch = pltpu.make_async_copy(query_hbm, query_ref, sem)
    fetch.start()
    blocks = (first + TOKENS - 1) // KEY_BLOCK + 1
    gain = math.log2(math.e) / math.sqrt(HEAD)

    def sort(keys_ref, values_ref):
        @pl.loop(0, SIDE * SIDE)
        def _(n):
            far, near = (
                jnp.where(i == 1, SIDE - 1, jnp.maximum(i - 1, 0)) for i in (n // SIDE, lax.rem(n, SIDE))
            )
            block = pl.multiple_of(n * TOKENS, 32)
            row, column = lax.rem(y + far, SIDE), lax.rem(x + near, SIDE)
            start = pl.multiple_of((row * SIDE + column) * TOKENS, 32)
            key[pl.ds(start, TOKENS), :] = keys_ref[pl.ds(block, TOKENS), :]
            row, column = lax.rem(y + near, SIDE), lax.rem(x + far, SIDE)
            start = pl.multiple_of((row * SIDE + column) * TOKENS, 32)
            wide[pl.ds(start, TOKENS), :HEAD] = values_ref[pl.ds(block, TOKENS), :]

    @pl.when(core == 0)
    def _():
        sort(held_ref, swapped_ref)

    @pl.when(core != 0)
    def _():
        sort(swapped_ref, held_ref)

    wide[:, HEAD:] = jnp.ones((KEYS, HEAD), jnp.bfloat16)
    fetch.wait()
    query_pos = first + lax.rem(
        lax.broadcasted_iota(jnp.int32, (GROUP, 128), 0), TOKENS
    )
    key_pos = lax.broadcasted_iota(jnp.int32, (GROUP, 128), 1)
    rows = [
        jnp.concatenate([query_ref[:, h * HEAD : (h + 1) * HEAD] for h in (2 * g, 2 * g + 1)], 0)
        for g in range(2)
    ]

    def score(j, best, masked):
        start = pl.multiple_of(j * KEY_BLOCK, 128)
        result = []
        for group in range(2):
            part = lax.dot_general(
                rows[group],
                key[pl.ds(start, KEY_BLOCK), :],
                (((1,), (1,)), ((), ())),
                preferred_element_type=jnp.float32,
            )
            top = best[group]
            for t in range(LANES):
                piece = part[:, t * 128 : (t + 1) * 128]
                if masked:
                    piece = jnp.where(key_pos <= query_pos - (start + t * 128), piece, -1e30)
                scores[group, j, :, t * 128 : (t + 1) * 128] = piece
                top = jnp.maximum(top, piece)
            result.append(top)
        return tuple(result)

    low = jnp.full((GROUP, 128), -1e30, jnp.float32)

    best = lax.fori_loop(0, blocks, lambda j, b: score(j, b, True), (low, low))
    tops = [jnp.broadcast_to(jnp.max(b, axis=-1, keepdims=True), (GROUP, 128)) for b in best]

    def mix(j, totals):
        start = pl.multiple_of(j * KEY_BLOCK, 128)
        result = []
        for group in range(2):
            weights = jnp.concatenate(
                [
                    jnp.exp2((scores[group, j, :, t * 128 : (t + 1) * 128] - tops[group]) * gain).astype(
                        jnp.bfloat16
                    )
                    for t in range(LANES)
                ],
                1,
            )
            result.append(
                totals[group]
                + jnp.dot(
                    weights, wide[pl.ds(start, KEY_BLOCK), :], preferred_element_type=jnp.float32
                )
            )
        return tuple(result)

    none = jnp.zeros((GROUP, 2 * HEAD), jnp.float32)
    totals = lax.fori_loop(0, blocks, mix, (none, none))
    for group in range(2):
        normed = (totals[group][:, :HEAD] / totals[group][:, HEAD:]).astype(jnp.bfloat16)
        for h in range(2):
            column = (2 * group + h) * HEAD
            o_ref[:, column : column + HEAD] = normed[h * TOKENS : (h + 1) * TOKENS]


VMEM = pl.BlockSpec(memory_space=pltpu.VMEM)
SMEM = pl.BlockSpec(memory_space=pltpu.SMEM)
ANY = pl.BlockSpec(memory_space=pl.ANY)


HBM = pl.BlockSpec(memory_space=pltpu.HBM)


def attention(place, queries, held, swapped):
    return pl.pallas_call(
        attention_kernel,
        out_shape=jax.ShapeDtypeStruct((TOKENS, WIDTH), jnp.bfloat16),
        in_specs=[SMEM, HBM, VMEM, VMEM],
        out_specs=VMEM,
        scratch_shapes=[
            pltpu.VMEM((KEYS, HEAD), jnp.bfloat16),
            pltpu.VMEM((KEYS, 2 * HEAD), jnp.bfloat16),
            pltpu.VMEM((2, KEYS // KEY_BLOCK, GROUP, KEY_BLOCK), jnp.float32),
            pltpu.VMEM((TOKENS, WIDTH), jnp.bfloat16),
            pltpu.SemaphoreType.DMA,
        ],
        compiler_params=pltpu.CompilerParams(vmem_limit_bytes=30 << 20),
        cost_estimate=pl.CostEstimate(
            flops=8 * GROUP * KEYS * HEAD, bytes_accessed=3 << 20, transcendentals=2 * GROUP * KEYS
        ),
        name="attend",
    )(place, queries, held, swapped)


def project_kernel(
    place_ref, mine_ref, theirs_ref, own_hbm, other_hbm, sign_ref, turn_ref, spread_ref, *refs
):
    o_refs, (own, other, sems) = refs[: 2 * CHIPS], refs[2 * CHIPS :]
    core, chip = place_ref[1], place_ref[2]

    def column(step):
        distance = 4 - (step + 1) // 2
        offset = jnp.where(lax.rem(step, 2) == 0, -distance, distance)
        return lax.rem(chip + offset + CHIPS, CHIPS) * CHUNK + core * SHARE

    def fetches(step):
        start = pl.multiple_of(column(step), SHARE)
        return [
            pltpu.make_async_copy(
                source.at[:, pl.ds(start, SHARE)], target.at[step], sems.at[n, step]
            )
            for n, (source, target) in enumerate(((own_hbm, own), (other_hbm, other)))
        ]

    @pl.loop(0, CHIPS)
    def _(step):
        for fetch in fetches(step):
            fetch.start()

    @pl.loop(0, CHIPS)
    def _(step):
        for fetch in fetches(step):
            fetch.wait()
        start = pl.multiple_of(column(step), SHARE)
        totals = []
        for half in range(2):
            columns = slice(half * COLS, (half + 1) * COLS)
            signs = (2 * sign_ref[:, pl.ds(start + half * COLS, COLS)] - 1).astype(jnp.float32)
            totals.append(
                clipped_partial(
                    ((mine_ref[...], own[step, :, columns]), (theirs_ref[...], other[step, :, columns])),
                    signs,
                    turn_ref,
                    spread_ref,
                )
            )
        for n in range(CHIPS):

            @pl.when(step == n)
            def _(n=n):
                for half in range(2):
                    o_ref = o_refs[2 * n + half]
                    for b in range(SUB):
                        piece = totals[half][:, b * BLOCK : (b + 1) * BLOCK]
                        o_ref[b * TOKENS : (b + 1) * TOKENS, :] = piece.astype(o_ref.dtype)


def project(place, mine, theirs, own, other, signs, turn, spread):
    half = jax.ShapeDtypeStruct((ROWS, BLOCK), jnp.bfloat16)
    full = jax.ShapeDtypeStruct((ROWS, BLOCK), jnp.float32)
    return pl.pallas_call(
        project_kernel,
        out_shape=(half,) * (2 * CHIPS - 2) + (full,) * 2,
        in_specs=[SMEM, VMEM, VMEM, HBM, HBM, VMEM, VMEM, VMEM],
        out_specs=(VMEM,) * (2 * CHIPS),
        scratch_shapes=[
            pltpu.VMEM((CHIPS, WIDTH, SHARE), jnp.bfloat16),
            pltpu.VMEM((CHIPS, WIDTH, SHARE), jnp.bfloat16),
            pltpu.SemaphoreType.DMA((2, CHIPS)),
        ],
        compiler_params=pltpu.CompilerParams(vmem_limit_bytes=50 << 20),
        cost_estimate=pl.CostEstimate(
            flops=2 * TOKENS * 1280 * D // 2, bytes_accessed=10 << 20, transcendentals=0
        ),
        name="project",
    )(place, mine, theirs, own, other, signs, turn, spread)


def pack_kernel(own0, own1, up0, up1, down0, down1, o0_ref, o1_ref, square):
    for own, up, down, out in ((own0, up0, down0, o0_ref), (own1, up1, down1, o1_ref)):
        lane = lax.broadcasted_iota(jnp.int32, (TOKENS, BLOCK), 1)
        columns = jnp.zeros((TOKENS, BLOCK), jnp.float32)
        for b in range(SUB):
            rows = slice(b * TOKENS, (b + 1) * TOKENS)
            came = up[rows, :].astype(jnp.float32) + down[rows, :].astype(jnp.float32)
            summed = (own[rows, :] + came) * (1.0 / math.sqrt(BLOCK))
            scale = jnp.max(jnp.abs(summed), axis=-1, keepdims=True) + 1e-06
            out[rows, :] = (summed / scale).astype(jnp.bfloat16)
            columns = jnp.where(lane == b, scale, columns)
        square[...] = jnp.zeros((2 * BLOCK, BLOCK), jnp.float32)
        square[:TOKENS, :] = columns
        turned = jnp.concatenate(
            [square[:BLOCK, :].T[:SUB, :], square[BLOCK:, :].T[:SUB, :]], 0
        )
        upper = turned.astype(jnp.bfloat16).astype(jnp.float32)
        tail = jnp.concatenate([upper, turned - upper, jnp.zeros((8, BLOCK), jnp.float32)], 0)
        out[ROWS:, :] = tail.astype(jnp.bfloat16)


def pack(own, up, down):
    shape = jax.ShapeDtypeStruct((MSG, BLOCK), jnp.bfloat16)
    return pl.pallas_call(
        pack_kernel,
        out_shape=(shape, shape),
        in_specs=[VMEM] * 6,
        out_specs=(VMEM, VMEM),
        scratch_shapes=[pltpu.VMEM((2 * BLOCK, BLOCK), jnp.float32)],
        compiler_params=pltpu.CompilerParams(vmem_limit_bytes=8 << 20),
        cost_estimate=pl.CostEstimate(flops=1 << 20, bytes_accessed=1 << 20, transcendentals=0),
        name="pack",
    )(*own, *up, *down)


def assemble_kernel(places, fresh, last, index_ref, *refs):
    count = 1 + max(place[0] for place in places)
    arrays, refs = refs[:count], refs[count:]
    joined = []
    if fresh:
        out_ref, table, joined_ref, tails, sems, tail_sems, join_sems = refs
        for n in range(count):
            joined.append(
                pltpu.make_async_copy(
                    arrays[n], joined_ref.at[pl.ds(n * MSG, MSG), :], join_sems.at[n]
                )
            )
            joined[-1].start()
    else:
        _, old_table, out_ref, table, tails, sems, tail_sems = refs[:7]
        if last:
            _, _, out_ref, scale_ref, table, tails, sems, tail_sems = refs
        table[...] = old_table[...]
    core, chip = index_ref[0], index_ref[1]

    def spot(swap, offset):
        side = (1 - core) if swap else core
        return side, lax.rem(chip + offset + CHIPS, CHIPS)

    copies, tail_copies = [], []
    for n, (array, row, swap, offset, half) in enumerate(places):
        tail_copies.append(
            pltpu.make_async_copy(
                arrays[array].at[pl.ds(row + ROWS, 16), :], tails.at[n], tail_sems.at[n]
            )
        )
        tail_copies[-1].start()
    for n, (array, row, swap, offset, half) in enumerate(places):
        side, place = spot(swap, offset)
        for b in range(SUB):
            column = pl.multiple_of(place * CHUNK + side * SHARE + half * COLS + b * BLOCK, BLOCK)
            copies.append(
                pltpu.make_async_copy(
                    arrays[array].at[pl.ds(row + b * TOKENS, TOKENS), :],
                    out_ref.at[:, pl.ds(column, BLOCK)],
                    sems.at[n * SUB + b],
                )
            )
            copies[-1].start()
    for n, (array, row, swap, offset, half) in enumerate(places):
        tail_copies[n].wait()
        side, place = spot(swap, offset)
        tail = tails[n].astype(jnp.float32)
        tail = tail[: 2 * SUB] + tail[2 * SUB : 4 * SUB]
        for t in range(2):
            table[place, side, half * SUB : (half + 1) * SUB, t * BLOCK : (t + 1) * BLOCK] = tail[
                t * SUB : (t + 1) * SUB
            ]
    if last:
        for place in range(CHIPS):
            for side in range(2):
                row = (2 * place + side) * 2 * SUB
                scale_ref[row : row + 2 * SUB, :] = table[place, side][:, :TOKENS]
    for copy in joined + copies:
        copy.wait()


def assemble(index, arrays, places, before, last):
    table_shape = (CHIPS, 2, 2 * SUB, 2 * BLOCK)
    out_shape = [jax.ShapeDtypeStruct((TOKENS, D), jnp.bfloat16)]
    out_shape.append(
        jax.ShapeDtypeStruct((D // BLOCK, TOKENS) if last else table_shape, jnp.float32)
    )
    scratch = [pltpu.VMEM(table_shape, jnp.float32)] if last else []
    fresh = before is None
    out_specs, more = [ANY, VMEM], []
    if fresh:
        out_shape.append(jax.ShapeDtypeStruct((len(arrays) * MSG, BLOCK), jnp.bfloat16))
        out_specs.append(ANY)
        more = [pltpu.SemaphoreType.DMA((len(arrays),))]
    payload = pl.pallas_call(
        functools.partial(assemble_kernel, places, fresh, last),
        out_shape=tuple(out_shape),
        in_specs=[SMEM] + [ANY] * len(arrays) + ([] if fresh else [ANY, VMEM]),
        out_specs=tuple(out_specs),
        scratch_shapes=scratch
        + [
            pltpu.VMEM((len(places), 16, BLOCK), jnp.bfloat16),
            pltpu.SemaphoreType.DMA((len(places) * SUB,)),
            pltpu.SemaphoreType.DMA((len(places),)),
            *more,
        ],
        input_output_aliases={} if fresh else {len(arrays) + 1: 0},
        compiler_params=pltpu.CompilerParams(vmem_limit_bytes=4 << 20),
        cost_estimate=pl.CostEstimate(flops=1 << 20, bytes_accessed=4 << 20, transcendentals=0),
        name="assemble",
    )(index, *arrays, *([] if fresh else before))
    return (payload[2], *payload[:2]) if fresh else payload


def add(arrived, own):
    return (arrived.astype(jnp.float32) + own.astype(jnp.float32)).astype(jnp.bfloat16)


def send(x, pairs):
    return lax.ppermute(x, "tp", pairs)


EARLY = 12


def layer(queries, keys, values, out_weight, signs):
    ctx, tp = lax.axis_index("ctx"), lax.axis_index("tp")
    core, chip = tp & 1, tp >> 1

    place = jnp.stack([ctx * TOKENS, core, chip, ctx >> 2, ctx & 3]).astype(jnp.int32)

    other_weight = send(out_weight, PAIR)

    def spread_out(x, pairs):
        up, down = (lax.ppermute(x, ("ctx", "tp"), way) for way in pairs)
        count = x.shape[0] // 2
        if count < TOKENS:
            far = (lax.ppermute(up, ("ctx", "tp"), pairs[0]),)
        else:
            far = (
                lax.ppermute(up[:count], ("ctx", "tp"), pairs[0]),
                lax.ppermute(down[count:], ("ctx", "tp"), pairs[1]),
            )
        return jnp.concatenate([x, up, down, *far], 0)

    key_part = lax.dynamic_slice_in_dim(keys, chip * HEAD, HEAD, 1)
    value_part = lax.dynamic_slice_in_dim(values, chip * HEAD, HEAD, 1)
    held = spread_out(jnp.where(core == 0, key_part, value_part), FIRST)
    held = spread_out(held, SECOND)
    swapped = send(held, PAIR)

    index = jnp.stack([core, chip]).astype(jnp.int32)
    turn = jnp.asarray(turn_matrix(), jnp.bfloat16)
    spread = jnp.asarray(spread_matrix(), jnp.bfloat16)
    attended = attention(place, queries, held, swapped)
    parts = project(
        place,
        attended,
        send(attended, PAIR),
        out_weight,
        other_weight,
        signs[None, :],
        turn,
        spread,
    )

    def plus(arrived, up, down):
        arrived = lax.optimization_barrier(arrived)
        return add(arrived[0], up), add(arrived[1], down)

    def both_ways(up, down):
        up = send(up, UP)
        down = send(down, DOWN)
        return up, down

    a = both_ways(parts[0], parts[1])
    b = both_ways(parts[3], parts[4])
    a = both_ways(*plus(a, parts[2], parts[5]))
    for near in (6, 10):
        b = both_ways(*plus(b, parts[near + 1], parts[near + 2]))
        a = both_ways(*plus(a, parts[near], parts[near + 3]))
    packed = pack(parts[14:], (a[0], b[0]), (b[1], a[1]))

    pieces, spots = list(packed), [(0, 0), (0, 1)]
    chains = [(packed[0], packed[1]), (packed[1], packed[0])]
    for step in range(7):
        h, hop = step % 2, step // 2 + 1
        chains[h] = both_ways(*lax.optimization_barrier(chains[h]))
        pieces += chains[h]
        spots += [(-hop, h), (hop, 1 - h)]

    def rows(swap, a, b, joined):
        return tuple(
            (0 if joined else n - a, (n - a) * MSG if joined else 0, swap, *spots[n])
            for n in range(a, b)
        )

    first = assemble(index, pieces[:EARLY], rows(False, 0, EARLY, False), None, False)
    early, *first = first
    early = send(early, PAIR)
    rest = jnp.concatenate(pieces[EARLY:], 0)
    late = send(rest, PAIR)
    second = assemble(index, [early], rows(True, 0, EARLY, True), first, False)
    count = len(pieces) - EARLY
    tail = rows(False, EARLY, EARLY + count, True) + tuple(
        (1, *where[1:]) for where in rows(True, EARLY, EARLY + count, True)
    )
    payload, scales = assemble(index, [rest, late], tail, second, True)
    return payload, scales.T


def solution(mesh):
    return jax.shard_map(
        layer,
        mesh=mesh,
        in_specs=(P("ctx", "tp"), P("ctx", None), P("ctx", None), P("tp", None), P()),
        out_specs=(P("ctx", None), P("ctx", None)),
        check_vma=False,
    )
```

profile of v0, /device:TPU:1, one launch (start us, length us, event | category | flops | bytes accessed | tf_op | source)
XLA Modules:
  0.0 122.6 jit_solution(17256623678704938044)
XLA Ops:
  0.6 3.3 %collective-permute-start.9 = (bf16[512,8192]{1,0:T(8,128)(2,1)}, bf16[512,8192]{1,0:T(8,128)(2,1)}, u32[]{:S(2)}, u32[]{:S(2)}) collective-permute-start(bf16[512,8192]{1,0:T(8,128)(2,1)} %own_hbm.1), channel_id=1, source_target_pairs={{0,1},{1,0},{2,3},{3,2},{4,5},{5,4},{6,7},{7,6},{8,9},{9,8},{10,11... | collective-permute-start | bytes 25165832 | tf_op jit(solution)/shard_map/ppermute | solution.py:424
  3.9 0.9 constant_dynamic-update-slice_fusion.7
  4.8 0.1 collective-permute-start
  4.9 2.7 %collective-permute-start.1 = (bf16[224,128]{1,0:T(8,128)(2,1)S(1)}, bf16[224,128]{1,0:T(8,128)(2,1)S(1)}, u32[]{:S(2)}, u32[]{:S(2)}) collective-permute-start(bf16[224,128]{1,0:T(8,128)(2,1)S(1)} %get-tuple-element.101), channel_id=1, source_target_pairs={{0,48},{1,193},{2,50},{3,195},{4,52},{5,197},{6,54},{7,199},{8,56}... | collective-permute-start | bytes 172040 | tf_op jit(solution)/shard_map/ppermute | solution.py:439
  7.5 1.9 %collective-permute-done = bf16[224,128]{1,0:T(8,128)(2,1)S(1)} collective-permute-done((bf16[224,128]{1,0:T(8,128)(2,1)S(1)}, bf16[224,128]{1,0:T(8,128)(2,1)S(1)}, u32[]{:S(2)}, u32[]{:S(2)}) %collective-permute-start) | collective-permute-done | bytes 57376 | tf_op jit(solution)/shard_map/ppermute | solution.py:439
  9.4 4.2 %collective-permute-done.2 = bf16[224,128]{1,0:T(8,128)(2,1)S(1)} collective-permute-done((bf16[224,128]{1,0:T(8,128)(2,1)S(1)}, bf16[224,128]{1,0:T(8,128)(2,1)S(1)}, u32[]{:S(2)}, u32[]{:S(2)}) %collective-permute-start.2) | collective-permute-done | bytes 57376 | tf_op jit(solution)/shard_map/ppermute | solution.py:442
  13.7 0.6 collective-permute-start.4
  14.3 0.9 collective-permute-start.3
  15.3 3.4 %collective-permute-done.4 = bf16[896,128]{1,0:T(8,128)(2,1)S(1)} collective-permute-done((bf16[896,128]{1,0:T(8,128)(2,1)S(1)}, bf16[896,128]{1,0:T(8,128)(2,1)S(1)}, u32[]{:S(2)}, u32[]{:S(2)}) %collective-permute-start.4) | collective-permute-done | bytes 229408 | tf_op jit(solution)/shard_map/ppermute | solution.py:439
  18.6 1.8 %collective-permute-start.6 = (bf16[448,128]{1,0:T(8,128)(2,1)S(1)}, bf16[448,128]{1,0:T(8,128)(2,1)S(1)}, u32[]{:S(2)}, u32[]{:S(2)}) collective-permute-start(bf16[448,128]{1,0:T(8,128)(2,1)S(1)} %slice.9), channel_id=1, source_target_pairs={{0,192},{1,49},{2,194},{3,51},{4,196},{5,53},{6,198},{7,55},{8,200... | collective-permute-start | bytes 344072 | tf_op jit(solution)/shard_map/ppermute | solution.py:446
  20.5 0.1 collective-permute-start.5
  20.7 4.8 %collective-permute-done.5 = bf16[448,128]{1,0:T(8,128)(2,1)S(1)} collective-permute-done((bf16[448,128]{1,0:T(8,128)(2,1)S(1)}, bf16[448,128]{1,0:T(8,128)(2,1)S(1)}, u32[]{:S(2)}, u32[]{:S(2)}) %collective-permute-start.5) | collective-permute-done | bytes 114720 | tf_op jit(solution)/shard_map/ppermute | solution.py:445
  25.5 5.2 %collective-permute-start.7 = (bf16[3584,128]{1,0:T(8,128)(2,1)S(1)}, bf16[3584,128]{1,0:T(8,128)(2,1)S(1)}, u32[]{:S(2)}, u32[]{:S(2)}) collective-permute-start(bf16[3584,128]{1,0:T(8,128)(2,1)S(1)} %constant_dynamic-update-slice_fusion.held_ref), channel_id=1, source_target_pairs={{0,1},{1,0},{2,3},{3,2},{4,5},{5,4},{6,7},{7,6},{8,9},{9,8},{10,11... | collective-permute-start | bytes 2752520 | tf_op jit(solution)/shard_map/ppermute | solution.py:424
  30.7 0.1 stack.29.place_ref
  30.8 2.0 %collective-permute-done.7.swapped_ref = bf16[3584,128]{1,0:T(8,128)(2,1)S(1)} collective-permute-done((bf16[3584,128]{1,0:T(8,128)(2,1)S(1)}, bf16[3584,128]{1,0:T(8,128)(2,1)S(1)}, u32[]{:S(2)}, u32[]{:S(2)}) %collective-permute-start.7) | collective-permute-done | bytes 917536 | tf_op jit(solution)/shard_map/ppermute | solution.py:424
  32.8 0.9 copy-done.3
  33.7 3.5 %attend.1.mine_ref = bf16[224,512]{1,0:T(8,128)(2,1)S(1)} custom-call(s32[5]{0:T(128)S(1)} %stack.29.place_ref, bf16[224,512]{1,0:T(8,128)(2,1)S(1)} %copy-done.3, bf16[3584,128]{1,0:T(8,128)(2,1)S(1)} %constant_dynamic-update-slice_fusion.held_ref, bf16[3584,128]{1,0:T(8,128)(2,1)S(1)} %collective-permute-done.7.swapped_ref), custom_call_target="tpu_custom_call" | custom-call | flops 1644167168 | bytes 3145728 | tf_op jit(solution)/shard_map/attend/pallas_call | solution.py:195
  37.2 0.5 collective-permute-start.8
  37.7 1.1 collective-permute-done.8.theirs_ref
  38.8 10.8 %project.1 = (bf16[448,128]{1,0:T(8,128)(2,1)S(1)}, bf16[448,128]{1,0:T(8,128)(2,1)S(1)}, bf16[448,128]{1,0:T(8,128)(2,1)S(1)}, bf16[448,128]{1,0:T(8,128)(2,1)S...) custom-call(s32[5]{0:T(128)S(1)} %stack.29.place_ref, ...), custom_call_target="tpu_custom_call" | custom-call | flops 2348810240 | bytes 10485760 | tf_op jit(solution)/shard_map/project/pallas_call | solution.py:271
  49.6 1.7 %collective-permute-start.10 = (bf16[448,128]{1,0:T(8,128)(2,1)S(1)}, bf16[448,128]{1,0:T(8,128)(2,1)S(1)}, u32[]{:S(2)}, u32[]{:S(2)}) collective-permute-start(bf16[448,128]{1,0:T(8,128)(2,1)S(1)} %get-tuple-element.53), channel_id=1, source_target_pairs={{0,2},{1,3},{2,4},{3,5},{4,6},{5,7},{6,8},{7,9},{8,10},{9,11},{10,... | collective-permute-start | bytes 344072 | tf_op jit(solution)/shard_map/ppermute | solution.py:424
  51.3 4.0 %collective-permute-start.11 = (bf16[448,128]{1,0:T(8,128)(2,1)S(1)}, bf16[448,128]{1,0:T(8,128)(2,1)S(1)}, u32[]{:S(2)}, u32[]{:S(2)}) collective-permute-start(bf16[448,128]{1,0:T(8,128)(2,1)S(1)} %get-tuple-element.54), channel_id=1, source_target_pairs={{0,14},{1,15},{2,0},{3,1},{4,2},{5,3},{6,4},{7,5},{8,6},{9,7},{10,... | collective-permute-start | bytes 344072 | tf_op jit(solution)/shard_map/ppermute | solution.py:424
  55.3 2.7 %collective-permute-start.18 = (bf16[448,128]{1,0:T(8,128)(2,1)S(1)}, bf16[448,128]{1,0:T(8,128)(2,1)S(1)}, u32[]{:S(2)}, u32[]{:S(2)}) collective-permute-start(bf16[448,128]{1,0:T(8,128)(2,1)S(1)} %get-tuple-element.66), channel_id=1, source_target_pairs={{0,14},{1,15},{2,0},{3,1},{4,2},{5,3},{6,4},{7,5},{8,6},{9,7},{10,... | collective-permute-start | bytes 344072 | tf_op jit(solution)/shard_map/ppermute | solution.py:424
  58.0 0.4 collective-permute-done.10
  58.4 2.6 %collective-permute-start.13 = (bf16[448,128]{1,0:T(8,128)(2,1)S(1)}, bf16[448,128]{1,0:T(8,128)(2,1)S(1)}, u32[]{:S(2)}, u32[]{:S(2)}) collective-permute-start(bf16[448,128]{1,0:T(8,128)(2,1)S(1)} %add_convert_fusion.8), channel_id=1, source_target_pairs={{0,14},{1,15},{2,0},{3,1},{4,2},{5,3},{6,4},{7,5},{8,6},{9,7},{10,... | collective-permute-start | bytes 344072 | tf_op jit(solution)/shard_map/ppermute | solution.py:424
  61.0 0.1 collective-permute-start.12
  61.2 2.7 %collective-permute-start.20 = (bf16[448,128]{1,0:T(8,128)(2,1)S(1)}, bf16[448,128]{1,0:T(8,128)(2,1)S(1)}, u32[]{:S(2)}, u32[]{:S(2)}) collective-permute-start(bf16[448,128]{1,0:T(8,128)(2,1)S(1)} %add_convert_fusion.3), channel_id=1, source_target_pairs={{0,14},{1,15},{2,0},{3,1},{4,2},{5,3},{6,4},{7,5},{8,6},{9,7},{10,... | collective-permute-start | bytes 344072 | tf_op jit(solution)/shard_map/ppermute | solution.py:424
  63.9 0.1 collective-permute-start.19
  64.0 1.9 %collective-permute-done.12 = bf16[448,128]{1,0:T(8,128)(2,1)S(1)} collective-permute-done((bf16[448,128]{1,0:T(8,128)(2,1)S(1)}, bf16[448,128]{1,0:T(8,128)(2,1)S(1)}, u32[]{:S(2)}, u32[]{:S(2)}) %collective-permute-start.12) | collective-permute-done | bytes 114720 | tf_op jit(solution)/shard_map/ppermute | solution.py:424
  66.0 0.8 collective-permute-start.15
  66.8 0.8 collective-permute-start.14
  67.6 1.5 %collective-permute-done.19 = bf16[448,128]{1,0:T(8,128)(2,1)S(1)} collective-permute-done((bf16[448,128]{1,0:T(8,128)(2,1)S(1)}, bf16[448,128]{1,0:T(8,128)(2,1)S(1)}, u32[]{:S(2)}, u32[]{:S(2)}) %collective-permute-start.19) | collective-permute-done | bytes 114720 | tf_op jit(solution)/shard_map/ppermute | solution.py:424
  69.2 0.5 collective-permute-start.22
  69.8 1.1 collective-permute-start.21
  70.9 1.8 %collective-permute-done.14 = bf16[448,128]{1,0:T(8,128)(2,1)S(1)} collective-permute-done((bf16[448,128]{1,0:T(8,128)(2,1)S(1)}, bf16[448,128]{1,0:T(8,128)(2,1)S(1)}, u32[]{:S(2)}, u32[]{:S(2)}) %collective-permute-start.14) | collective-permute-done | bytes 114720 | tf_op jit(solution)/shard_map/ppermute | solution.py:424
  72.7 0.1 collective-permute-start.23
  72.8 1.5 %collective-permute-start.16 = (bf16[448,128]{1,0:T(8,128)(2,1)S(1)}, bf16[448,128]{1,0:T(8,128)(2,1)S(1)}, u32[]{:S(2)}, u32[]{:S(2)}) collective-permute-start(bf16[448,128]{1,0:T(8,128)(2,1)S(1)} %add_convert_fusion.5), channel_id=1, source_target_pairs={{0,2},{1,3},{2,4},{3,5},{4,6},{5,7},{6,8},{7,9},{8,10},{9,11},{10,... | collective-permute-start | bytes 344072 | tf_op jit(solution)/shard_map/ppermute | solution.py:424
  74.3 1.2 collective-permute-done.21.up1
  75.5 1.6 %collective-permute-done.23.down1 = bf16[448,128]{1,0:T(8,128)(2,1)S(1)} collective-permute-done((bf16[448,128]{1,0:T(8,128)(2,1)S(1)}, bf16[448,128]{1,0:T(8,128)(2,1)S(1)}, u32[]{:S(2)}, u32[]{:S(2)}) %collective-permute-start.23) | collective-permute-done | bytes 114720 | tf_op jit(solution)/shard_map/ppermute | solution.py:424
  77.1 1.0 collective-permute-done.16.up0
  78.1 0.3 pack.1
  78.4 0.4 collective-permute-start.30
  78.8 2.3 %collective-permute-start.31 = (bf16[464,128]{1,0:T(8,128)(2,1)S(1)}, bf16[464,128]{1,0:T(8,128)(2,1)S(1)}, u32[]{:S(2)}, u32[]{:S(2)}) collective-permute-start(bf16[464,128]{1,0:T(8,128)(2,1)S(1)} %get-tuple-element.79.refs_1_), channel_id=1, source_target_pairs={{0,14},{1,15},{2,0},{3,1},{4,2},{5,3},{6,4},{7,5},{8,6},{9,7},{10,... | collective-permute-start | bytes 356360 | tf_op jit(solution)/shard_map/ppermute | solution.py:424
  81.1 2.7 %collective-permute-start.25 = (bf16[464,128]{1,0:T(8,128)(2,1)S(1)}, bf16[464,128]{1,0:T(8,128)(2,1)S(1)}, u32[]{:S(2)}, u32[]{:S(2)}) collective-permute-start(bf16[464,128]{1,0:T(8,128)(2,1)S(1)} %get-tuple-element.80.refs_0_), channel_id=1, source_target_pairs={{0,14},{1,15},{2,0},{3,1},{4,2},{5,3},{6,4},{7,5},{8,6},{9,7},{10,... | collective-permute-start | bytes 356360 | tf_op jit(solution)/shard_map/ppermute | solution.py:424
  83.8 2.7 %collective-permute-start.33 = (bf16[464,128]{1,0:T(8,128)(2,1)S(1)}, bf16[464,128]{1,0:T(8,128)(2,1)S(1)}, u32[]{:S(2)}, u32[]{:S(2)}) collective-permute-start(bf16[464,128]{1,0:T(8,128)(2,1)S(1)} %collective-permute-done.31.refs_3_), channel_id=1, source_target_pairs={{0,14},{1,15},{2,0},{3,1},{4,2},{5,3},{6,4},{7,5},{8,6},{9,7},{10,... | collective-permute-start | bytes 356360 | tf_op jit(solution)/shard_map/ppermute | solution.py:424
  86.5 2.7 %collective-permute-start.27 = (bf16[464,128]{1,0:T(8,128)(2,1)S(1)}, bf16[464,128]{1,0:T(8,128)(2,1)S(1)}, u32[]{:S(2)}, u32[]{:S(2)}) collective-permute-start(bf16[464,128]{1,0:T(8,128)(2,1)S(1)} %collective-permute-done.25.refs_5_), channel_id=1, source_target_pairs={{0,14},{1,15},{2,0},{3,1},{4,2},{5,3},{6,4},{7,5},{8,6},{9,7},{10,... | collective-permute-start | bytes 356360 | tf_op jit(solution)/shard_map/ppermute | solution.py:424
  89.1 0.7 collective-permute-done.32.refs_6_
  89.9 2.2 %collective-permute-start.34 = (bf16[464,128]{1,0:T(8,128)(2,1)S(1)}, bf16[464,128]{1,0:T(8,128)(2,1)S(1)}, u32[]{:S(2)}, u32[]{:S(2)}) collective-permute-start(bf16[464,128]{1,0:T(8,128)(2,1)S(1)} %collective-permute-done.32.refs_6_), channel_id=1, source_target_pairs={{0,2},{1,3},{2,4},{3,5},{4,6},{5,7},{6,8},{7,9},{8,10},{9,11},{10,... | collective-permute-start | bytes 356360 | tf_op jit(solution)/shard_map/ppermute | solution.py:424
  92.1 0.5 collective-permute-start.35
  92.6 0.1 pad_add_fusion.index_ref
  92.7 2.5 %collective-permute-done.34.refs_10_ = bf16[464,128]{1,0:T(8,128)(2,1)S(1)} collective-permute-done((bf16[464,128]{1,0:T(8,128)(2,1)S(1)}, bf16[464,128]{1,0:T(8,128)(2,1)S(1)}, u32[]{:S(2)}, u32[]{:S(2)}) %collective-permute-start.34) | collective-permute-done | bytes 118816 | tf_op jit(solution)/shard_map/ppermute | solution.py:424
  95.2 1.2 collective-permute-done.35.refs_11_
  96.4 3.9 %assemble.3 = (bf16[224,8192]{1,0:T(8,128)(2,1)}, f32[8,2,4,256]{3,2,1,0:T(4,128)S(1)}, bf16[5568,128]{1,0:T(8,128)(2,1)S(1)}) custom-call(s32[2]{0:T(128)S(1)} %pad_add_fusion.index_ref, bf16[464,128]{1,0:T(8,128)(2,1)S(1)} %get-tuple-element.80.refs_0_, bf16[464,128]{1,0:T(8,128)(2,1)S(1)} %get-tuple-element.79.refs_1_, ...), custom_call_target="tpu_custom_call" | custom-call | flops 1048576 | bytes 4194304 | tf_op jit(solution)/shard_map/assemble/pallas_call | solution.py:399
  100.3 8.0 %collective-permute-start.39 = (bf16[5568,128]{1,0:T(8,128)(2,1)S(1)}, bf16[5568,128]{1,0:T(8,128)(2,1)S(1)}, u32[]{:S(2)}, u32[]{:S(2)}) collective-permute-start(bf16[5568,128]{1,0:T(8,128)(2,1)S(1)} %get-tuple-element.93), channel_id=1, source_target_pairs={{0,1},{1,0},{2,3},{3,2},{4,5},{5,4},{6,7},{7,6},{8,9},{9,8},{10,11... | collective-permute-start | bytes 4276232 | tf_op jit(solution)/shard_map/ppermute | solution.py:424
  108.3 1.5 %collective-permute-start.28 = (bf16[464,128]{1,0:T(8,128)(2,1)S(1)}, bf16[464,128]{1,0:T(8,128)(2,1)S(1)}, u32[]{:S(2)}, u32[]{:S(2)}) collective-permute-start(bf16[464,128]{1,0:T(8,128)(2,1)S(1)} %collective-permute-done.26.refs_8_), channel_id=1, source_target_pairs={{0,2},{1,3},{2,4},{3,5},{4,6},{5,7},{6,8},{7,9},{8,10},{9,11},{10,... | collective-permute-start | bytes 356360 | tf_op jit(solution)/shard_map/ppermute | solution.py:424
  109.8 1.2 collective-permute-start.29
  111.0 0.3 collective-permute-start.36
  111.2 2.4 %collective-permute-start.37 = (bf16[464,128]{1,0:T(8,128)(2,1)S(1)}, bf16[464,128]{1,0:T(8,128)(2,1)S(1)}, u32[]{:S(2)}, u32[]{:S(2)}) collective-permute-start(bf16[464,128]{1,0:T(8,128)(2,1)S(1)} %collective-permute-done.35.refs_11_), channel_id=1, source_target_pairs={{0,14},{1,15},{2,0},{3,1},{4,2},{5,3},{6,4},{7,5},{8,6},{9,7},{10,... | collective-permute-start | bytes 356360 | tf_op jit(solution)/shard_map/ppermute | solution.py:424
  113.7 0.6 collective-permute-done.28
  114.3 2.1 %collective-permute-done.36 = bf16[464,128]{1,0:T(8,128)(2,1)S(1)} collective-permute-done((bf16[464,128]{1,0:T(8,128)(2,1)S(1)}, bf16[464,128]{1,0:T(8,128)(2,1)S(1)}, u32[]{:S(2)}, u32[]{:S(2)}) %collective-permute-start.36) | collective-permute-done | bytes 118816 | tf_op jit(solution)/shard_map/ppermute | solution.py:424
  116.4 0.4 collective-permute-done.37
  116.8 1.3 %collective-permute-start.38 = (bf16[1856,128]{1,0:T(8,128)(2,1)S(1)}, bf16[1856,128]{1,0:T(8,128)(2,1)S(1)}, u32[]{:S(2)}, u32[]{:S(2)}) collective-permute-start(bf16[1856,128]{1,0:T(8,128)(2,1)S(1)} %constant_dynamic-update-slice_fusion.8.refs_0_), channel_id=1, source_target_pairs={{0,1},{1,0},{2,3},{3,2},{4,5},{5,4},{6,7},{7,6},{8,9},{9,8},{10,11... | collective-permute-start | bytes 1425416 | tf_op jit(solution)/shard_map/ppermute | solution.py:424
  118.1 2.0 %assemble.4 = (bf16[224,8192]{1,0:T(8,128)(2,1)}, f32[8,2,4,256]{3,2,1,0:T(4,128)S(1)}) custom-call(s32[2]{0:T(128)S(1)} %pad_add_fusion.index_ref, bf16[5568,128]{1,0:T(8,128)(2,1)S(1)} %collective-permute-done.39.refs_0_, bf16[224,8192]{1,0:T(8,128)(2,1)} %get-tuple-element.94.refs_1_, ...), custom_call_target="tpu_custom_call", output_to_operand_aliasing={{0}: (2, {})} | custom-call | flops 1048576 | bytes 4194304 | tf_op jit(solution)/shard_map/assemble/pallas_call | solution.py:399
  120.1 2.3 %assemble.5 = (bf16[224,8192]{1,0:T(8,128)(2,1)}, f32[64,224]{1,0:T(8,128)}) custom-call(s32[2]{0:T(128)S(1)} %pad_add_fusion.index_ref, bf16[1856,128]{1,0:T(8,128)(2,1)S(1)} %constant_dynamic-update-slice_fusion.8.refs_0_, bf16[1856,128]{1,0:T(8,128)(2,1)S(1)} %collective-permute-done.38.refs_1_, ...), custom_call_target="tpu_custom_call", output_to_operand_aliasing={{0}: (3, {})} | custom-call | flops 1048576 | bytes 4194304 | tf_op jit(solution)/shard_map/assemble/pallas_call | solution.py:399
  (57 shorter events, 0.7 us)
Async XLA Ops:
  0.6 38.2 %collective-permute-start.9 = (bf16[512,8192]{1,0:T(8,128)(2,1)}, bf16[512,8192]{1,0:T(8,128)(2,1)}, u32[]{:S(2)}, u32[]{:S(2)}) collective-permute-start(bf16[512,8192]{1,0:T(8,128)(2,1)} %own_hbm.1), channel_id=1, source_target_pairs={{0,1},{1,0},{2,3},{3,2},{4,5},{5,4},{6,7},{7,6},{8,9},{9,8},{10,11... | collective-permute-start | bytes 25165832 | tf_op jit(solution)/shard_map/ppermute | solution.py:424
  4.8 4.6 %collective-permute-start = (bf16[224,128]{1,0:T(8,128)(2,1)S(1)}, bf16[224,128]{1,0:T(8,128)(2,1)S(1)}, u32[]{:S(2)}, u32[]{:S(2)}) collective-permute-start(bf16[224,128]{1,0:T(8,128)(2,1)S(1)} %get-tuple-element.101), channel_id=1, source_target_pairs={{0,16},{1,65},{2,18},{3,67},{4,20},{5,69},{6,22},{7,71},{8,24},{9,... | collective-permute-start | bytes 172040 | tf_op jit(solution)/shard_map/ppermute | solution.py:439
  4.9 4.5 %collective-permute-start.1 = (bf16[224,128]{1,0:T(8,128)(2,1)S(1)}, bf16[224,128]{1,0:T(8,128)(2,1)S(1)}, u32[]{:S(2)}, u32[]{:S(2)}) collective-permute-start(bf16[224,128]{1,0:T(8,128)(2,1)S(1)} %get-tuple-element.101), channel_id=1, source_target_pairs={{0,48},{1,193},{2,50},{3,195},{4,52},{5,197},{6,54},{7,199},{8,56}... | collective-permute-start | bytes 172040 | tf_op jit(solution)/shard_map/ppermute | solution.py:439
  9.4 4.2 %collective-permute-start.2 = (bf16[224,128]{1,0:T(8,128)(2,1)S(1)}, bf16[224,128]{1,0:T(8,128)(2,1)S(1)}, u32[]{:S(2)}, u32[]{:S(2)}) collective-permute-start(bf16[224,128]{1,0:T(8,128)(2,1)S(1)} %collective-permute-done), channel_id=1, source_target_pairs={{0,16},{1,65},{2,18},{3,67},{4,20},{5,69},{6,22},{7,71},{8,24},{9,... | collective-permute-start | bytes 172040 | tf_op jit(solution)/shard_map/ppermute | solution.py:442
  13.7 4.9 %collective-permute-start.4 = (bf16[896,128]{1,0:T(8,128)(2,1)S(1)}, bf16[896,128]{1,0:T(8,128)(2,1)S(1)}, u32[]{:S(2)}, u32[]{:S(2)}) collective-permute-start(bf16[896,128]{1,0:T(8,128)(2,1)S(1)} %pad_maximum_fusion), channel_id=1, source_target_pairs={{0,192},{1,49},{2,194},{3,51},{4,196},{5,53},{6,198},{7,55},{8,200... | collective-permute-start | bytes 688136 | tf_op jit(solution)/shard_map/ppermute | solution.py:439
  14.3 6.2 %collective-permute-start.3 = (bf16[896,128]{1,0:T(8,128)(2,1)S(1)}, bf16[896,128]{1,0:T(8,128)(2,1)S(1)}, u32[]{:S(2)}, u32[]{:S(2)}) collective-permute-start(bf16[896,128]{1,0:T(8,128)(2,1)S(1)} %pad_maximum_fusion), channel_id=1, source_target_pairs={{0,64},{1,17},{2,66},{3,19},{4,68},{5,21},{6,70},{7,23},{8,72},{9,... | collective-permute-start | bytes 688136 | tf_op jit(solution)/shard_map/ppermute | solution.py:439
  18.6 6.8 %collective-permute-start.6 = (bf16[448,128]{1,0:T(8,128)(2,1)S(1)}, bf16[448,128]{1,0:T(8,128)(2,1)S(1)}, u32[]{:S(2)}, u32[]{:S(2)}) collective-permute-start(bf16[448,128]{1,0:T(8,128)(2,1)S(1)} %slice.9), channel_id=1, source_target_pairs={{0,192},{1,49},{2,194},{3,51},{4,196},{5,53},{6,198},{7,55},{8,200... | collective-permute-start | bytes 344072 | tf_op jit(solution)/shard_map/ppermute | solution.py:446
  20.5 18.4 %copy-start = (bf16[256,256]{1,0:T(8,128)(2,1)S(1)}, bf16[256,256]{1,0:T(8,128)(2,1)}, u32[]{:S(2)}) copy-start(bf16[256,256]{1,0:T(8,128)(2,1)} %constant.25.clone.turn_ref) | copy-start | bytes 393220
  20.5 18.3 %copy-start.1 = (bf16[128,256]{1,0:T(8,128)(2,1)S(1)}, bf16[128,256]{1,0:T(8,128)(2,1)}, u32[]{:S(2)}) copy-start(bf16[128,256]{1,0:T(8,128)(2,1)} %constant.26.clone.spread_ref) | copy-start | bytes 196612
  20.5 18.3 %copy-start.2 = (s32[8192]{0:T(1024)S(1)}, s32[8192]{0:T(1024)}, u32[]{:S(2)}) copy-start(s32[8192]{0:T(1024)} %param.11) | copy-start | bytes 98308
  20.5 4.9 %collective-permute-start.5 = (bf16[448,128]{1,0:T(8,128)(2,1)S(1)}, bf16[448,128]{1,0:T(8,128)(2,1)S(1)}, u32[]{:S(2)}, u32[]{:S(2)}) collective-permute-start(bf16[448,128]{1,0:T(8,128)(2,1)S(1)} %slice.8), channel_id=1, source_target_pairs={{0,64},{1,17},{2,66},{3,19},{4,68},{5,21},{6,70},{7,23},{8,72},{9,... | collective-permute-start | bytes 344072 | tf_op jit(solution)/shard_map/ppermute | solution.py:445
  25.5 7.3 %collective-permute-start.7 = (bf16[3584,128]{1,0:T(8,128)(2,1)S(1)}, bf16[3584,128]{1,0:T(8,128)(2,1)S(1)}, u32[]{:S(2)}, u32[]{:S(2)}) collective-permute-start(bf16[3584,128]{1,0:T(8,128)(2,1)S(1)} %constant_dynamic-update-slice_fusion.held_ref), channel_id=1, source_target_pairs={{0,1},{1,0},{2,3},{3,2},{4,5},{5,4},{6,7},{7,6},{8,9},{9,8},{10,11... | collective-permute-start | bytes 2752520 | tf_op jit(solution)/shard_map/ppermute | solution.py:424
  32.8 0.9 copy-start.3
  37.2 1.6 %collective-permute-start.8 = (bf16[224,512]{1,0:T(8,128)(2,1)S(1)}, bf16[224,512]{1,0:T(8,128)(2,1)S(1)}, u32[]{:S(2)}, u32[]{:S(2)}) collective-permute-start(bf16[224,512]{1,0:T(8,128)(2,1)S(1)} %attend.1.mine_ref), channel_id=1, source_target_pairs={{0,1},{1,0},{2,3},{3,2},{4,5},{5,4},{6,7},{7,6},{8,9},{9,8},{10,11... | collective-permute-start | bytes 688136 | tf_op jit(solution)/shard_map/ppermute | solution.py:424
  49.6 8.8 %collective-permute-start.10 = (bf16[448,128]{1,0:T(8,128)(2,1)S(1)}, bf16[448,128]{1,0:T(8,128)(2,1)S(1)}, u32[]{:S(2)}, u32[]{:S(2)}) collective-permute-start(bf16[448,128]{1,0:T(8,128)(2,1)S(1)} %get-tuple-element.53), channel_id=1, source_target_pairs={{0,2},{1,3},{2,4},{3,5},{4,6},{5,7},{6,8},{7,9},{8,10},{9,11},{10,... | collective-permute-start | bytes 344072 | tf_op jit(solution)/shard_map/ppermute | solution.py:424
  51.3 7.1 %collective-permute-start.11 = (bf16[448,128]{1,0:T(8,128)(2,1)S(1)}, bf16[448,128]{1,0:T(8,128)(2,1)S(1)}, u32[]{:S(2)}, u32[]{:S(2)}) collective-permute-start(bf16[448,128]{1,0:T(8,128)(2,1)S(1)} %get-tuple-element.54), channel_id=1, source_target_pairs={{0,14},{1,15},{2,0},{3,1},{4,2},{5,3},{6,4},{7,5},{8,6},{9,7},{10,... | collective-permute-start | bytes 344072 | tf_op jit(solution)/shard_map/ppermute | solution.py:424
  55.3 5.8 %collective-permute-start.17 = (bf16[448,128]{1,0:T(8,128)(2,1)S(1)}, bf16[448,128]{1,0:T(8,128)(2,1)S(1)}, u32[]{:S(2)}, u32[]{:S(2)}) collective-permute-start(bf16[448,128]{1,0:T(8,128)(2,1)S(1)} %get-tuple-element.65), channel_id=1, source_target_pairs={{0,2},{1,3},{2,4},{3,5},{4,6},{5,7},{6,8},{7,9},{8,10},{9,11},{10,... | collective-permute-start | bytes 344072 | tf_op jit(solution)/shard_map/ppermute | solution.py:424
  55.3 5.8 %collective-permute-start.18 = (bf16[448,128]{1,0:T(8,128)(2,1)S(1)}, bf16[448,128]{1,0:T(8,128)(2,1)S(1)}, u32[]{:S(2)}, u32[]{:S(2)}) collective-permute-start(bf16[448,128]{1,0:T(8,128)(2,1)S(1)} %get-tuple-element.66), channel_id=1, source_target_pairs={{0,14},{1,15},{2,0},{3,1},{4,2},{5,3},{6,4},{7,5},{8,6},{9,7},{10,... | collective-permute-start | bytes 344072 | tf_op jit(solution)/shard_map/ppermute | solution.py:424
  58.4 5.6 %collective-permute-start.13 = (bf16[448,128]{1,0:T(8,128)(2,1)S(1)}, bf16[448,128]{1,0:T(8,128)(2,1)S(1)}, u32[]{:S(2)}, u32[]{:S(2)}) collective-permute-start(bf16[448,128]{1,0:T(8,128)(2,1)S(1)} %add_convert_fusion.8), channel_id=1, source_target_pairs={{0,14},{1,15},{2,0},{3,1},{4,2},{5,3},{6,4},{7,5},{8,6},{9,7},{10,... | collective-permute-start | bytes 344072 | tf_op jit(solution)/shard_map/ppermute | solution.py:424
  61.0 4.9 %collective-permute-start.12 = (bf16[448,128]{1,0:T(8,128)(2,1)S(1)}, bf16[448,128]{1,0:T(8,128)(2,1)S(1)}, u32[]{:S(2)}, u32[]{:S(2)}) collective-permute-start(bf16[448,128]{1,0:T(8,128)(2,1)S(1)} %add_convert_fusion.9), channel_id=1, source_target_pairs={{0,2},{1,3},{2,4},{3,5},{4,6},{5,7},{6,8},{7,9},{8,10},{9,11},{10,... | collective-permute-start | bytes 344072 | tf_op jit(solution)/shard_map/ppermute | solution.py:424
  61.2 6.5 %collective-permute-start.20 = (bf16[448,128]{1,0:T(8,128)(2,1)S(1)}, bf16[448,128]{1,0:T(8,128)(2,1)S(1)}, u32[]{:S(2)}, u32[]{:S(2)}) collective-permute-start(bf16[448,128]{1,0:T(8,128)(2,1)S(1)} %add_convert_fusion.3), channel_id=1, source_target_pairs={{0,14},{1,15},{2,0},{3,1},{4,2},{5,3},{6,4},{7,5},{8,6},{9,7},{10,... | collective-permute-start | bytes 344072 | tf_op jit(solution)/shard_map/ppermute | solution.py:424
  63.9 5.2 %collective-permute-start.19 = (bf16[448,128]{1,0:T(8,128)(2,1)S(1)}, bf16[448,128]{1,0:T(8,128)(2,1)S(1)}, u32[]{:S(2)}, u32[]{:S(2)}) collective-permute-start(bf16[448,128]{1,0:T(8,128)(2,1)S(1)} %add_convert_fusion.4), channel_id=1, source_target_pairs={{0,2},{1,3},{2,4},{3,5},{4,6},{5,7},{6,8},{7,9},{8,10},{9,11},{10,... | collective-permute-start | bytes 344072 | tf_op jit(solution)/shard_map/ppermute | solution.py:424
  66.0 4.9 %collective-permute-start.15 = (bf16[448,128]{1,0:T(8,128)(2,1)S(1)}, bf16[448,128]{1,0:T(8,128)(2,1)S(1)}, u32[]{:S(2)}, u32[]{:S(2)}) collective-permute-start(bf16[448,128]{1,0:T(8,128)(2,1)S(1)} %add_convert_fusion.6), channel_id=1, source_target_pairs={{0,14},{1,15},{2,0},{3,1},{4,2},{5,3},{6,4},{7,5},{8,6},{9,7},{10,... | collective-permute-start | bytes 344072 | tf_op jit(solution)/shard_map/ppermute | solution.py:424
  66.8 5.8 %collective-permute-start.14 = (bf16[448,128]{1,0:T(8,128)(2,1)S(1)}, bf16[448,128]{1,0:T(8,128)(2,1)S(1)}, u32[]{:S(2)}, u32[]{:S(2)}) collective-permute-start(bf16[448,128]{1,0:T(8,128)(2,1)S(1)} %add_convert_fusion.7), channel_id=1, source_target_pairs={{0,2},{1,3},{2,4},{3,5},{4,6},{5,7},{6,8},{7,9},{8,10},{9,11},{10,... | collective-permute-start | bytes 344072 | tf_op jit(solution)/shard_map/ppermute | solution.py:424
  69.2 5.1 %collective-permute-start.22 = (bf16[448,128]{1,0:T(8,128)(2,1)S(1)}, bf16[448,128]{1,0:T(8,128)(2,1)S(1)}, u32[]{:S(2)}, u32[]{:S(2)}) collective-permute-start(bf16[448,128]{1,0:T(8,128)(2,1)S(1)} %add_convert_fusion.1), channel_id=1, source_target_pairs={{0,14},{1,15},{2,0},{3,1},{4,2},{5,3},{6,4},{7,5},{8,6},{9,7},{10,... | collective-permute-start | bytes 344072 | tf_op jit(solution)/shard_map/ppermute | solution.py:424
  69.8 5.7 %collective-permute-start.21 = (bf16[448,128]{1,0:T(8,128)(2,1)S(1)}, bf16[448,128]{1,0:T(8,128)(2,1)S(1)}, u32[]{:S(2)}, u32[]{:S(2)}) collective-permute-start(bf16[448,128]{1,0:T(8,128)(2,1)S(1)} %add_convert_fusion.2), channel_id=1, source_target_pairs={{0,2},{1,3},{2,4},{3,5},{4,6},{5,7},{6,8},{7,9},{8,10},{9,11},{10,... | collective-permute-start | bytes 344072 | tf_op jit(solution)/shard_map/ppermute | solution.py:424
  72.7 4.5 %collective-permute-start.23 = (bf16[448,128]{1,0:T(8,128)(2,1)S(1)}, bf16[448,128]{1,0:T(8,128)(2,1)S(1)}, u32[]{:S(2)}, u32[]{:S(2)}) collective-permute-start(bf16[448,128]{1,0:T(8,128)(2,1)S(1)} %add_convert_fusion), channel_id=1, source_target_pairs={{0,14},{1,15},{2,0},{3,1},{4,2},{5,3},{6,4},{7,5},{8,6},{9,7},{10,... | collective-permute-start | bytes 344072 | tf_op jit(solution)/shard_map/ppermute | solution.py:424
  72.8 5.3 %collective-permute-start.16 = (bf16[448,128]{1,0:T(8,128)(2,1)S(1)}, bf16[448,128]{1,0:T(8,128)(2,1)S(1)}, u32[]{:S(2)}, u32[]{:S(2)}) collective-permute-start(bf16[448,128]{1,0:T(8,128)(2,1)S(1)} %add_convert_fusion.5), channel_id=1, source_target_pairs={{0,2},{1,3},{2,4},{3,5},{4,6},{5,7},{6,8},{7,9},{8,10},{9,11},{10,... | collective-permute-start | bytes 344072 | tf_op jit(solution)/shard_map/ppermute | solution.py:424
  78.4 5.4 %collective-permute-start.30 = (bf16[464,128]{1,0:T(8,128)(2,1)S(1)}, bf16[464,128]{1,0:T(8,128)(2,1)S(1)}, u32[]{:S(2)}, u32[]{:S(2)}) collective-permute-start(bf16[464,128]{1,0:T(8,128)(2,1)S(1)} %get-tuple-element.80.refs_0_), channel_id=1, source_target_pairs={{0,2},{1,3},{2,4},{3,5},{4,6},{5,7},{6,8},{7,9},{8,10},{9,11},{10,... | collective-permute-start | bytes 356360 | tf_op jit(solution)/shard_map/ppermute | solution.py:424
  78.8 5.0 %collective-permute-start.31 = (bf16[464,128]{1,0:T(8,128)(2,1)S(1)}, bf16[464,128]{1,0:T(8,128)(2,1)S(1)}, u32[]{:S(2)}, u32[]{:S(2)}) collective-permute-start(bf16[464,128]{1,0:T(8,128)(2,1)S(1)} %get-tuple-element.79.refs_1_), channel_id=1, source_target_pairs={{0,14},{1,15},{2,0},{3,1},{4,2},{5,3},{6,4},{7,5},{8,6},{9,7},{10,... | collective-permute-start | bytes 356360 | tf_op jit(solution)/shard_map/ppermute | solution.py:424
  81.1 5.4 %collective-permute-start.24 = (bf16[464,128]{1,0:T(8,128)(2,1)S(1)}, bf16[464,128]{1,0:T(8,128)(2,1)S(1)}, u32[]{:S(2)}, u32[]{:S(2)}) collective-permute-start(bf16[464,128]{1,0:T(8,128)(2,1)S(1)} %get-tuple-element.79.refs_1_), channel_id=1, source_target_pairs={{0,2},{1,3},{2,4},{3,5},{4,6},{5,7},{6,8},{7,9},{8,10},{9,11},{10,... | collective-permute-start | bytes 356360 | tf_op jit(solution)/shard_map/ppermute | solution.py:424
  81.1 5.4 %collective-permute-start.25 = (bf16[464,128]{1,0:T(8,128)(2,1)S(1)}, bf16[464,128]{1,0:T(8,128)(2,1)S(1)}, u32[]{:S(2)}, u32[]{:S(2)}) collective-permute-start(bf16[464,128]{1,0:T(8,128)(2,1)S(1)} %get-tuple-element.80.refs_0_), channel_id=1, source_target_pairs={{0,14},{1,15},{2,0},{3,1},{4,2},{5,3},{6,4},{7,5},{8,6},{9,7},{10,... | collective-permute-start | bytes 356360 | tf_op jit(solution)/shard_map/ppermute | solution.py:424
  83.8 6.1 %collective-permute-start.32 = (bf16[464,128]{1,0:T(8,128)(2,1)S(1)}, bf16[464,128]{1,0:T(8,128)(2,1)S(1)}, u32[]{:S(2)}, u32[]{:S(2)}) collective-permute-start(bf16[464,128]{1,0:T(8,128)(2,1)S(1)} %collective-permute-done.30.refs_2_), channel_id=1, source_target_pairs={{0,2},{1,3},{2,4},{3,5},{4,6},{5,7},{6,8},{7,9},{8,10},{9,11},{10,... | collective-permute-start | bytes 356360 | tf_op jit(solution)/shard_map/ppermute | solution.py:424
  83.8 6.1 %collective-permute-start.33 = (bf16[464,128]{1,0:T(8,128)(2,1)S(1)}, bf16[464,128]{1,0:T(8,128)(2,1)S(1)}, u32[]{:S(2)}, u32[]{:S(2)}) collective-permute-start(bf16[464,128]{1,0:T(8,128)(2,1)S(1)} %collective-permute-done.31.refs_3_), channel_id=1, source_target_pairs={{0,14},{1,15},{2,0},{3,1},{4,2},{5,3},{6,4},{7,5},{8,6},{9,7},{10,... | collective-permute-start | bytes 356360 | tf_op jit(solution)/shard_map/ppermute | solution.py:424
  86.5 6.2 %collective-permute-start.26 = (bf16[464,128]{1,0:T(8,128)(2,1)S(1)}, bf16[464,128]{1,0:T(8,128)(2,1)S(1)}, u32[]{:S(2)}, u32[]{:S(2)}) collective-permute-start(bf16[464,128]{1,0:T(8,128)(2,1)S(1)} %collective-permute-done.24.refs_4_), channel_id=1, source_target_pairs={{0,2},{1,3},{2,4},{3,5},{4,6},{5,7},{6,8},{7,9},{8,10},{9,11},{10,... | collective-permute-start | bytes 356360 | tf_op jit(solution)/shard_map/ppermute | solution.py:424
  86.5 6.2 %collective-permute-start.27 = (bf16[464,128]{1,0:T(8,128)(2,1)S(1)}, bf16[464,128]{1,0:T(8,128)(2,1)S(1)}, u32[]{:S(2)}, u32[]{:S(2)}) collective-permute-start(bf16[464,128]{1,0:T(8,128)(2,1)S(1)} %collective-permute-done.25.refs_5_), channel_id=1, source_target_pairs={{0,14},{1,15},{2,0},{3,1},{4,2},{5,3},{6,4},{7,5},{8,6},{9,7},{10,... | collective-permute-start | bytes 356360 | tf_op jit(solution)/shard_map/ppermute | solution.py:424
  89.9 5.3 %collective-permute-start.34 = (bf16[464,128]{1,0:T(8,128)(2,1)S(1)}, bf16[464,128]{1,0:T(8,128)(2,1)S(1)}, u32[]{:S(2)}, u32[]{:S(2)}) collective-permute-start(bf16[464,128]{1,0:T(8,128)(2,1)S(1)} %collective-permute-done.32.refs_6_), channel_id=1, source_target_pairs={{0,2},{1,3},{2,4},{3,5},{4,6},{5,7},{6,8},{7,9},{8,10},{9,11},{10,... | collective-permute-start | bytes 356360 | tf_op jit(solution)/shard_map/ppermute | solution.py:424
  92.1 4.3 %collective-permute-start.35 = (bf16[464,128]{1,0:T(8,128)(2,1)S(1)}, bf16[464,128]{1,0:T(8,128)(2,1)S(1)}, u32[]{:S(2)}, u32[]{:S(2)}) collective-permute-start(bf16[464,128]{1,0:T(8,128)(2,1)S(1)} %collective-permute-done.33.refs_7_), channel_id=1, source_target_pairs={{0,14},{1,15},{2,0},{3,1},{4,2},{5,3},{6,4},{7,5},{8,6},{9,7},{10,... | collective-permute-start | bytes 356360 | tf_op jit(solution)/shard_map/ppermute | solution.py:424
  100.3 17.8 %collective-permute-start.39 = (bf16[5568,128]{1,0:T(8,128)(2,1)S(1)}, bf16[5568,128]{1,0:T(8,128)(2,1)S(1)}, u32[]{:S(2)}, u32[]{:S(2)}) collective-permute-start(bf16[5568,128]{1,0:T(8,128)(2,1)S(1)} %get-tuple-element.93), channel_id=1, source_target_pairs={{0,1},{1,0},{2,3},{3,2},{4,5},{5,4},{6,7},{7,6},{8,9},{9,8},{10,11... | collective-permute-start | bytes 4276232 | tf_op jit(solution)/shard_map/ppermute | solution.py:424
  108.3 5.9 %collective-permute-start.28 = (bf16[464,128]{1,0:T(8,128)(2,1)S(1)}, bf16[464,128]{1,0:T(8,128)(2,1)S(1)}, u32[]{:S(2)}, u32[]{:S(2)}) collective-permute-start(bf16[464,128]{1,0:T(8,128)(2,1)S(1)} %collective-permute-done.26.refs_8_), channel_id=1, source_target_pairs={{0,2},{1,3},{2,4},{3,5},{4,6},{5,7},{6,8},{7,9},{8,10},{9,11},{10,... | collective-permute-start | bytes 356360 | tf_op jit(solution)/shard_map/ppermute | solution.py:424
  109.8 4.5 %collective-permute-start.29 = (bf16[464,128]{1,0:T(8,128)(2,1)S(1)}, bf16[464,128]{1,0:T(8,128)(2,1)S(1)}, u32[]{:S(2)}, u32[]{:S(2)}) collective-permute-start(bf16[464,128]{1,0:T(8,128)(2,1)S(1)} %collective-permute-done.27.refs_9_), channel_id=1, source_target_pairs={{0,14},{1,15},{2,0},{3,1},{4,2},{5,3},{6,4},{7,5},{8,6},{9,7},{10,... | collective-permute-start | bytes 356360 | tf_op jit(solution)/shard_map/ppermute | solution.py:424
  111.0 5.4 %collective-permute-start.36 = (bf16[464,128]{1,0:T(8,128)(2,1)S(1)}, bf16[464,128]{1,0:T(8,128)(2,1)S(1)}, u32[]{:S(2)}, u32[]{:S(2)}) collective-permute-start(bf16[464,128]{1,0:T(8,128)(2,1)S(1)} %collective-permute-done.34.refs_10_), channel_id=1, source_target_pairs={{0,2},{1,3},{2,4},{3,5},{4,6},{5,7},{6,8},{7,9},{8,10},{9,11},{10,... | collective-permute-start | bytes 356360 | tf_op jit(solution)/shard_map/ppermute | solution.py:424
  111.2 5.5 %collective-permute-start.37 = (bf16[464,128]{1,0:T(8,128)(2,1)S(1)}, bf16[464,128]{1,0:T(8,128)(2,1)S(1)}, u32[]{:S(2)}, u32[]{:S(2)}) collective-permute-start(bf16[464,128]{1,0:T(8,128)(2,1)S(1)} %collective-permute-done.35.refs_11_), channel_id=1, source_target_pairs={{0,14},{1,15},{2,0},{3,1},{4,2},{5,3},{6,4},{7,5},{8,6},{9,7},{10,... | collective-permute-start | bytes 356360 | tf_op jit(solution)/shard_map/ppermute | solution.py:424
  116.8 3.3 %collective-permute-start.38 = (bf16[1856,128]{1,0:T(8,128)(2,1)S(1)}, bf16[1856,128]{1,0:T(8,128)(2,1)S(1)}, u32[]{:S(2)}, u32[]{:S(2)}) collective-permute-start(bf16[1856,128]{1,0:T(8,128)(2,1)S(1)} %constant_dynamic-update-slice_fusion.8.refs_0_), channel_id=1, source_target_pairs={{0,1},{1,0},{2,3},{3,2},{4,5},{5,4},{6,7},{7,6},{8,9},{9,8},{10,11... | collective-permute-start | bytes 1425416 | tf_op jit(solution)/shard_map/ppermute | solution.py:424
where the time goes:
time: 123 us
  starting transfers between devices  61.9 us (50%)
  waiting for transfers between devices  34.2 us (28%)
  Pallas kernels  22.8 us (19%)
  other arithmetic  1.3 us (1%)
  local copies, waits for them, and re-layouts  1.25 us (1%)
    ppermute x33, starting transfers between devices, send(): return lax.ppermute(x, 'tp', pairs)  55.7 us
    ppermute x33, waiting for transfers between devices, send(): return lax.ppermute(x, 'tp', pairs)  20 us
    pallas_call x1, Pallas kernels, project(): pl.pallas_call(project_kernel, out_shape=(half,) * (2 * CHIPS - 2) + (ful...  10.8 us
    pallas_call x3, Pallas kernels, assemble(): pl.pallas_call(functools.partial(assemble_kernel, places, fresh, last), o...  8.25 us
    ppermute x4, waiting for transfers between devices, spread_out(): up, down = (lax.ppermute(x, ('ctx', 'tp'), way) for way in pairs)  5.22 us
    ppermute x1, waiting for transfers between devices, spread_out(): lax.ppermute(up[:count], ('ctx', 'tp'), pairs[0])  4.76 us
    ppermute x4, starting transfers between devices, spread_out(): up, down = (lax.ppermute(x, ('ctx', 'tp'), way) for way in pairs)  4.29 us
    ppermute x1, waiting for transfers between devices, spread_out(): far = (lax.ppermute(up, ('ctx', 'tp'), pairs[0]),)  4.23 us
  transfers between devices with their start and end apart: 40, of which 19 were waited for; matrix products, arithmetic and copies ran while one was open for 1% of the time, Pallas kernels for 4%

commit v1 on v0

--- a/solution.py
+++ b/solution.py
@@ -26,8 +26,8 @@
 ROWS = SUB * TOKENS
 MSG = ROWS + 16
 
-UP = [(t, (t + 2) % 16) for t in range(16)]
-DOWN = [(t, (t - 2) % 16) for t in range(16)]
+WAY_A = [(t, (t + 2 if t // 2 % 2 == 0 else t - 2) % 16) for t in range(16)]
+WAY_B = [(t, (t - 2 if t // 2 % 2 == 0 else t + 2) % 16) for t in range(16)]
 PAIR = [(t, t ^ 1) for t in range(16)]
 
 SIDE = 4
@@ -215,12 +215,12 @@
 def project_kernel(
     place_ref, mine_ref, theirs_ref, own_hbm, other_hbm, sign_ref, turn_ref, spread_ref, *refs
 ):
-    o_refs, (own, other, sems) = refs[: 2 * CHIPS], refs[2 * CHIPS :]
-    core, chip = place_ref[1], place_ref[2]
+    o_refs, (own, other, sems) = refs[: CHIPS + 1], refs[CHIPS + 1 :]
+    core, chip, way = place_ref[1], place_ref[2], place_ref[5]
 
     def column(step):
         distance = 4 - (step + 1) // 2
-        offset = jnp.where(lax.rem(step, 2) == 0, -distance, distance)
+        offset = way * jnp.where(lax.rem(step, 2) == 0, -distance, distance)
         return lax.rem(chip + offset + CHIPS, CHIPS) * CHUNK + core * SHARE
 
     def fetches(step):
@@ -259,20 +259,21 @@
             @pl.when(step == n)
             def _(n=n):
                 for half in range(2):
-                    o_ref = o_refs[2 * n + half]
+                    o_ref, row = (o_refs[half], 0) if n == 0 else (o_refs[n + 1], half * ROWS)
                     for b in range(SUB):
                         piece = totals[half][:, b * BLOCK : (b + 1) * BLOCK]
-                        o_ref[b * TOKENS : (b + 1) * TOKENS, :] = piece.astype(o_ref.dtype)
+                        o_ref[row + b * TOKENS : row + (b + 1) * TOKENS, :] = piece.astype(o_ref.dtype)
 
 
 def project(place, mine, theirs, own, other, signs, turn, spread):
     half = jax.ShapeDtypeStruct((ROWS, BLOCK), jnp.bfloat16)
-    full = jax.ShapeDtypeStruct((ROWS, BLOCK), jnp.float32)
+    both = jax.ShapeDtypeStruct((2 * ROWS, BLOCK), jnp.bfloat16)
+    full = jax.ShapeDtypeStruct((2 * ROWS, BLOCK), jnp.float32)
     return pl.pallas_call(
         project_kernel,
-        out_shape=(half,) * (2 * CHIPS - 2) + (full,) * 2,
+        out_shape=(half,) * 2 + (both,) * (CHIPS - 2) + (full,),
         in_specs=[SMEM, VMEM, VMEM, HBM, HBM, VMEM, VMEM, VMEM],
-        out_specs=(VMEM,) * (2 * CHIPS),
+        out_specs=(VMEM,) * (CHIPS + 1),
         scratch_shapes=[
             pltpu.VMEM((CHIPS, WIDTH, SHARE), jnp.bfloat16),
             pltpu.VMEM((CHIPS, WIDTH, SHARE), jnp.bfloat16),
@@ -286,16 +287,17 @@
     )(place, mine, theirs, own, other, signs, turn, spread)
 
 
-def pack_kernel(own0, own1, up0, up1, down0, down1, o0_ref, o1_ref, square):
-    for own, up, down, out in ((own0, up0, down0, o0_ref), (own1, up1, down1, o1_ref)):
+def pack_kernel(own, one, two, out, square):
+    for half in range(2):
         lane = lax.broadcasted_iota(jnp.int32, (TOKENS, BLOCK), 1)
         columns = jnp.zeros((TOKENS, BLOCK), jnp.float32)
         for b in range(SUB):
-            rows = slice(b * TOKENS, (b + 1) * TOKENS)
-            came = up[rows, :].astype(jnp.float32) + down[rows, :].astype(jnp.float32)
+            rows = slice(half * ROWS + b * TOKENS, half * ROWS + (b + 1) * TOKENS)
+            came = one[rows, :].astype(jnp.float32) + two[rows, :].astype(jnp.float32)
             summed = (own[rows, :] + came) * (1.0 / math.sqrt(BLOCK))
             scale = jnp.max(jnp.abs(summed), axis=-1, keepdims=True) + 1e-06
-            out[rows, :] = (summed / scale).astype(jnp.bfloat16)
+            to = half * MSG + b * TOKENS
+            out[to : to + TOKENS, :] = (summed / scale).astype(jnp.bfloat16)
             columns = jnp.where(lane == b, scale, columns)
         square[...] = jnp.zeros((2 * BLOCK, BLOCK), jnp.float32)
         square[:TOKENS, :] = columns
@@ -304,46 +306,37 @@
         )
         upper = turned.astype(jnp.bfloat16).astype(jnp.float32)
         tail = jnp.concatenate([upper, turned - upper, jnp.zeros((8, BLOCK), jnp.float32)], 0)
-        out[ROWS:, :] = tail.astype(jnp.bfloat16)
-
-
-def pack(own, up, down):
-    shape = jax.ShapeDtypeStruct((MSG, BLOCK), jnp.bfloat16)
+        out[half * MSG + ROWS : (half + 1) * MSG, :] = tail.astype(jnp.bfloat16)
+
+
+def pack(own, one, two):
     return pl.pallas_call(
         pack_kernel,
-        out_shape=(shape, shape),
-        in_specs=[VMEM] * 6,
-        out_specs=(VMEM, VMEM),
+        out_shape=jax.ShapeDtypeStruct((2 * MSG, BLOCK), jnp.bfloat16),
+        in_specs=[VMEM] * 3,
+        out_specs=VMEM,
         scratch_shapes=[pltpu.VMEM((2 * BLOCK, BLOCK), jnp.float32)],
         compiler_params=pltpu.CompilerParams(vmem_limit_bytes=8 << 20),
         cost_estimate=pl.CostEstimate(flops=1 << 20, bytes_accessed=1 << 20, transcendentals=0),
         name="pack",
-    )(*own, *up, *down)
+    )(own, one, two)
 
 
 def assemble_kernel(places, fresh, last, index_ref, *refs):
     count = 1 + max(place[0] for place in places)
     arrays, refs = refs[:count], refs[count:]
-    joined = []
     if fresh:
-        out_ref, table, joined_ref, tails, sems, tail_sems, join_sems = refs
-        for n in range(count):
-            joined.append(
-                pltpu.make_async_copy(
-                    arrays[n], joined_ref.at[pl.ds(n * MSG, MSG), :], join_sems.at[n]
-                )
-            )
-            joined[-1].start()
+        out_ref, table, tails, sems, tail_sems = refs
     else:
         _, old_table, out_ref, table, tails, sems, tail_sems = refs[:7]
         if last:
             _, _, out_ref, scale_ref, table, tails, sems, tail_sems = refs
         table[...] = old_table[...]
-    core, chip = index_ref[0], index_ref[1]
+    core, chip, way = index_ref[1], index_ref[2], index_ref[5]
 
     def spot(swap, offset):
         side = (1 - core) if swap else core
-        return side, lax.rem(chip + offset + CHIPS, CHIPS)
+        return side, lax.rem(chip + way * offset + CHIPS, CHIPS)
 
     copies, tail_copies = [], []
     for n, (array, row, swap, offset, half) in enumerate(places):
@@ -379,7 +372,7 @@
             for side in range(2):
                 row = (2 * place + side) * 2 * SUB
                 scale_ref[row : row + 2 * SUB, :] = table[place, side][:, :TOKENS]
-    for copy in joined + copies:
+    for copy in copies:
         copy.wait()
 
 
@@ -391,29 +384,22 @@
     )
     scratch = [pltpu.VMEM(table_shape, jnp.float32)] if last else []
     fresh = before is None
-    out_specs, more = [ANY, VMEM], []
-    if fresh:
-        out_shape.append(jax.ShapeDtypeStruct((len(arrays) * MSG, BLOCK), jnp.bfloat16))
-        out_specs.append(ANY)
-        more = [pltpu.SemaphoreType.DMA((len(arrays),))]
-    payload = pl.pallas_call(
+    return pl.pallas_call(
         functools.partial(assemble_kernel, places, fresh, last),
         out_shape=tuple(out_shape),
         in_specs=[SMEM] + [ANY] * len(arrays) + ([] if fresh else [ANY, VMEM]),
-        out_specs=tuple(out_specs),
+        out_specs=(ANY, VMEM),
         scratch_shapes=scratch
         + [
             pltpu.VMEM((len(places), 16, BLOCK), jnp.bfloat16),
             pltpu.SemaphoreType.DMA((len(places) * SUB,)),
             pltpu.SemaphoreType.DMA((len(places),)),
-            *more,
         ],
         input_output_aliases={} if fresh else {len(arrays) + 1: 0},
         compiler_params=pltpu.CompilerParams(vmem_limit_bytes=4 << 20),
         cost_estimate=pl.CostEstimate(flops=1 << 20, bytes_accessed=4 << 20, transcendentals=0),
         name="assemble",
     )(index, *arrays, *([] if fresh else before))
-    return (payload[2], *payload[:2]) if fresh else payload
 
 
 def add(arrived, own):
@@ -422,16 +408,15 @@
 
 def send(x, pairs):
     return lax.ppermute(x, "tp", pairs)
-
-
-EARLY = 12
 
 
 def layer(queries, keys, values, out_weight, signs):
     ctx, tp = lax.axis_index("ctx"), lax.axis_index("tp")
     core, chip = tp & 1, tp >> 1
 
-    place = jnp.stack([ctx * TOKENS, core, chip, ctx >> 2, ctx & 3]).astype(jnp.int32)
+    place = jnp.stack(
+        [ctx * TOKENS, core, chip, ctx >> 2, ctx & 3, 1 - 2 * (chip & 1)]
+    ).astype(jnp.int32)
 
     other_weight = send(out_weight, PAIR)
 
@@ -453,7 +438,6 @@
     held = spread_out(held, SECOND)
     swapped = send(held, PAIR)
 
-    index = jnp.stack([core, chip]).astype(jnp.int32)
     turn = jnp.asarray(turn_matrix(), jnp.bfloat16)
     spread = jnp.asarray(spread_matrix(), jnp.bfloat16)
     attended = attention(place, queries, held, swapped)
@@ -468,48 +452,48 @@
         spread,
     )
 
-    def plus(arrived, up, down):
-        arrived = lax.optimization_barrier(arrived)
-        return add(arrived[0], up), add(arrived[1], down)
-
-    def both_ways(up, down):
-        up = send(up, UP)
-        down = send(down, DOWN)
-        return up, down
-
-    a = both_ways(parts[0], parts[1])
-    b = both_ways(parts[3], parts[4])
-    a = both_ways(*plus(a, parts[2], parts[5]))
-    for near in (6, 10):
-        b = both_ways(*plus(b, parts[near + 1], parts[near + 2]))
-        a = both_ways(*plus(a, parts[near], parts[near + 3]))
-    packed = pack(parts[14:], (a[0], b[0]), (b[1], a[1]))
-
-    pieces, spots = list(packed), [(0, 0), (0, 1)]
-    chains = [(packed[0], packed[1]), (packed[1], packed[0])]
-    for step in range(7):
-        h, hop = step % 2, step // 2 + 1
-        chains[h] = both_ways(*lax.optimization_barrier(chains[h]))
-        pieces += chains[h]
-        spots += [(-hop, h), (hop, 1 - h)]
-
-    def rows(swap, a, b, joined):
-        return tuple(
-            (0 if joined else n - a, (n - a) * MSG if joined else 0, swap, *spots[n])
-            for n in range(a, b)
-        )
-
-    first = assemble(index, pieces[:EARLY], rows(False, 0, EARLY, False), None, False)
-    early, *first = first
-    early = send(early, PAIR)
-    rest = jnp.concatenate(pieces[EARLY:], 0)
-    late = send(rest, PAIR)
-    second = assemble(index, [early], rows(True, 0, EARLY, True), first, False)
-    count = len(pieces) - EARLY
-    tail = rows(False, EARLY, EARLY + count, True) + tuple(
-        (1, *where[1:]) for where in rows(True, EARLY, EARLY + count, True)
-    )
-    payload, scales = assemble(index, [rest, late], tail, second, True)
+    def exchange(for_a, for_b):
+        came_b = send(for_a, WAY_A)
+        came_a = send(for_b, WAY_B)
+        return came_a, came_b
+
+    came_a, came_b = exchange(parts[0], parts[1])
+    for_a, for_b = parts[2], parts[3]
+    for_a = lax.dynamic_update_slice(for_a, add(came_a, for_a[ROWS:]), (ROWS, 0))
+    for_b = lax.dynamic_update_slice(for_b, add(came_b, for_b[:ROWS]), (0, 0))
+    came_a, came_b = exchange(for_a, for_b)
+    came_a, came_b = exchange(add(came_a, parts[4]), add(came_b, parts[5]))
+    came_a, came_b = exchange(add(came_a, parts[6]), add(came_b, parts[7]))
+    packed = pack(parts[8], came_a, came_b)
+
+    stages = [[(packed, 0, None)]]
+    came_a = came_b = packed
+    for hop in range(1, 5):
+        if hop < 4:
+            came_a, came_b = exchange(came_a, came_b)
+            stages.append([(came_a, -hop, None), (came_b, hop, None)])
+        else:
+            came_a, came_b = exchange(came_a[:MSG], came_b[MSG:])
+            stages.append([(came_a, hop, 1), (came_b, hop, 0)])
+    swapped_stages = []
+    for stage in stages:
+        swapped_stages.append([(send(array, PAIR), *rest) for array, *rest in stage])
+
+    def gather(hops, before, last=False):
+        arrays, places = [], []
+        for swap, source in ((False, stages), (True, swapped_stages)):
+            for hop in hops:
+                for array, offset, half in source[hop]:
+                    for h in (0, 1) if half is None else (half,):
+                        row = h * MSG if half is None else 0
+                        places.append((len(arrays), row, swap, offset, h))
+                    arrays.append(array)
+        return assemble(place, arrays, tuple(places), before, last)
+
+    result = gather((0, 1), None)
+    result = gather((2,), result)
+    result = gather((3,), result)
+    payload, scales = gather((4,), result, True)
     return payload, scales.T
 
 

time: 123 us -> 125 us (1.016)
  waiting for transfers between devices: 34.2 us -> 44.8 us
  starting transfers between devices: 61.9 us -> 54.3 us
    ppermute x33 -> x28, waiting for transfers between devices: 20 us -> 30.6 us  [send(): return lax.ppermute(x, 'tp', pairs)]
    ppermute x33 -> x28, starting transfers between devices: 55.7 us -> 48.1 us  [send(): return lax.ppermute(x, 'tp', pairs)]
    pallas_call x3 -> x4, Pallas kernels: 8.25 us -> 7.48 us  [assemble(): pl.pallas_call(functools.partial(assemble_kernel, places, fresh, last), o...]
  transfers between devices with their start and end apart: 40 -> 35, of which waited for: 19 -> 16; matrix products, arithmetic and copies ran while one was open for 1% -> 1% of each run, Pallas kernels for 4% -> 7%
where the time goes in v1:
time: 125 us
  starting transfers between devices  54.3 us (43%)
  waiting for transfers between devices  44.8 us (36%)
  Pallas kernels  22 us (18%)
  other arithmetic  1.36 us (1%)
    ppermute x28, starting transfers between devices, send(): return lax.ppermute(x, 'tp', pairs)  48.1 us
    ppermute x28, waiting for transfers between devices, send(): return lax.ppermute(x, 'tp', pairs)  30.6 us
    pallas_call x1, Pallas kernels, project(): pl.pallas_call(project_kernel, out_shape=(half,) * 2 + (both,) * (CHIPS -...  10.8 us
    pallas_call x4, Pallas kernels, assemble(): pl.pallas_call(functools.partial(assemble_kernel, places, fresh, last), o...  7.48 us
    ppermute x4, waiting for transfers between devices, spread_out(): up, down = (lax.ppermute(x, ('ctx', 'tp'), way) for way in pairs)  5.22 us
    ppermute x1, waiting for transfers between devices, spread_out(): lax.ppermute(up[:count], ('ctx', 'tp'), pairs[0])  4.76 us
    ppermute x4, starting transfers between devices, spread_out(): up, down = (lax.ppermute(x, ('ctx', 'tp'), way) for way in pairs)  4.29 us
    ppermute x1, waiting for transfers between devices, spread_out(): far = (lax.ppermute(up, ('ctx', 'tp'), pairs[0]),)  4.23 us
  transfers between devices with their start and end apart: 35, of which 16 were waited for; matrix products, arithmetic and copies ran while one was open for 1% of the time, Pallas kernels for 7%

profile of v1, /device:TPU:1, one launch (start us, length us, event | category | flops | bytes accessed | tf_op | source)
XLA Modules:
  0.0 124.7 jit_solution(3155678975000467796)
XLA Ops:
  0.6 3.3 %collective-permute-start.9 = (bf16[512,8192]{1,0:T(8,128)(2,1)}, bf16[512,8192]{1,0:T(8,128)(2,1)}, u32[]{:S(2)}, u32[]{:S(2)}) collective-permute-start(bf16[512,8192]{1,0:T(8,128)(2,1)} %own_hbm.1), channel_id=1, source_target_pairs={{0,1},{1,0},{2,3},{3,2},{4,5},{5,4},{6,7},{7,6},{8,9},{9,8},{10,11... | collective-permute-start | bytes 25165832 | tf_op jit(solution)/shard_map/ppermute | solution.py:410
  3.9 0.9 constant_dynamic-update-slice_fusion.7
  4.8 0.1 collective-permute-start
  4.9 2.7 %collective-permute-start.1 = (bf16[224,128]{1,0:T(8,128)(2,1)S(1)}, bf16[224,128]{1,0:T(8,128)(2,1)S(1)}, u32[]{:S(2)}, u32[]{:S(2)}) collective-permute-start(bf16[224,128]{1,0:T(8,128)(2,1)S(1)} %get-tuple-element.37), channel_id=1, source_target_pairs={{0,48},{1,193},{2,50},{3,195},{4,52},{5,197},{6,54},{7,199},{8,56}... | collective-permute-start | bytes 172040 | tf_op jit(solution)/shard_map/ppermute | solution.py:424
  7.5 1.9 %collective-permute-done = bf16[224,128]{1,0:T(8,128)(2,1)S(1)} collective-permute-done((bf16[224,128]{1,0:T(8,128)(2,1)S(1)}, bf16[224,128]{1,0:T(8,128)(2,1)S(1)}, u32[]{:S(2)}, u32[]{:S(2)}) %collective-permute-start) | collective-permute-done | bytes 57376 | tf_op jit(solution)/shard_map/ppermute | solution.py:424
  9.4 4.2 %collective-permute-done.2 = bf16[224,128]{1,0:T(8,128)(2,1)S(1)} collective-permute-done((bf16[224,128]{1,0:T(8,128)(2,1)S(1)}, bf16[224,128]{1,0:T(8,128)(2,1)S(1)}, u32[]{:S(2)}, u32[]{:S(2)}) %collective-permute-start.2) | collective-permute-done | bytes 57376 | tf_op jit(solution)/shard_map/ppermute | solution.py:427
  13.7 0.6 collective-permute-start.4
  14.3 0.9 collective-permute-start.3
  15.3 3.4 %collective-permute-done.4 = bf16[896,128]{1,0:T(8,128)(2,1)S(1)} collective-permute-done((bf16[896,128]{1,0:T(8,128)(2,1)S(1)}, bf16[896,128]{1,0:T(8,128)(2,1)S(1)}, u32[]{:S(2)}, u32[]{:S(2)}) %collective-permute-start.4) | collective-permute-done | bytes 229408 | tf_op jit(solution)/shard_map/ppermute | solution.py:424
  18.6 1.8 %collective-permute-start.6 = (bf16[448,128]{1,0:T(8,128)(2,1)S(1)}, bf16[448,128]{1,0:T(8,128)(2,1)S(1)}, u32[]{:S(2)}, u32[]{:S(2)}) collective-permute-start(bf16[448,128]{1,0:T(8,128)(2,1)S(1)} %slice.25), channel_id=1, source_target_pairs={{0,192},{1,49},{2,194},{3,51},{4,196},{5,53},{6,198},{7,55},{8,200... | collective-permute-start | bytes 344072 | tf_op jit(solution)/shard_map/ppermute | solution.py:431
  20.5 0.0 copy-start
  20.5 0.0 copy-start.1
  20.5 0.0 copy-start.2
  20.5 0.1 collective-permute-start.5
  20.7 4.8 %collective-permute-done.5 = bf16[448,128]{1,0:T(8,128)(2,1)S(1)} collective-permute-done((bf16[448,128]{1,0:T(8,128)(2,1)S(1)}, bf16[448,128]{1,0:T(8,128)(2,1)S(1)}, u32[]{:S(2)}, u32[]{:S(2)}) %collective-permute-start.5) | collective-permute-done | bytes 114720 | tf_op jit(solution)/shard_map/ppermute | solution.py:430
  25.5 5.2 %collective-permute-start.7 = (bf16[3584,128]{1,0:T(8,128)(2,1)S(1)}, bf16[3584,128]{1,0:T(8,128)(2,1)S(1)}, u32[]{:S(2)}, u32[]{:S(2)}) collective-permute-start(bf16[3584,128]{1,0:T(8,128)(2,1)S(1)} %constant_dynamic-update-slice_fusion.held_ref), channel_id=1, source_target_pairs={{0,1},{1,0},{2,3},{3,2},{4,5},{5,4},{6,7},{7,6},{8,9},{9,8},{10,11... | collective-permute-start | bytes 2752520 | tf_op jit(solution)/shard_map/ppermute | solution.py:410
  30.7 0.1 stack.27.place_ref.index_ref
  30.8 2.0 %collective-permute-done.7.swapped_ref = bf16[3584,128]{1,0:T(8,128)(2,1)S(1)} collective-permute-done((bf16[3584,128]{1,0:T(8,128)(2,1)S(1)}, bf16[3584,128]{1,0:T(8,128)(2,1)S(1)}, u32[]{:S(2)}, u32[]{:S(2)}) %collective-permute-start.7) | collective-permute-done | bytes 917536 | tf_op jit(solution)/shard_map/ppermute | solution.py:410
  32.8 0.9 copy-done.3
  33.7 3.5 %attend.1.mine_ref = bf16[224,512]{1,0:T(8,128)(2,1)S(1)} custom-call(s32[6]{0:T(128)S(1)} %stack.27.place_ref.index_ref, bf16[224,512]{1,0:T(8,128)(2,1)S(1)} %copy-done.3, bf16[3584,128]{1,0:T(8,128)(2,1)S(1)} %constant_dynamic-update-slice_fusion.held_ref, bf16[3584,128]{1,0:T(8,128)(2,1)S(1)} %collective-permute-done.7.swapped_ref), custom_call_target="tpu_custom_call" | custom-call | flops 1644167168 | bytes 3145728 | tf_op jit(solution)/shard_map/attend/pallas_call | solution.py:195
  37.2 0.5 collective-permute-start.8
  37.7 1.1 collective-permute-done.8.theirs_ref
  38.8 10.8 %project.1 = (bf16[448,128]{1,0:T(8,128)(2,1)S(1)}, bf16[448,128]{1,0:T(8,128)(2,1)S(1)}, bf16[896,128]{1,0:T(8,128)(2,1)S(1)}, bf16[896,128]{1,0:T(8,128)(2,1)S...) custom-call(s32[6]{0:T(128)S(1)} %stack.27.place_ref.index_ref, ...), custom_call_target="tpu_custom_call" | custom-call | flops 2348810240 | bytes 10485760 | tf_op jit(solution)/shard_map/project/pallas_call | solution.py:272
  49.6 5.6 %collective-permute-start.14 = (bf16[448,128]{1,0:T(8,128)(2,1)S(1)}, bf16[448,128]{1,0:T(8,128)(2,1)S(1)}, u32[]{:S(2)}, u32[]{:S(2)}) collective-permute-start(bf16[448,128]{1,0:T(8,128)(2,1)S(1)} %get-tuple-element.25), channel_id=1, source_target_pairs={{0,14},{1,15},{2,4},{3,5},{4,2},{5,3},{6,8},{7,9},{8,6},{9,7},{10,... | collective-permute-start | bytes 344072 | tf_op jit(solution)/shard_map/ppermute | solution.py:410
  55.3 3.1 %collective-permute-done.14 = bf16[448,128]{1,0:T(8,128)(2,1)S(1)} collective-permute-done((bf16[448,128]{1,0:T(8,128)(2,1)S(1)}, bf16[448,128]{1,0:T(8,128)(2,1)S(1)}, u32[]{:S(2)}, u32[]{:S(2)}) %collective-permute-start.14) | collective-permute-done | bytes 114720 | tf_op jit(solution)/shard_map/ppermute | solution.py:410
  58.4 0.1 fusion.1
  58.5 0.3 collective-permute-start.15
  58.8 0.5 collective-permute-done.10
  59.3 0.1 fusion
  59.4 2.0 %collective-permute-start.11 = (bf16[896,128]{1,0:T(8,128)(2,1)S(1)}, bf16[896,128]{1,0:T(8,128)(2,1)S(1)}, u32[]{:S(2)}, u32[]{:S(2)}) collective-permute-start(bf16[896,128]{1,0:T(8,128)(2,1)S(1)} %fusion), channel_id=1, source_target_pairs={{0,14},{1,15},{2,4},{3,5},{4,2},{5,3},{6,8},{7,9},{8,6},{9,7},{10,... | collective-permute-start | bytes 688136 | tf_op jit(solution)/shard_map/ppermute | solution.py:410
  61.4 3.6 %collective-permute-done.15 = bf16[896,128]{1,0:T(8,128)(2,1)S(1)} collective-permute-done((bf16[896,128]{1,0:T(8,128)(2,1)S(1)}, bf16[896,128]{1,0:T(8,128)(2,1)S(1)}, u32[]{:S(2)}, u32[]{:S(2)}) %collective-permute-start.15) | collective-permute-done | bytes 229408 | tf_op jit(solution)/shard_map/ppermute | solution.py:410
  65.0 0.1 add_convert_fusion.1
  65.1 2.2 %collective-permute-start.16 = (bf16[896,128]{1,0:T(8,128)(2,1)S(1)}, bf16[896,128]{1,0:T(8,128)(2,1)S(1)}, u32[]{:S(2)}, u32[]{:S(2)}) collective-permute-start(bf16[896,128]{1,0:T(8,128)(2,1)S(1)} %add_convert_fusion.1), channel_id=1, source_target_pairs={{0,14},{1,15},{2,4},{3,5},{4,2},{5,3},{6,8},{7,9},{8,6},{9,7},{10,... | collective-permute-start | bytes 688136 | tf_op jit(solution)/shard_map/ppermute | solution.py:410
  67.3 0.1 add_convert_fusion.3
  67.3 0.1 collective-permute-start.12
  67.4 4.3 %collective-permute-done.16 = bf16[896,128]{1,0:T(8,128)(2,1)S(1)} collective-permute-done((bf16[896,128]{1,0:T(8,128)(2,1)S(1)}, bf16[896,128]{1,0:T(8,128)(2,1)S(1)}, u32[]{:S(2)}, u32[]{:S(2)}) %collective-permute-start.16) | collective-permute-done | bytes 229408 | tf_op jit(solution)/shard_map/ppermute | solution.py:410
  71.7 0.1 add_convert_fusion
  71.8 0.1 collective-permute-start.17
  71.9 0.7 collective-permute-done.12
  72.6 0.1 add_convert_fusion.2
  72.6 1.4 %collective-permute-start.13 = (bf16[896,128]{1,0:T(8,128)(2,1)S(1)}, bf16[896,128]{1,0:T(8,128)(2,1)S(1)}, u32[]{:S(2)}, u32[]{:S(2)}) collective-permute-start(bf16[896,128]{1,0:T(8,128)(2,1)S(1)} %add_convert_fusion.2), channel_id=1, source_target_pairs={{0,14},{1,15},{2,4},{3,5},{4,2},{5,3},{6,8},{7,9},{8,6},{9,7},{10,... | collective-permute-start | bytes 688136 | tf_op jit(solution)/shard_map/ppermute | solution.py:410
  74.0 4.0 %collective-permute-done.17.two = bf16[896,128]{1,0:T(8,128)(2,1)S(1)} collective-permute-done((bf16[896,128]{1,0:T(8,128)(2,1)S(1)}, bf16[896,128]{1,0:T(8,128)(2,1)S(1)}, u32[]{:S(2)}, u32[]{:S(2)}) %collective-permute-start.17) | collective-permute-done | bytes 229408 | tf_op jit(solution)/shard_map/ppermute | solution.py:410
  78.0 0.8 collective-permute-done.13.one
  78.8 0.3 pack.1.refs_0_
  79.1 1.3 %collective-permute-start.22 = (bf16[928,128]{1,0:T(8,128)(2,1)S(1)}, bf16[928,128]{1,0:T(8,128)(2,1)S(1)}, u32[]{:S(2)}, u32[]{:S(2)}) collective-permute-start(bf16[928,128]{1,0:T(8,128)(2,1)S(1)} %pack.1.refs_0_), channel_id=1, source_target_pairs={{0,14},{1,15},{2,4},{3,5},{4,2},{5,3},{6,8},{7,9},{8,6},{9,7},{10,... | collective-permute-start | bytes 712712 | tf_op jit(solution)/shard_map/ppermute | solution.py:410
  80.4 5.5 %collective-permute-done.22.refs_1_ = bf16[928,128]{1,0:T(8,128)(2,1)S(1)} collective-permute-done((bf16[928,128]{1,0:T(8,128)(2,1)S(1)}, bf16[928,128]{1,0:T(8,128)(2,1)S(1)}, u32[]{:S(2)}, u32[]{:S(2)}) %collective-permute-start.22) | collective-permute-done | bytes 237600 | tf_op jit(solution)/shard_map/ppermute | solution.py:410
  85.9 0.9 collective-permute-start.19
  86.8 8.3 %collective-permute-start.32 = (bf16[928,128]{1,0:T(8,128)(2,1)S(1)}, bf16[928,128]{1,0:T(8,128)(2,1)S(1)}, u32[]{:S(2)}, u32[]{:S(2)}) collective-permute-start(bf16[928,128]{1,0:T(8,128)(2,1)S(1)} %pack.1.refs_0_), channel_id=1, source_target_pairs={{0,1},{1,0},{2,3},{3,2},{4,5},{5,4},{6,7},{7,6},{8,9},{9,8},{10,11... | collective-permute-start | bytes 712712 | tf_op jit(solution)/shard_map/ppermute | solution.py:410
  95.1 2.2 %collective-permute-start.24 = (bf16[928,128]{1,0:T(8,128)(2,1)S(1)}, bf16[928,128]{1,0:T(8,128)(2,1)S(1)}, u32[]{:S(2)}, u32[]{:S(2)}) collective-permute-start(bf16[928,128]{1,0:T(8,128)(2,1)S(1)} %collective-permute-done.23.refs_1_), channel_id=1, source_target_pairs={{0,14},{1,15},{2,4},{3,5},{4,2},{5,3},{6,8},{7,9},{8,6},{9,7},{10,... | collective-permute-start | bytes 712712 | tf_op jit(solution)/shard_map/ppermute | solution.py:410
  97.2 0.7 collective-permute-start.20
  98.0 6.2 %collective-permute-start.34 = (bf16[928,128]{1,0:T(8,128)(2,1)S(1)}, bf16[928,128]{1,0:T(8,128)(2,1)S(1)}, u32[]{:S(2)}, u32[]{:S(2)}) collective-permute-start(bf16[928,128]{1,0:T(8,128)(2,1)S(1)} %collective-permute-done.18.refs_2_), channel_id=1, source_target_pairs={{0,1},{1,0},{2,3},{3,2},{4,5},{5,4},{6,7},{7,6},{8,9},{9,8},{10,11... | collective-permute-start | bytes 712712 | tf_op jit(solution)/shard_map/ppermute | solution.py:410
  104.1 0.5 collective-permute-start.30
  104.6 3.1 %collective-permute-start.28 = (bf16[928,128]{1,0:T(8,128)(2,1)S(1)}, bf16[928,128]{1,0:T(8,128)(2,1)S(1)}, u32[]{:S(2)}, u32[]{:S(2)}) collective-permute-start(bf16[928,128]{1,0:T(8,128)(2,1)S(1)} %collective-permute-done.24.refs_0_), channel_id=1, source_target_pairs={{0,1},{1,0},{2,3},{3,2},{4,5},{5,4},{6,7},{7,6},{8,9},{9,8},{10,11... | collective-permute-start | bytes 712712 | tf_op jit(solution)/shard_map/ppermute | solution.py:410
  107.7 2.2 %collective-permute-start.29 = (bf16[928,128]{1,0:T(8,128)(2,1)S(1)}, bf16[928,128]{1,0:T(8,128)(2,1)S(1)}, u32[]{:S(2)}, u32[]{:S(2)}) collective-permute-start(bf16[928,128]{1,0:T(8,128)(2,1)S(1)} %collective-permute-done.20.refs_1_), channel_id=1, source_target_pairs={{0,1},{1,0},{2,3},{3,2},{4,5},{5,4},{6,7},{7,6},{8,9},{9,8},{10,11... | collective-permute-start | bytes 712712 | tf_op jit(solution)/shard_map/ppermute | solution.py:410
  109.9 0.1 collective-permute-start.25
  110.1 0.1 collective-permute-start.21
  110.1 4.7 %collective-permute-done.25.refs_1_ = bf16[464,128]{1,0:T(8,128)(2,1)S(1)} collective-permute-done((bf16[464,128]{1,0:T(8,128)(2,1)S(1)}, bf16[464,128]{1,0:T(8,128)(2,1)S(1)}, u32[]{:S(2)}, u32[]{:S(2)}) %collective-permute-start.25) | collective-permute-done | bytes 118816 | tf_op jit(solution)/shard_map/ppermute | solution.py:410
  114.8 0.9 collective-permute-start.27
  115.7 0.2 collective-permute-done.21.refs_0_
  115.9 1.1 collective-permute-start.26
  117.0 2.0 %assemble.4 = (bf16[224,8192]{1,0:T(8,128)(2,1)}, f32[8,2,4,256]{3,2,1,0:T(4,128)S(1)}) custom-call(s32[6]{0:T(128)S(1)} %stack.27.place_ref.index_ref, bf16[928,128]{1,0:T(8,128)(2,1)S(1)} %pack.1.refs_0_, bf16[928,128]{1,0:T(8,128)(2,1)S(1)} %collective-permute-done.22.refs_1_, bf16[928,128]{1,0:T(8,128)(2,1)S(1)} %collective-permute-done.18.refs_2_, ...), custom_call_target="tpu_custom_call" | custom-call | flops 1048576 | bytes 4194304 | tf_op jit(solution)/shard_map/assemble/pallas_call | solution.py:387
  119.0 1.7 %assemble.5 = (bf16[224,8192]{1,0:T(8,128)(2,1)}, f32[8,2,4,256]{3,2,1,0:T(4,128)S(1)}) custom-call(s32[6]{0:T(128)S(1)} %stack.27.place_ref.index_ref, bf16[928,128]{1,0:T(8,128)(2,1)S(1)} %collective-permute-done.19.refs_0_, bf16[928,128]{1,0:T(8,128)(2,1)S(1)} %collective-permute-done.23.refs_1_, ...), custom_call_target="tpu_custom_call", output_to_operand_aliasing={{0}: (5, {})} | custom-call | flops 1048576 | bytes 4194304 | tf_op jit(solution)/shard_map/assemble/pallas_call | solution.py:387
  120.7 1.7 %assemble.6 = (bf16[224,8192]{1,0:T(8,128)(2,1)}, f32[8,2,4,256]{3,2,1,0:T(4,128)S(1)}) custom-call(s32[6]{0:T(128)S(1)} %stack.27.place_ref.index_ref, bf16[928,128]{1,0:T(8,128)(2,1)S(1)} %collective-permute-done.24.refs_0_, bf16[928,128]{1,0:T(8,128)(2,1)S(1)} %collective-permute-done.20.refs_1_, ...), custom_call_target="tpu_custom_call", output_to_operand_aliasing={{0}: (5, {})} | custom-call | flops 1048576 | bytes 4194304 | tf_op jit(solution)/shard_map/assemble/pallas_call | solution.py:387
  122.5 2.1 %assemble.7 = (bf16[224,8192]{1,0:T(8,128)(2,1)}, f32[64,224]{1,0:T(8,128)}) custom-call(s32[6]{0:T(128)S(1)} %stack.27.place_ref.index_ref, bf16[464,128]{1,0:T(8,128)(2,1)S(1)} %collective-permute-done.21.refs_0_, bf16[464,128]{1,0:T(8,128)(2,1)S(1)} %collective-permute-done.25.refs_1_, ...), custom_call_target="tpu_custom_call", output_to_operand_aliasing={{0}: (5, {})} | custom-call | flops 1048576 | bytes 4194304 | tf_op jit(solution)/shard_map/assemble/pallas_call | solution.py:387
  (41 shorter events, 0.3 us)
Async XLA Ops:
  0.6 38.2 %collective-permute-start.9 = (bf16[512,8192]{1,0:T(8,128)(2,1)}, bf16[512,8192]{1,0:T(8,128)(2,1)}, u32[]{:S(2)}, u32[]{:S(2)}) collective-permute-start(bf16[512,8192]{1,0:T(8,128)(2,1)} %own_hbm.1), channel_id=1, source_target_pairs={{0,1},{1,0},{2,3},{3,2},{4,5},{5,4},{6,7},{7,6},{8,9},{9,8},{10,11... | collective-permute-start | bytes 25165832 | tf_op jit(solution)/shard_map/ppermute | solution.py:410
  4.8 4.6 %collective-permute-start = (bf16[224,128]{1,0:T(8,128)(2,1)S(1)}, bf16[224,128]{1,0:T(8,128)(2,1)S(1)}, u32[]{:S(2)}, u32[]{:S(2)}) collective-permute-start(bf16[224,128]{1,0:T(8,128)(2,1)S(1)} %get-tuple-element.37), channel_id=1, source_target_pairs={{0,16},{1,65},{2,18},{3,67},{4,20},{5,69},{6,22},{7,71},{8,24},{9,... | collective-permute-start | bytes 172040 | tf_op jit(solution)/shard_map/ppermute | solution.py:424
  4.9 4.5 %collective-permute-start.1 = (bf16[224,128]{1,0:T(8,128)(2,1)S(1)}, bf16[224,128]{1,0:T(8,128)(2,1)S(1)}, u32[]{:S(2)}, u32[]{:S(2)}) collective-permute-start(bf16[224,128]{1,0:T(8,128)(2,1)S(1)} %get-tuple-element.37), channel_id=1, source_target_pairs={{0,48},{1,193},{2,50},{3,195},{4,52},{5,197},{6,54},{7,199},{8,56}... | collective-permute-start | bytes 172040 | tf_op jit(solution)/shard_map/ppermute | solution.py:424
  9.4 4.2 %collective-permute-start.2 = (bf16[224,128]{1,0:T(8,128)(2,1)S(1)}, bf16[224,128]{1,0:T(8,128)(2,1)S(1)}, u32[]{:S(2)}, u32[]{:S(2)}) collective-permute-start(bf16[224,128]{1,0:T(8,128)(2,1)S(1)} %collective-permute-done), channel_id=1, source_target_pairs={{0,16},{1,65},{2,18},{3,67},{4,20},{5,69},{6,22},{7,71},{8,24},{9,... | collective-permute-start | bytes 172040 | tf_op jit(solution)/shard_map/ppermute | solution.py:427
  13.7 4.9 %collective-permute-start.4 = (bf16[896,128]{1,0:T(8,128)(2,1)S(1)}, bf16[896,128]{1,0:T(8,128)(2,1)S(1)}, u32[]{:S(2)}, u32[]{:S(2)}) collective-permute-start(bf16[896,128]{1,0:T(8,128)(2,1)S(1)} %pad_maximum_fusion), channel_id=1, source_target_pairs={{0,192},{1,49},{2,194},{3,51},{4,196},{5,53},{6,198},{7,55},{8,200... | collective-permute-start | bytes 688136 | tf_op jit(solution)/shard_map/ppermute | solution.py:424
  14.3 6.2 %collective-permute-start.3 = (bf16[896,128]{1,0:T(8,128)(2,1)S(1)}, bf16[896,128]{1,0:T(8,128)(2,1)S(1)}, u32[]{:S(2)}, u32[]{:S(2)}) collective-permute-start(bf16[896,128]{1,0:T(8,128)(2,1)S(1)} %pad_maximum_fusion), channel_id=1, source_target_pairs={{0,64},{1,17},{2,66},{3,19},{4,68},{5,21},{6,70},{7,23},{8,72},{9,... | collective-permute-start | bytes 688136 | tf_op jit(solution)/shard_map/ppermute | solution.py:424
  18.6 6.8 %collective-permute-start.6 = (bf16[448,128]{1,0:T(8,128)(2,1)S(1)}, bf16[448,128]{1,0:T(8,128)(2,1)S(1)}, u32[]{:S(2)}, u32[]{:S(2)}) collective-permute-start(bf16[448,128]{1,0:T(8,128)(2,1)S(1)} %slice.25), channel_id=1, source_target_pairs={{0,192},{1,49},{2,194},{3,51},{4,196},{5,53},{6,198},{7,55},{8,200... | collective-permute-start | bytes 344072 | tf_op jit(solution)/shard_map/ppermute | solution.py:431
  20.5 18.4 %copy-start = (bf16[256,256]{1,0:T(8,128)(2,1)S(1)}, bf16[256,256]{1,0:T(8,128)(2,1)}, u32[]{:S(2)}) copy-start(bf16[256,256]{1,0:T(8,128)(2,1)} %constant.27.clone.turn_ref) | copy-start | bytes 393220
  20.5 18.3 %copy-start.1 = (bf16[128,256]{1,0:T(8,128)(2,1)S(1)}, bf16[128,256]{1,0:T(8,128)(2,1)}, u32[]{:S(2)}) copy-start(bf16[128,256]{1,0:T(8,128)(2,1)} %constant.28.clone.spread_ref) | copy-start | bytes 196612
  20.5 18.3 %copy-start.2 = (s32[8192]{0:T(1024)S(1)}, s32[8192]{0:T(1024)}, u32[]{:S(2)}) copy-start(s32[8192]{0:T(1024)} %param.11) | copy-start | bytes 98308
  20.5 4.9 %collective-permute-start.5 = (bf16[448,128]{1,0:T(8,128)(2,1)S(1)}, bf16[448,128]{1,0:T(8,128)(2,1)S(1)}, u32[]{:S(2)}, u32[]{:S(2)}) collective-permute-start(bf16[448,128]{1,0:T(8,128)(2,1)S(1)} %slice.24), channel_id=1, source_target_pairs={{0,64},{1,17},{2,66},{3,19},{4,68},{5,21},{6,70},{7,23},{8,72},{9,... | collective-permute-start | bytes 344072 | tf_op jit(solution)/shard_map/ppermute | solution.py:430
  25.5 7.3 %collective-permute-start.7 = (bf16[3584,128]{1,0:T(8,128)(2,1)S(1)}, bf16[3584,128]{1,0:T(8,128)(2,1)S(1)}, u32[]{:S(2)}, u32[]{:S(2)}) collective-permute-start(bf16[3584,128]{1,0:T(8,128)(2,1)S(1)} %constant_dynamic-update-slice_fusion.held_ref), channel_id=1, source_target_pairs={{0,1},{1,0},{2,3},{3,2},{4,5},{5,4},{6,7},{7,6},{8,9},{9,8},{10,11... | collective-permute-start | bytes 2752520 | tf_op jit(solution)/shard_map/ppermute | solution.py:410
  32.8 0.9 copy-start.3
  37.2 1.6 %collective-permute-start.8 = (bf16[224,512]{1,0:T(8,128)(2,1)S(1)}, bf16[224,512]{1,0:T(8,128)(2,1)S(1)}, u32[]{:S(2)}, u32[]{:S(2)}) collective-permute-start(bf16[224,512]{1,0:T(8,128)(2,1)S(1)} %attend.1.mine_ref), channel_id=1, source_target_pairs={{0,1},{1,0},{2,3},{3,2},{4,5},{5,4},{6,7},{7,6},{8,9},{9,8},{10,11... | collective-permute-start | bytes 688136 | tf_op jit(solution)/shard_map/ppermute | solution.py:410
  49.6 8.8 %collective-permute-start.14 = (bf16[448,128]{1,0:T(8,128)(2,1)S(1)}, bf16[448,128]{1,0:T(8,128)(2,1)S(1)}, u32[]{:S(2)}, u32[]{:S(2)}) collective-permute-start(bf16[448,128]{1,0:T(8,128)(2,1)S(1)} %get-tuple-element.25), channel_id=1, source_target_pairs={{0,14},{1,15},{2,4},{3,5},{4,2},{5,3},{6,8},{7,9},{8,6},{9,7},{10,... | collective-permute-start | bytes 344072 | tf_op jit(solution)/shard_map/ppermute | solution.py:410
  55.3 4.0 %collective-permute-start.10 = (bf16[448,128]{1,0:T(8,128)(2,1)S(1)}, bf16[448,128]{1,0:T(8,128)(2,1)S(1)}, u32[]{:S(2)}, u32[]{:S(2)}) collective-permute-start(bf16[448,128]{1,0:T(8,128)(2,1)S(1)} %get-tuple-element.21), channel_id=1, source_target_pairs={{0,2},{1,3},{2,0},{3,1},{4,6},{5,7},{6,4},{7,5},{8,10},{9,11},{10,... | collective-permute-start | bytes 344072 | tf_op jit(solution)/shard_map/ppermute | solution.py:410
  58.5 6.5 %collective-permute-start.15 = (bf16[896,128]{1,0:T(8,128)(2,1)S(1)}, bf16[896,128]{1,0:T(8,128)(2,1)S(1)}, u32[]{:S(2)}, u32[]{:S(2)}) collective-permute-start(bf16[896,128]{1,0:T(8,128)(2,1)S(1)} %fusion.1), channel_id=1, source_target_pairs={{0,2},{1,3},{2,0},{3,1},{4,6},{5,7},{6,4},{7,5},{8,10},{9,11},{10,... | collective-permute-start | bytes 688136 | tf_op jit(solution)/shard_map/ppermute | solution.py:410
  59.4 7.8 %collective-permute-start.11 = (bf16[896,128]{1,0:T(8,128)(2,1)S(1)}, bf16[896,128]{1,0:T(8,128)(2,1)S(1)}, u32[]{:S(2)}, u32[]{:S(2)}) collective-permute-start(bf16[896,128]{1,0:T(8,128)(2,1)S(1)} %fusion), channel_id=1, source_target_pairs={{0,14},{1,15},{2,4},{3,5},{4,2},{5,3},{6,8},{7,9},{8,6},{9,7},{10,... | collective-permute-start | bytes 688136 | tf_op jit(solution)/shard_map/ppermute | solution.py:410
  65.1 6.7 %collective-permute-start.16 = (bf16[896,128]{1,0:T(8,128)(2,1)S(1)}, bf16[896,128]{1,0:T(8,128)(2,1)S(1)}, u32[]{:S(2)}, u32[]{:S(2)}) collective-permute-start(bf16[896,128]{1,0:T(8,128)(2,1)S(1)} %add_convert_fusion.1), channel_id=1, source_target_pairs={{0,14},{1,15},{2,4},{3,5},{4,2},{5,3},{6,8},{7,9},{8,6},{9,7},{10,... | collective-permute-start | bytes 688136 | tf_op jit(solution)/shard_map/ppermute | solution.py:410
  67.3 5.3 %collective-permute-start.12 = (bf16[896,128]{1,0:T(8,128)(2,1)S(1)}, bf16[896,128]{1,0:T(8,128)(2,1)S(1)}, u32[]{:S(2)}, u32[]{:S(2)}) collective-permute-start(bf16[896,128]{1,0:T(8,128)(2,1)S(1)} %add_convert_fusion.3), channel_id=1, source_target_pairs={{0,2},{1,3},{2,0},{3,1},{4,6},{5,7},{6,4},{7,5},{8,10},{9,11},{10,... | collective-permute-start | bytes 688136 | tf_op jit(solution)/shard_map/ppermute | solution.py:410
  71.8 6.3 %collective-permute-start.17 = (bf16[896,128]{1,0:T(8,128)(2,1)S(1)}, bf16[896,128]{1,0:T(8,128)(2,1)S(1)}, u32[]{:S(2)}, u32[]{:S(2)}) collective-permute-start(bf16[896,128]{1,0:T(8,128)(2,1)S(1)} %add_convert_fusion), channel_id=1, source_target_pairs={{0,2},{1,3},{2,0},{3,1},{4,6},{5,7},{6,4},{7,5},{8,10},{9,11},{10,... | collective-permute-start | bytes 688136 | tf_op jit(solution)/shard_map/ppermute | solution.py:410
  72.6 6.2 %collective-permute-start.13 = (bf16[896,128]{1,0:T(8,128)(2,1)S(1)}, bf16[896,128]{1,0:T(8,128)(2,1)S(1)}, u32[]{:S(2)}, u32[]{:S(2)}) collective-permute-start(bf16[896,128]{1,0:T(8,128)(2,1)S(1)} %add_convert_fusion.2), channel_id=1, source_target_pairs={{0,14},{1,15},{2,4},{3,5},{4,2},{5,3},{6,8},{7,9},{8,6},{9,7},{10,... | collective-permute-start | bytes 688136 | tf_op jit(solution)/shard_map/ppermute | solution.py:410
  79.1 6.8 %collective-permute-start.22 = (bf16[928,128]{1,0:T(8,128)(2,1)S(1)}, bf16[928,128]{1,0:T(8,128)(2,1)S(1)}, u32[]{:S(2)}, u32[]{:S(2)}) collective-permute-start(bf16[928,128]{1,0:T(8,128)(2,1)S(1)} %pack.1.refs_0_), channel_id=1, source_target_pairs={{0,14},{1,15},{2,4},{3,5},{4,2},{5,3},{6,8},{7,9},{8,6},{9,7},{10,... | collective-permute-start | bytes 712712 | tf_op jit(solution)/shard_map/ppermute | solution.py:410
  80.4 5.5 %collective-permute-start.18 = (bf16[928,128]{1,0:T(8,128)(2,1)S(1)}, bf16[928,128]{1,0:T(8,128)(2,1)S(1)}, u32[]{:S(2)}, u32[]{:S(2)}) collective-permute-start(bf16[928,128]{1,0:T(8,128)(2,1)S(1)} %pack.1.refs_0_), channel_id=1, source_target_pairs={{0,2},{1,3},{2,0},{3,1},{4,6},{5,7},{6,4},{7,5},{8,10},{9,11},{10,... | collective-permute-start | bytes 712712 | tf_op jit(solution)/shard_map/ppermute | solution.py:410
  85.9 9.2 %collective-permute-start.23 = (bf16[928,128]{1,0:T(8,128)(2,1)S(1)}, bf16[928,128]{1,0:T(8,128)(2,1)S(1)}, u32[]{:S(2)}, u32[]{:S(2)}) collective-permute-start(bf16[928,128]{1,0:T(8,128)(2,1)S(1)} %collective-permute-done.22.refs_1_), channel_id=1, source_target_pairs={{0,2},{1,3},{2,0},{3,1},{4,6},{5,7},{6,4},{7,5},{8,10},{9,11},{10,... | collective-permute-start | bytes 712712 | tf_op jit(solution)/shard_map/ppermute | solution.py:410
  85.9 11.4 %collective-permute-start.19 = (bf16[928,128]{1,0:T(8,128)(2,1)S(1)}, bf16[928,128]{1,0:T(8,128)(2,1)S(1)}, u32[]{:S(2)}, u32[]{:S(2)}) collective-permute-start(bf16[928,128]{1,0:T(8,128)(2,1)S(1)} %collective-permute-done.18.refs_2_), channel_id=1, source_target_pairs={{0,14},{1,15},{2,4},{3,5},{4,2},{5,3},{6,8},{7,9},{8,6},{9,7},{10,... | collective-permute-start | bytes 712712 | tf_op jit(solution)/shard_map/ppermute | solution.py:410
  86.8 17.3 %collective-permute-start.32 = (bf16[928,128]{1,0:T(8,128)(2,1)S(1)}, bf16[928,128]{1,0:T(8,128)(2,1)S(1)}, u32[]{:S(2)}, u32[]{:S(2)}) collective-permute-start(bf16[928,128]{1,0:T(8,128)(2,1)S(1)} %pack.1.refs_0_), channel_id=1, source_target_pairs={{0,1},{1,0},{2,3},{3,2},{4,5},{5,4},{6,7},{7,6},{8,9},{9,8},{10,11... | collective-permute-start | bytes 712712 | tf_op jit(solution)/shard_map/ppermute | solution.py:410
  95.1 9.1 %collective-permute-start.33 = (bf16[928,128]{1,0:T(8,128)(2,1)S(1)}, bf16[928,128]{1,0:T(8,128)(2,1)S(1)}, u32[]{:S(2)}, u32[]{:S(2)}) collective-permute-start(bf16[928,128]{1,0:T(8,128)(2,1)S(1)} %collective-permute-done.22.refs_1_), channel_id=1, source_target_pairs={{0,1},{1,0},{2,3},{3,2},{4,5},{5,4},{6,7},{7,6},{8,9},{9,8},{10,11... | collective-permute-start | bytes 712712 | tf_op jit(solution)/shard_map/ppermute | solution.py:410
  95.1 9.6 %collective-permute-start.24 = (bf16[928,128]{1,0:T(8,128)(2,1)S(1)}, bf16[928,128]{1,0:T(8,128)(2,1)S(1)}, u32[]{:S(2)}, u32[]{:S(2)}) collective-permute-start(bf16[928,128]{1,0:T(8,128)(2,1)S(1)} %collective-permute-done.23.refs_1_), channel_id=1, source_target_pairs={{0,14},{1,15},{2,4},{3,5},{4,2},{5,3},{6,8},{7,9},{8,6},{9,7},{10,... | collective-permute-start | bytes 712712 | tf_op jit(solution)/shard_map/ppermute | solution.py:410
  97.2 10.5 %collective-permute-start.20 = (bf16[928,128]{1,0:T(8,128)(2,1)S(1)}, bf16[928,128]{1,0:T(8,128)(2,1)S(1)}, u32[]{:S(2)}, u32[]{:S(2)}) collective-permute-start(bf16[928,128]{1,0:T(8,128)(2,1)S(1)} %collective-permute-done.19.refs_0_), channel_id=1, source_target_pairs={{0,2},{1,3},{2,0},{3,1},{4,6},{5,7},{6,4},{7,5},{8,10},{9,11},{10,... | collective-permute-start | bytes 712712 | tf_op jit(solution)/shard_map/ppermute | solution.py:410
  98.0 12.0 %collective-permute-start.34 = (bf16[928,128]{1,0:T(8,128)(2,1)S(1)}, bf16[928,128]{1,0:T(8,128)(2,1)S(1)}, u32[]{:S(2)}, u32[]{:S(2)}) collective-permute-start(bf16[928,128]{1,0:T(8,128)(2,1)S(1)} %collective-permute-done.18.refs_2_), channel_id=1, source_target_pairs={{0,1},{1,0},{2,3},{3,2},{4,5},{5,4},{6,7},{7,6},{8,9},{9,8},{10,11... | collective-permute-start | bytes 712712 | tf_op jit(solution)/shard_map/ppermute | solution.py:410
  104.1 6.0 %collective-permute-start.31 = (bf16[928,128]{1,0:T(8,128)(2,1)S(1)}, bf16[928,128]{1,0:T(8,128)(2,1)S(1)}, u32[]{:S(2)}, u32[]{:S(2)}) collective-permute-start(bf16[928,128]{1,0:T(8,128)(2,1)S(1)} %collective-permute-done.23.refs_1_), channel_id=1, source_target_pairs={{0,1},{1,0},{2,3},{3,2},{4,5},{5,4},{6,7},{7,6},{8,9},{9,8},{10,11... | collective-permute-start | bytes 712712 | tf_op jit(solution)/shard_map/ppermute | solution.py:410
  104.1 14.9 %collective-permute-start.30 = (bf16[928,128]{1,0:T(8,128)(2,1)S(1)}, bf16[928,128]{1,0:T(8,128)(2,1)S(1)}, u32[]{:S(2)}, u32[]{:S(2)}) collective-permute-start(bf16[928,128]{1,0:T(8,128)(2,1)S(1)} %collective-permute-done.19.refs_0_), channel_id=1, source_target_pairs={{0,1},{1,0},{2,3},{3,2},{4,5},{5,4},{6,7},{7,6},{8,9},{9,8},{10,11... | collective-permute-start | bytes 712712 | tf_op jit(solution)/shard_map/ppermute | solution.py:410
  104.6 16.1 %collective-permute-start.28 = (bf16[928,128]{1,0:T(8,128)(2,1)S(1)}, bf16[928,128]{1,0:T(8,128)(2,1)S(1)}, u32[]{:S(2)}, u32[]{:S(2)}) collective-permute-start(bf16[928,128]{1,0:T(8,128)(2,1)S(1)} %collective-permute-done.24.refs_0_), channel_id=1, source_target_pairs={{0,1},{1,0},{2,3},{3,2},{4,5},{5,4},{6,7},{7,6},{8,9},{9,8},{10,11... | collective-permute-start | bytes 712712 | tf_op jit(solution)/shard_map/ppermute | solution.py:410
  107.7 13.0 %collective-permute-start.29 = (bf16[928,128]{1,0:T(8,128)(2,1)S(1)}, bf16[928,128]{1,0:T(8,128)(2,1)S(1)}, u32[]{:S(2)}, u32[]{:S(2)}) collective-permute-start(bf16[928,128]{1,0:T(8,128)(2,1)S(1)} %collective-permute-done.20.refs_1_), channel_id=1, source_target_pairs={{0,1},{1,0},{2,3},{3,2},{4,5},{5,4},{6,7},{7,6},{8,9},{9,8},{10,11... | collective-permute-start | bytes 712712 | tf_op jit(solution)/shard_map/ppermute | solution.py:410
  109.9 4.9 %collective-permute-start.25 = (bf16[464,128]{1,0:T(8,128)(2,1)S(1)}, bf16[464,128]{1,0:T(8,128)(2,1)S(1)}, u32[]{:S(2)}, u32[]{:S(2)}) collective-permute-start(bf16[464,128]{1,0:T(8,128)(2,1)S(1)} %slice.27), channel_id=1, source_target_pairs={{0,2},{1,3},{2,0},{3,1},{4,6},{5,7},{6,4},{7,5},{8,10},{9,11},{10,... | collective-permute-start | bytes 356360 | tf_op jit(solution)/shard_map/ppermute | solution.py:410
  110.1 5.8 %collective-permute-start.21 = (bf16[464,128]{1,0:T(8,128)(2,1)S(1)}, bf16[464,128]{1,0:T(8,128)(2,1)S(1)}, u32[]{:S(2)}, u32[]{:S(2)}) collective-permute-start(bf16[464,128]{1,0:T(8,128)(2,1)S(1)} %slice.26), channel_id=1, source_target_pairs={{0,14},{1,15},{2,4},{3,5},{4,2},{5,3},{6,8},{7,9},{8,6},{9,7},{10,... | collective-permute-start | bytes 356360 | tf_op jit(solution)/shard_map/ppermute | solution.py:410
  114.8 7.7 %collective-permute-start.27 = (bf16[464,128]{1,0:T(8,128)(2,1)S(1)}, bf16[464,128]{1,0:T(8,128)(2,1)S(1)}, u32[]{:S(2)}, u32[]{:S(2)}) collective-permute-start(bf16[464,128]{1,0:T(8,128)(2,1)S(1)} %collective-permute-done.25.refs_1_), channel_id=1, source_target_pairs={{0,1},{1,0},{2,3},{3,2},{4,5},{5,4},{6,7},{7,6},{8,9},{9,8},{10,11... | collective-permute-start | bytes 356360 | tf_op jit(solution)/shard_map/ppermute | solution.py:410
  115.9 6.6 %collective-permute-start.26 = (bf16[464,128]{1,0:T(8,128)(2,1)S(1)}, bf16[464,128]{1,0:T(8,128)(2,1)S(1)}, u32[]{:S(2)}, u32[]{:S(2)}) collective-permute-start(bf16[464,128]{1,0:T(8,128)(2,1)S(1)} %collective-permute-done.21.refs_0_), channel_id=1, source_target_pairs={{0,1},{1,0},{2,3},{3,2},{4,5},{5,4},{6,7},{7,6},{8,9},{9,8},{10,11... | collective-permute-start | bytes 356360 | tf_op jit(solution)/shard_map/ppermute | solution.py:410

commit v2 on v1

--- a/solution.py
+++ b/solution.py
@@ -46,8 +46,8 @@
     return pairs
 
 
-FIRST = torus_pairs("xy", 1), torus_pairs("xy", -1)
-SECOND = torus_pairs("yx", 1), torus_pairs("yx", -1)
+FIRST = torus_pairs("xy", 1), torus_pairs("xy", -1), torus_pairs("xy", 2)
+SECOND = torus_pairs("yx", 1), torus_pairs("yx", -1), torus_pairs("yx", 2)
 
 
 def turn_matrix():
@@ -58,12 +58,12 @@
     return np.kron(np.eye(2), 1 - 2 * (parity % 2)).astype(np.float32)
 
 
-def spread_matrix():
-    row, column = np.arange(BLOCK)[:, None], np.arange(COLS)[None, :]
-    return ((row % SUB == column // BLOCK) & (row < 2 * SUB)).astype(np.float32)
-
-
-def clipped_partial(pairs, signs, turn_ref, spread_ref):
+def gather_matrix():
+    row, column = np.arange(SHARE)[:, None], np.arange(BLOCK)[None, :]
+    return (row // BLOCK == column).astype(np.float32)
+
+
+def clipped_partial(pairs, signs, turn_ref, gather_ref):
     flat = jnp.concatenate(
         [
             (jnp.dot(rows, weight, preferred_element_type=jnp.float32) * signs).astype(jnp.bfloat16)
@@ -71,17 +71,20 @@
         ],
         0,
     )
-    squares = lax.dot_general(
-        flat * flat, spread_ref[...], (((1,), (1,)), ((), ())), preferred_element_type=jnp.float32
-    )
+    squares = jnp.dot(flat * flat, gather_ref[...], preferred_element_type=jnp.float32)
     limit = 2.0 * jnp.sqrt(squares + BLOCK * 1e-06)
-    upper = limit.astype(jnp.bfloat16).astype(jnp.float32)
-    lane = lax.broadcasted_iota(jnp.int32, limit.shape, 1)
-    limit = jnp.where(lane < SUB, upper, limit - upper).astype(jnp.bfloat16)
-    limit = jnp.dot(limit, spread_ref[...], preferred_element_type=jnp.float32)
-    turned = jnp.dot(flat, turn_ref[...], preferred_element_type=jnp.float32)
-    clipped = jnp.minimum(jnp.maximum(turned, -limit), limit)
-    return clipped[:TOKENS] + clipped[TOKENS:]
+    blocks = []
+    for pair in range(2):
+        columns = slice(pair * COLS, (pair + 1) * COLS)
+        turned = jnp.dot(flat[:, columns], turn_ref[...], preferred_element_type=jnp.float32)
+        for b in range(SUB):
+            n = pair * SUB + b
+            bound = jnp.broadcast_to(limit[:, n : n + 1], (2 * TOKENS, BLOCK))
+            clipped = jnp.minimum(
+                jnp.maximum(turned[:, b * BLOCK : (b + 1) * BLOCK], -bound), bound
+            )
+            blocks.append(clipped[:TOKENS] + clipped[TOKENS:])
+    return blocks
 
 
 GROUP = HEADS // 2 * TOKENS
@@ -119,6 +122,7 @@
 
     wide[:, HEAD:] = jnp.ones((KEYS, HEAD), jnp.bfloat16)
     fetch.wait()
+    whole = first // KEY_BLOCK
     query_pos = first + lax.rem(
         lax.broadcasted_iota(jnp.int32, (GROUP, 128), 0), TOKENS
     )
@@ -150,7 +154,8 @@
 
     low = jnp.full((GROUP, 128), -1e30, jnp.float32)
 
-    best = lax.fori_loop(0, blocks, lambda j, b: score(j, b, True), (low, low))
+    best = lax.fori_loop(0, whole, lambda j, b: score(j, b, False), (low, low))
+    best = lax.fori_loop(whole, blocks, lambda j, b: score(j, b, True), best)
     tops = [jnp.broadcast_to(jnp.max(b, axis=-1, keepdims=True), (GROUP, 128)) for b in best]
 
     def mix(j, totals):
@@ -213,7 +218,7 @@
 
 
 def project_kernel(
-    place_ref, mine_ref, theirs_ref, own_hbm, other_hbm, sign_ref, turn_ref, spread_ref, *refs
+    place_ref, mine_ref, theirs_ref, own_hbm, other_hbm, sign_ref, turn_ref, gather_ref, *refs
 ):
     o_refs, (own, other, sems) = refs[: CHIPS + 1], refs[CHIPS + 1 :]
     core, chip, way = place_ref[1], place_ref[2], place_ref[5]
@@ -242,18 +247,10 @@
         for fetch in fetches(step):
             fetch.wait()
         start = pl.multiple_of(column(step), SHARE)
-        totals = []
-        for half in range(2):
-            columns = slice(half * COLS, (half + 1) * COLS)
-            signs = (2 * sign_ref[:, pl.ds(start + half * COLS, COLS)] - 1).astype(jnp.float32)
-            totals.append(
-                clipped_partial(
-                    ((mine_ref[...], own[step, :, columns]), (theirs_ref[...], other[step, :, columns])),
-                    signs,
-                    turn_ref,
-                    spread_ref,
-                )
-            )
+        signs = (2 * sign_ref[:, pl.ds(start, SHARE)] - 1).astype(jnp.float32)
+        blocks = clipped_partial(
+            ((mine_ref[...], own[step]), (theirs_ref[...], other[step])), signs, turn_ref, gather_ref
+        )
         for n in range(CHIPS):
 
             @pl.when(step == n)
@@ -261,11 +258,11 @@
                 for half in range(2):
                     o_ref, row = (o_refs[half], 0) if n == 0 else (o_refs[n + 1], half * ROWS)
                     for b in range(SUB):
-                        piece = totals[half][:, b * BLOCK : (b + 1) * BLOCK]
+                        piece = blocks[half * SUB + b]
                         o_ref[row + b * TOKENS : row + (b + 1) * TOKENS, :] = piece.astype(o_ref.dtype)
 
 
-def project(place, mine, theirs, own, other, signs, turn, spread):
+def project(place, mine, theirs, own, other, signs, turn, gatherer):
     half = jax.ShapeDtypeStruct((ROWS, BLOCK), jnp.bfloat16)
     both = jax.ShapeDtypeStruct((2 * ROWS, BLOCK), jnp.bfloat16)
     full = jax.ShapeDtypeStruct((2 * ROWS, BLOCK), jnp.float32)
@@ -284,7 +281,7 @@
             flops=2 * TOKENS * 1280 * D // 2, bytes_accessed=10 << 20, transcendentals=0
         ),
         name="project",
-    )(place, mine, theirs, own, other, signs, turn, spread)
+    )(place, mine, theirs, own, other, signs, turn, gatherer)
 
 
 def pack_kernel(own, one, two, out, square):
@@ -421,16 +418,8 @@
     other_weight = send(out_weight, PAIR)
 
     def spread_out(x, pairs):
-        up, down = (lax.ppermute(x, ("ctx", "tp"), way) for way in pairs)
-        count = x.shape[0] // 2
-        if count < TOKENS:
-            far = (lax.ppermute(up, ("ctx", "tp"), pairs[0]),)
-        else:
-            far = (
-                lax.ppermute(up[:count], ("ctx", "tp"), pairs[0]),
-                lax.ppermute(down[count:], ("ctx", "tp"), pairs[1]),
-            )
-        return jnp.concatenate([x, up, down, *far], 0)
+        came = [lax.ppermute(x, ("ctx", "tp"), way) for way in pairs]
+        return jnp.concatenate([x, *came], 0)
 
     key_part = lax.dynamic_slice_in_dim(keys, chip * HEAD, HEAD, 1)
     value_part = lax.dynamic_slice_in_dim(values, chip * HEAD, HEAD, 1)
@@ -439,7 +428,7 @@
     swapped = send(held, PAIR)
 
     turn = jnp.asarray(turn_matrix(), jnp.bfloat16)
-    spread = jnp.asarray(spread_matrix(), jnp.bfloat16)
+    gatherer = jnp.asarray(gather_matrix(), jnp.bfloat16)
     attended = attention(place, queries, held, swapped)
     parts = project(
         place,
@@ -449,7 +438,7 @@
         other_weight,
         signs[None, :],
         turn,
-        spread,
+        gatherer,
     )
 
     def exchange(for_a, for_b):

time: 125 us -> 119 us (0.952); the launches traced: 125 us -> 117 us
  waiting for transfers between devices: 44.8 us -> 39.1 us
    ppermute x7 -> x6, waiting for transfers between devices: 14.2 us -> 8.94 us  [spread_out(): came = [lax.ppermute(x, ('ctx', 'tp'), way) for way in pairs]]
    ppermute x28, starting transfers between devices: 48.1 us -> 46.6 us  [send(): return lax.ppermute(x, 'tp', pairs)]
    ppermute x7 -> x6, starting transfers between devices: 6.2 us -> 7.06 us  [spread_out(): came = [lax.ppermute(x, ('ctx', 'tp'), way) for way in pairs]]
  transfers between devices with their start and end apart: 35 -> 34, of which waited for: 16 -> 15; matrix products, arithmetic and copies ran while one was open for 1% -> 1% of each run, Pallas kernels for 7% -> 8%
where the time goes in v2:
time: 119 us; the launch traced here: 117 us
  starting transfers between devices  53.7 us (45%)
  waiting for transfers between devices  39.1 us (33%)
  Pallas kernels  21 us (18%)
  other arithmetic  1.36 us (1%)
  local copies, waits for them, and re-layouts  1.19 us (1%)
    ppermute x28, starting transfers between devices, send(): return lax.ppermute(x, 'tp', pairs)  46.6 us
    ppermute x28, waiting for transfers between devices, send(): return lax.ppermute(x, 'tp', pairs)  30.1 us
    pallas_call x1, Pallas kernels, project(): pl.pallas_call(project_kernel, out_shape=(half,) * 2 + (both,) * (CHIPS -...  9.73 us
    ppermute x6, waiting for transfers between devices, spread_out(): came = [lax.ppermute(x, ('ctx', 'tp'), way) for way in pairs]  8.94 us
    pallas_call x4, Pallas kernels, assemble(): pl.pallas_call(functools.partial(assemble_kernel, places, fresh, last), o...  7.48 us
    ppermute x6, starting transfers between devices, spread_out(): came = [lax.ppermute(x, ('ctx', 'tp'), way) for way in pairs]  7.06 us
    pallas_call x1, Pallas kernels, attention(): pl.pallas_call(attention_kernel, out_shape=jax.ShapeDtypeStruct((TOKENS,...  3.55 us
  transfers between devices with their start and end apart: 34, of which 15 were waited for; matrix products, arithmetic and copies ran while one was open for 1% of the time, Pallas kernels for 8%

profile of v2, /device:TPU:1, one launch (start us, length us, event | category | flops | bytes accessed | tf_op | source)
XLA Modules:
  0.0 117.4 jit_solution(1679128268805081311)
XLA Ops:
  0.6 3.3 %collective-permute-start.8 = (bf16[512,8192]{1,0:T(8,128)(2,1)}, bf16[512,8192]{1,0:T(8,128)(2,1)}, u32[]{:S(2)}, u32[]{:S(2)}) collective-permute-start(bf16[512,8192]{1,0:T(8,128)(2,1)} %own_hbm.1), channel_id=1, source_target_pairs={{0,1},{1,0},{2,3},{3,2},{4,5},{5,4},{6,7},{7,6},{8,9},{9,8},{10,11... | collective-permute-start | bytes 25165832 | tf_op jit(solution)/shard_map/ppermute | solution.py:407
  3.9 0.9 constant_dynamic-update-slice_fusion.6
  4.8 1.3 %collective-permute-start.2 = (bf16[224,128]{1,0:T(8,128)(2,1)S(1)}, bf16[224,128]{1,0:T(8,128)(2,1)S(1)}, u32[]{:S(2)}, u32[]{:S(2)}) collective-permute-start(bf16[224,128]{1,0:T(8,128)(2,1)S(1)} %get-tuple-element.37), channel_id=1, source_target_pairs={{0,32},{1,129},{2,34},{3,131},{4,36},{5,133},{6,38},{7,135},{8,40}... | collective-permute-start | bytes 172040 | tf_op jit(solution)/shard_map/ppermute | solution.py:421
  6.1 0.8 collective-permute-start.1
  6.9 0.7 collective-permute-start
  7.5 2.2 %collective-permute-done.2 = bf16[224,128]{1,0:T(8,128)(2,1)S(1)} collective-permute-done((bf16[224,128]{1,0:T(8,128)(2,1)S(1)}, bf16[224,128]{1,0:T(8,128)(2,1)S(1)}, u32[]{:S(2)}, u32[]{:S(2)}) %collective-permute-start.2) | collective-permute-done | bytes 57376 | tf_op jit(solution)/shard_map/ppermute | solution.py:421
  9.7 0.0 collective-permute-done.1
  9.7 1.4 %collective-permute-done = bf16[224,128]{1,0:T(8,128)(2,1)S(1)} collective-permute-done((bf16[224,128]{1,0:T(8,128)(2,1)S(1)}, bf16[224,128]{1,0:T(8,128)(2,1)S(1)}, u32[]{:S(2)}, u32[]{:S(2)}) %collective-permute-start) | collective-permute-done | bytes 57376 | tf_op jit(solution)/shard_map/ppermute | solution.py:421
  11.1 2.8 %collective-permute-start.5 = (bf16[896,128]{1,0:T(8,128)(2,1)S(1)}, bf16[896,128]{1,0:T(8,128)(2,1)S(1)}, u32[]{:S(2)}, u32[]{:S(2)}) collective-permute-start(bf16[896,128]{1,0:T(8,128)(2,1)S(1)} %pad_maximum_fusion), channel_id=1, source_target_pairs={{0,128},{1,33},{2,130},{3,35},{4,132},{5,37},{6,134},{7,39},{8,136... | collective-permute-start | bytes 688136 | tf_op jit(solution)/shard_map/ppermute | solution.py:421
  13.9 0.9 collective-permute-start.4
  14.8 0.6 collective-permute-start.3
  15.5 0.0 copy-start
  15.5 0.0 copy-start.1
  15.5 0.0 copy-start.2
  15.5 5.4 %collective-permute-done.3 = bf16[896,128]{1,0:T(8,128)(2,1)S(1)} collective-permute-done((bf16[896,128]{1,0:T(8,128)(2,1)S(1)}, bf16[896,128]{1,0:T(8,128)(2,1)S(1)}, u32[]{:S(2)}, u32[]{:S(2)}) %collective-permute-start.3) | collective-permute-done | bytes 229408 | tf_op jit(solution)/shard_map/ppermute | solution.py:421
  21.0 3.5 %collective-permute-start.6 = (bf16[3584,128]{1,0:T(8,128)(2,1)S(1)}, bf16[3584,128]{1,0:T(8,128)(2,1)S(1)}, u32[]{:S(2)}, u32[]{:S(2)}) collective-permute-start(bf16[3584,128]{1,0:T(8,128)(2,1)S(1)} %constant_dynamic-update-slice_fusion.held_ref), channel_id=1, source_target_pairs={{0,1},{1,0},{2,3},{3,2},{4,5},{5,4},{6,7},{7,6},{8,9},{9,8},{10,11... | collective-permute-start | bytes 2752520 | tf_op jit(solution)/shard_map/ppermute | solution.py:407
  24.6 0.1 stack.27.place_ref.index_ref
  24.7 2.0 %collective-permute-done.6.swapped_ref = bf16[3584,128]{1,0:T(8,128)(2,1)S(1)} collective-permute-done((bf16[3584,128]{1,0:T(8,128)(2,1)S(1)}, bf16[3584,128]{1,0:T(8,128)(2,1)S(1)}, u32[]{:S(2)}, u32[]{:S(2)}) %collective-permute-start.6) | collective-permute-done | bytes 917536 | tf_op jit(solution)/shard_map/ppermute | solution.py:407
  26.7 0.9 copy-done.3
  27.6 3.6 %attend.1.mine_ref = bf16[224,512]{1,0:T(8,128)(2,1)S(1)} custom-call(s32[6]{0:T(128)S(1)} %stack.27.place_ref.index_ref, bf16[224,512]{1,0:T(8,128)(2,1)S(1)} %copy-done.3, bf16[3584,128]{1,0:T(8,128)(2,1)S(1)} %constant_dynamic-update-slice_fusion.held_ref, bf16[3584,128]{1,0:T(8,128)(2,1)S(1)} %collective-permute-done.6.swapped_ref), custom_call_target="tpu_custom_call" | custom-call | flops 1644167168 | bytes 3145728 | tf_op jit(solution)/shard_map/attend/pallas_call | solution.py:200
  31.2 0.5 collective-permute-start.7
  31.6 1.1 collective-permute-done.7.theirs_ref
  32.8 9.7 %project.1 = (bf16[448,128]{1,0:T(8,128)(2,1)S(1)}, bf16[448,128]{1,0:T(8,128)(2,1)S(1)}, bf16[896,128]{1,0:T(8,128)(2,1)S(1)}, bf16[896,128]{1,0:T(8,128)(2,1)S...) custom-call(s32[6]{0:T(128)S(1)} %stack.27.place_ref.index_ref, ...), custom_call_target="tpu_custom_call" | custom-call | flops 2348810240 | bytes 10485760 | tf_op jit(solution)/shard_map/project/pallas_call | solution.py:269
  42.5 5.7 %collective-permute-start.13 = (bf16[448,128]{1,0:T(8,128)(2,1)S(1)}, bf16[448,128]{1,0:T(8,128)(2,1)S(1)}, u32[]{:S(2)}, u32[]{:S(2)}) collective-permute-start(bf16[448,128]{1,0:T(8,128)(2,1)S(1)} %get-tuple-element.25), channel_id=1, source_target_pairs={{0,14},{1,15},{2,4},{3,5},{4,2},{5,3},{6,8},{7,9},{8,6},{9,7},{10,... | collective-permute-start | bytes 344072 | tf_op jit(solution)/shard_map/ppermute | solution.py:407
  48.2 3.2 %collective-permute-done.13 = bf16[448,128]{1,0:T(8,128)(2,1)S(1)} collective-permute-done((bf16[448,128]{1,0:T(8,128)(2,1)S(1)}, bf16[448,128]{1,0:T(8,128)(2,1)S(1)}, u32[]{:S(2)}, u32[]{:S(2)}) %collective-permute-start.13) | collective-permute-done | bytes 114720 | tf_op jit(solution)/shard_map/ppermute | solution.py:407
  51.4 0.1 fusion.1
  51.5 0.1 collective-permute-start.14
  51.6 0.7 collective-permute-done.9
  52.3 0.1 fusion
  52.4 2.0 %collective-permute-start.10 = (bf16[896,128]{1,0:T(8,128)(2,1)S(1)}, bf16[896,128]{1,0:T(8,128)(2,1)S(1)}, u32[]{:S(2)}, u32[]{:S(2)}) collective-permute-start(bf16[896,128]{1,0:T(8,128)(2,1)S(1)} %fusion), channel_id=1, source_target_pairs={{0,14},{1,15},{2,4},{3,5},{4,2},{5,3},{6,8},{7,9},{8,6},{9,7},{10,... | collective-permute-start | bytes 688136 | tf_op jit(solution)/shard_map/ppermute | solution.py:407
  54.4 3.5 %collective-permute-done.14 = bf16[896,128]{1,0:T(8,128)(2,1)S(1)} collective-permute-done((bf16[896,128]{1,0:T(8,128)(2,1)S(1)}, bf16[896,128]{1,0:T(8,128)(2,1)S(1)}, u32[]{:S(2)}, u32[]{:S(2)}) %collective-permute-start.14) | collective-permute-done | bytes 229408 | tf_op jit(solution)/shard_map/ppermute | solution.py:407
  57.8 0.1 add_convert_fusion.1
  57.9 2.2 %collective-permute-start.15 = (bf16[896,128]{1,0:T(8,128)(2,1)S(1)}, bf16[896,128]{1,0:T(8,128)(2,1)S(1)}, u32[]{:S(2)}, u32[]{:S(2)}) collective-permute-start(bf16[896,128]{1,0:T(8,128)(2,1)S(1)} %add_convert_fusion.1), channel_id=1, source_target_pairs={{0,14},{1,15},{2,4},{3,5},{4,2},{5,3},{6,8},{7,9},{8,6},{9,7},{10,... | collective-permute-start | bytes 688136 | tf_op jit(solution)/shard_map/ppermute | solution.py:407
  60.1 0.1 add_convert_fusion.3
  60.1 0.1 collective-permute-start.11
  60.2 4.3 %collective-permute-done.15 = bf16[896,128]{1,0:T(8,128)(2,1)S(1)} collective-permute-done((bf16[896,128]{1,0:T(8,128)(2,1)S(1)}, bf16[896,128]{1,0:T(8,128)(2,1)S(1)}, u32[]{:S(2)}, u32[]{:S(2)}) %collective-permute-start.15) | collective-permute-done | bytes 229408 | tf_op jit(solution)/shard_map/ppermute | solution.py:407
  64.6 0.1 add_convert_fusion
  64.6 0.1 collective-permute-start.16
  64.7 0.7 collective-permute-done.11
  65.4 0.1 add_convert_fusion.2
  65.5 1.5 %collective-permute-start.12 = (bf16[896,128]{1,0:T(8,128)(2,1)S(1)}, bf16[896,128]{1,0:T(8,128)(2,1)S(1)}, u32[]{:S(2)}, u32[]{:S(2)}) collective-permute-start(bf16[896,128]{1,0:T(8,128)(2,1)S(1)} %add_convert_fusion.2), channel_id=1, source_target_pairs={{0,14},{1,15},{2,4},{3,5},{4,2},{5,3},{6,8},{7,9},{8,6},{9,7},{10,... | collective-permute-start | bytes 688136 | tf_op jit(solution)/shard_map/ppermute | solution.py:407
  67.0 3.8 %collective-permute-done.16.two = bf16[896,128]{1,0:T(8,128)(2,1)S(1)} collective-permute-done((bf16[896,128]{1,0:T(8,128)(2,1)S(1)}, bf16[896,128]{1,0:T(8,128)(2,1)S(1)}, u32[]{:S(2)}, u32[]{:S(2)}) %collective-permute-start.16) | collective-permute-done | bytes 229408 | tf_op jit(solution)/shard_map/ppermute | solution.py:407
  70.8 0.8 collective-permute-done.12.one
  71.6 0.3 pack.1.refs_0_
  71.9 1.5 %collective-permute-start.21 = (bf16[928,128]{1,0:T(8,128)(2,1)S(1)}, bf16[928,128]{1,0:T(8,128)(2,1)S(1)}, u32[]{:S(2)}, u32[]{:S(2)}) collective-permute-start(bf16[928,128]{1,0:T(8,128)(2,1)S(1)} %pack.1.refs_0_), channel_id=1, source_target_pairs={{0,14},{1,15},{2,4},{3,5},{4,2},{5,3},{6,8},{7,9},{8,6},{9,7},{10,... | collective-permute-start | bytes 712712 | tf_op jit(solution)/shard_map/ppermute | solution.py:407
  73.4 5.2 %collective-permute-done.21.refs_1_ = bf16[928,128]{1,0:T(8,128)(2,1)S(1)} collective-permute-done((bf16[928,128]{1,0:T(8,128)(2,1)S(1)}, bf16[928,128]{1,0:T(8,128)(2,1)S(1)}, u32[]{:S(2)}, u32[]{:S(2)}) %collective-permute-start.21) | collective-permute-done | bytes 237600 | tf_op jit(solution)/shard_map/ppermute | solution.py:407
  78.6 1.0 collective-permute-start.18
  79.6 8.5 %collective-permute-start.31 = (bf16[928,128]{1,0:T(8,128)(2,1)S(1)}, bf16[928,128]{1,0:T(8,128)(2,1)S(1)}, u32[]{:S(2)}, u32[]{:S(2)}) collective-permute-start(bf16[928,128]{1,0:T(8,128)(2,1)S(1)} %pack.1.refs_0_), channel_id=1, source_target_pairs={{0,1},{1,0},{2,3},{3,2},{4,5},{5,4},{6,7},{7,6},{8,9},{9,8},{10,11... | collective-permute-start | bytes 712712 | tf_op jit(solution)/shard_map/ppermute | solution.py:407
  88.1 1.7 %collective-permute-start.23 = (bf16[928,128]{1,0:T(8,128)(2,1)S(1)}, bf16[928,128]{1,0:T(8,128)(2,1)S(1)}, u32[]{:S(2)}, u32[]{:S(2)}) collective-permute-start(bf16[928,128]{1,0:T(8,128)(2,1)S(1)} %collective-permute-done.22.refs_1_), channel_id=1, source_target_pairs={{0,14},{1,15},{2,4},{3,5},{4,2},{5,3},{6,8},{7,9},{8,6},{9,7},{10,... | collective-permute-start | bytes 712712 | tf_op jit(solution)/shard_map/ppermute | solution.py:407
  89.8 0.9 collective-permute-start.19
  90.7 6.2 %collective-permute-start.33 = (bf16[928,128]{1,0:T(8,128)(2,1)S(1)}, bf16[928,128]{1,0:T(8,128)(2,1)S(1)}, u32[]{:S(2)}, u32[]{:S(2)}) collective-permute-start(bf16[928,128]{1,0:T(8,128)(2,1)S(1)} %collective-permute-done.17.refs_2_), channel_id=1, source_target_pairs={{0,1},{1,0},{2,3},{3,2},{4,5},{5,4},{6,7},{7,6},{8,9},{9,8},{10,11... | collective-permute-start | bytes 712712 | tf_op jit(solution)/shard_map/ppermute | solution.py:407
  96.8 0.0 collective-permute-start.30
  96.8 0.5 collective-permute-start.29
  97.4 2.9 %collective-permute-start.27 = (bf16[928,128]{1,0:T(8,128)(2,1)S(1)}, bf16[928,128]{1,0:T(8,128)(2,1)S(1)}, u32[]{:S(2)}, u32[]{:S(2)}) collective-permute-start(bf16[928,128]{1,0:T(8,128)(2,1)S(1)} %collective-permute-done.23.refs_0_), channel_id=1, source_target_pairs={{0,1},{1,0},{2,3},{3,2},{4,5},{5,4},{6,7},{7,6},{8,9},{9,8},{10,11... | collective-permute-start | bytes 712712 | tf_op jit(solution)/shard_map/ppermute | solution.py:407
  100.2 1.7 %collective-permute-start.28 = (bf16[928,128]{1,0:T(8,128)(2,1)S(1)}, bf16[928,128]{1,0:T(8,128)(2,1)S(1)}, u32[]{:S(2)}, u32[]{:S(2)}) collective-permute-start(bf16[928,128]{1,0:T(8,128)(2,1)S(1)} %collective-permute-done.19.refs_1_), channel_id=1, source_target_pairs={{0,1},{1,0},{2,3},{3,2},{4,5},{5,4},{6,7},{7,6},{8,9},{9,8},{10,11... | collective-permute-start | bytes 712712 | tf_op jit(solution)/shard_map/ppermute | solution.py:407
  102.0 0.8 collective-permute-start.24
  102.8 4.1 %collective-permute-done.24.refs_1_ = bf16[464,128]{1,0:T(8,128)(2,1)S(1)} collective-permute-done((bf16[464,128]{1,0:T(8,128)(2,1)S(1)}, bf16[464,128]{1,0:T(8,128)(2,1)S(1)}, u32[]{:S(2)}, u32[]{:S(2)}) %collective-permute-start.24) | collective-permute-done | bytes 118816 | tf_op jit(solution)/shard_map/ppermute | solution.py:407
  106.9 0.9 collective-permute-start.26
  107.7 0.8 collective-permute-done.20.refs_0_
  108.5 1.1 collective-permute-start.25
  109.7 2.0 %assemble.4 = (bf16[224,8192]{1,0:T(8,128)(2,1)}, f32[8,2,4,256]{3,2,1,0:T(4,128)S(1)}) custom-call(s32[6]{0:T(128)S(1)} %stack.27.place_ref.index_ref, bf16[928,128]{1,0:T(8,128)(2,1)S(1)} %pack.1.refs_0_, bf16[928,128]{1,0:T(8,128)(2,1)S(1)} %collective-permute-done.21.refs_1_, bf16[928,128]{1,0:T(8,128)(2,1)S(1)} %collective-permute-done.17.refs_2_, ...), custom_call_target="tpu_custom_call" | custom-call | flops 1048576 | bytes 4194304 | tf_op jit(solution)/shard_map/assemble/pallas_call | solution.py:384
  111.7 1.7 %assemble.5 = (bf16[224,8192]{1,0:T(8,128)(2,1)}, f32[8,2,4,256]{3,2,1,0:T(4,128)S(1)}) custom-call(s32[6]{0:T(128)S(1)} %stack.27.place_ref.index_ref, bf16[928,128]{1,0:T(8,128)(2,1)S(1)} %collective-permute-done.18.refs_0_, bf16[928,128]{1,0:T(8,128)(2,1)S(1)} %collective-permute-done.22.refs_1_, ...), custom_call_target="tpu_custom_call", output_to_operand_aliasing={{0}: (5, {})} | custom-call | flops 1048576 | bytes 4194304 | tf_op jit(solution)/shard_map/assemble/pallas_call | solution.py:384
  113.4 1.7 %assemble.6 = (bf16[224,8192]{1,0:T(8,128)(2,1)}, f32[8,2,4,256]{3,2,1,0:T(4,128)S(1)}) custom-call(s32[6]{0:T(128)S(1)} %stack.27.place_ref.index_ref, bf16[928,128]{1,0:T(8,128)(2,1)S(1)} %collective-permute-done.23.refs_0_, bf16[928,128]{1,0:T(8,128)(2,1)S(1)} %collective-permute-done.19.refs_1_, ...), custom_call_target="tpu_custom_call", output_to_operand_aliasing={{0}: (5, {})} | custom-call | flops 1048576 | bytes 4194304 | tf_op jit(solution)/shard_map/assemble/pallas_call | solution.py:384
  115.1 2.1 %assemble.7 = (bf16[224,8192]{1,0:T(8,128)(2,1)}, f32[64,224]{1,0:T(8,128)}) custom-call(s32[6]{0:T(128)S(1)} %stack.27.place_ref.index_ref, bf16[464,128]{1,0:T(8,128)(2,1)S(1)} %collective-permute-done.20.refs_0_, bf16[464,128]{1,0:T(8,128)(2,1)S(1)} %collective-permute-done.24.refs_1_, ...), custom_call_target="tpu_custom_call", output_to_operand_aliasing={{0}: (5, {})} | custom-call | flops 1048576 | bytes 4194304 | tf_op jit(solution)/shard_map/assemble/pallas_call | solution.py:384
  (36 shorter events, 0.2 us)
Async XLA Ops:
  0.6 32.1 %collective-permute-start.8 = (bf16[512,8192]{1,0:T(8,128)(2,1)}, bf16[512,8192]{1,0:T(8,128)(2,1)}, u32[]{:S(2)}, u32[]{:S(2)}) collective-permute-start(bf16[512,8192]{1,0:T(8,128)(2,1)} %own_hbm.1), channel_id=1, source_target_pairs={{0,1},{1,0},{2,3},{3,2},{4,5},{5,4},{6,7},{7,6},{8,9},{9,8},{10,11... | collective-permute-start | bytes 25165832 | tf_op jit(solution)/shard_map/ppermute | solution.py:407
  4.8 4.9 %collective-permute-start.2 = (bf16[224,128]{1,0:T(8,128)(2,1)S(1)}, bf16[224,128]{1,0:T(8,128)(2,1)S(1)}, u32[]{:S(2)}, u32[]{:S(2)}) collective-permute-start(bf16[224,128]{1,0:T(8,128)(2,1)S(1)} %get-tuple-element.37), channel_id=1, source_target_pairs={{0,32},{1,129},{2,34},{3,131},{4,36},{5,133},{6,38},{7,135},{8,40}... | collective-permute-start | bytes 172040 | tf_op jit(solution)/shard_map/ppermute | solution.py:421
  6.1 3.6 %collective-permute-start.1 = (bf16[224,128]{1,0:T(8,128)(2,1)S(1)}, bf16[224,128]{1,0:T(8,128)(2,1)S(1)}, u32[]{:S(2)}, u32[]{:S(2)}) collective-permute-start(bf16[224,128]{1,0:T(8,128)(2,1)S(1)} %get-tuple-element.37), channel_id=1, source_target_pairs={{0,48},{1,193},{2,50},{3,195},{4,52},{5,197},{6,54},{7,199},{8,56}... | collective-permute-start | bytes 172040 | tf_op jit(solution)/shard_map/ppermute | solution.py:421
  6.9 4.2 %collective-permute-start = (bf16[224,128]{1,0:T(8,128)(2,1)S(1)}, bf16[224,128]{1,0:T(8,128)(2,1)S(1)}, u32[]{:S(2)}, u32[]{:S(2)}) collective-permute-start(bf16[224,128]{1,0:T(8,128)(2,1)S(1)} %get-tuple-element.37), channel_id=1, source_target_pairs={{0,16},{1,65},{2,18},{3,67},{4,20},{5,69},{6,22},{7,71},{8,24},{9,... | collective-permute-start | bytes 172040 | tf_op jit(solution)/shard_map/ppermute | solution.py:421
  11.1 9.9 %collective-permute-start.5 = (bf16[896,128]{1,0:T(8,128)(2,1)S(1)}, bf16[896,128]{1,0:T(8,128)(2,1)S(1)}, u32[]{:S(2)}, u32[]{:S(2)}) collective-permute-start(bf16[896,128]{1,0:T(8,128)(2,1)S(1)} %pad_maximum_fusion), channel_id=1, source_target_pairs={{0,128},{1,33},{2,130},{3,35},{4,132},{5,37},{6,134},{7,39},{8,136... | collective-permute-start | bytes 688136 | tf_op jit(solution)/shard_map/ppermute | solution.py:421
  13.9 7.0 %collective-permute-start.4 = (bf16[896,128]{1,0:T(8,128)(2,1)S(1)}, bf16[896,128]{1,0:T(8,128)(2,1)S(1)}, u32[]{:S(2)}, u32[]{:S(2)}) collective-permute-start(bf16[896,128]{1,0:T(8,128)(2,1)S(1)} %pad_maximum_fusion), channel_id=1, source_target_pairs={{0,192},{1,49},{2,194},{3,51},{4,196},{5,53},{6,198},{7,55},{8,200... | collective-permute-start | bytes 688136 | tf_op jit(solution)/shard_map/ppermute | solution.py:421
  14.8 6.1 %collective-permute-start.3 = (bf16[896,128]{1,0:T(8,128)(2,1)S(1)}, bf16[896,128]{1,0:T(8,128)(2,1)S(1)}, u32[]{:S(2)}, u32[]{:S(2)}) collective-permute-start(bf16[896,128]{1,0:T(8,128)(2,1)S(1)} %pad_maximum_fusion), channel_id=1, source_target_pairs={{0,64},{1,17},{2,66},{3,19},{4,68},{5,21},{6,70},{7,23},{8,72},{9,... | collective-permute-start | bytes 688136 | tf_op jit(solution)/shard_map/ppermute | solution.py:421
  15.5 17.3 %copy-start = (bf16[512,128]{1,0:T(8,128)(2,1)S(1)}, bf16[512,128]{1,0:T(8,128)(2,1)}, u32[]{:S(2)}) copy-start(bf16[512,128]{1,0:T(8,128)(2,1)} %constant.28.clone.gather_ref) | copy-start | bytes 393220
  15.5 17.3 %copy-start.1 = (bf16[256,256]{1,0:T(8,128)(2,1)S(1)}, bf16[256,256]{1,0:T(8,128)(2,1)}, u32[]{:S(2)}) copy-start(bf16[256,256]{1,0:T(8,128)(2,1)} %constant.27.clone.turn_ref) | copy-start | bytes 393220
  15.5 17.3 %copy-start.2 = (s32[8192]{0:T(1024)S(1)}, s32[8192]{0:T(1024)}, u32[]{:S(2)}) copy-start(s32[8192]{0:T(1024)} %param.11) | copy-start | bytes 98308
  21.0 5.6 %collective-permute-start.6 = (bf16[3584,128]{1,0:T(8,128)(2,1)S(1)}, bf16[3584,128]{1,0:T(8,128)(2,1)S(1)}, u32[]{:S(2)}, u32[]{:S(2)}) collective-permute-start(bf16[3584,128]{1,0:T(8,128)(2,1)S(1)} %constant_dynamic-update-slice_fusion.held_ref), channel_id=1, source_target_pairs={{0,1},{1,0},{2,3},{3,2},{4,5},{5,4},{6,7},{7,6},{8,9},{9,8},{10,11... | collective-permute-start | bytes 2752520 | tf_op jit(solution)/shard_map/ppermute | solution.py:407
  26.7 0.9 copy-start.3
  31.2 1.6 %collective-permute-start.7 = (bf16[224,512]{1,0:T(8,128)(2,1)S(1)}, bf16[224,512]{1,0:T(8,128)(2,1)S(1)}, u32[]{:S(2)}, u32[]{:S(2)}) collective-permute-start(bf16[224,512]{1,0:T(8,128)(2,1)S(1)} %attend.1.mine_ref), channel_id=1, source_target_pairs={{0,1},{1,0},{2,3},{3,2},{4,5},{5,4},{6,7},{7,6},{8,9},{9,8},{10,11... | collective-permute-start | bytes 688136 | tf_op jit(solution)/shard_map/ppermute | solution.py:407
  42.5 8.9 %collective-permute-start.13 = (bf16[448,128]{1,0:T(8,128)(2,1)S(1)}, bf16[448,128]{1,0:T(8,128)(2,1)S(1)}, u32[]{:S(2)}, u32[]{:S(2)}) collective-permute-start(bf16[448,128]{1,0:T(8,128)(2,1)S(1)} %get-tuple-element.25), channel_id=1, source_target_pairs={{0,14},{1,15},{2,4},{3,5},{4,2},{5,3},{6,8},{7,9},{8,6},{9,7},{10,... | collective-permute-start | bytes 344072 | tf_op jit(solution)/shard_map/ppermute | solution.py:407
  48.2 4.1 %collective-permute-start.9 = (bf16[448,128]{1,0:T(8,128)(2,1)S(1)}, bf16[448,128]{1,0:T(8,128)(2,1)S(1)}, u32[]{:S(2)}, u32[]{:S(2)}) collective-permute-start(bf16[448,128]{1,0:T(8,128)(2,1)S(1)} %get-tuple-element.21), channel_id=1, source_target_pairs={{0,2},{1,3},{2,0},{3,1},{4,6},{5,7},{6,4},{7,5},{8,10},{9,11},{10,... | collective-permute-start | bytes 344072 | tf_op jit(solution)/shard_map/ppermute | solution.py:407
  51.5 6.3 %collective-permute-start.14 = (bf16[896,128]{1,0:T(8,128)(2,1)S(1)}, bf16[896,128]{1,0:T(8,128)(2,1)S(1)}, u32[]{:S(2)}, u32[]{:S(2)}) collective-permute-start(bf16[896,128]{1,0:T(8,128)(2,1)S(1)} %fusion.1), channel_id=1, source_target_pairs={{0,2},{1,3},{2,0},{3,1},{4,6},{5,7},{6,4},{7,5},{8,10},{9,11},{10,... | collective-permute-start | bytes 688136 | tf_op jit(solution)/shard_map/ppermute | solution.py:407
  52.4 7.7 %collective-permute-start.10 = (bf16[896,128]{1,0:T(8,128)(2,1)S(1)}, bf16[896,128]{1,0:T(8,128)(2,1)S(1)}, u32[]{:S(2)}, u32[]{:S(2)}) collective-permute-start(bf16[896,128]{1,0:T(8,128)(2,1)S(1)} %fusion), channel_id=1, source_target_pairs={{0,14},{1,15},{2,4},{3,5},{4,2},{5,3},{6,8},{7,9},{8,6},{9,7},{10,... | collective-permute-start | bytes 688136 | tf_op jit(solution)/shard_map/ppermute | solution.py:407
  57.9 6.7 %collective-permute-start.15 = (bf16[896,128]{1,0:T(8,128)(2,1)S(1)}, bf16[896,128]{1,0:T(8,128)(2,1)S(1)}, u32[]{:S(2)}, u32[]{:S(2)}) collective-permute-start(bf16[896,128]{1,0:T(8,128)(2,1)S(1)} %add_convert_fusion.1), channel_id=1, source_target_pairs={{0,14},{1,15},{2,4},{3,5},{4,2},{5,3},{6,8},{7,9},{8,6},{9,7},{10,... | collective-permute-start | bytes 688136 | tf_op jit(solution)/shard_map/ppermute | solution.py:407
  60.1 5.3 %collective-permute-start.11 = (bf16[896,128]{1,0:T(8,128)(2,1)S(1)}, bf16[896,128]{1,0:T(8,128)(2,1)S(1)}, u32[]{:S(2)}, u32[]{:S(2)}) collective-permute-start(bf16[896,128]{1,0:T(8,128)(2,1)S(1)} %add_convert_fusion.3), channel_id=1, source_target_pairs={{0,2},{1,3},{2,0},{3,1},{4,6},{5,7},{6,4},{7,5},{8,10},{9,11},{10,... | collective-permute-start | bytes 688136 | tf_op jit(solution)/shard_map/ppermute | solution.py:407
  64.6 6.2 %collective-permute-start.16 = (bf16[896,128]{1,0:T(8,128)(2,1)S(1)}, bf16[896,128]{1,0:T(8,128)(2,1)S(1)}, u32[]{:S(2)}, u32[]{:S(2)}) collective-permute-start(bf16[896,128]{1,0:T(8,128)(2,1)S(1)} %add_convert_fusion), channel_id=1, source_target_pairs={{0,2},{1,3},{2,0},{3,1},{4,6},{5,7},{6,4},{7,5},{8,10},{9,11},{10,... | collective-permute-start | bytes 688136 | tf_op jit(solution)/shard_map/ppermute | solution.py:407
  65.5 6.2 %collective-permute-start.12 = (bf16[896,128]{1,0:T(8,128)(2,1)S(1)}, bf16[896,128]{1,0:T(8,128)(2,1)S(1)}, u32[]{:S(2)}, u32[]{:S(2)}) collective-permute-start(bf16[896,128]{1,0:T(8,128)(2,1)S(1)} %add_convert_fusion.2), channel_id=1, source_target_pairs={{0,14},{1,15},{2,4},{3,5},{4,2},{5,3},{6,8},{7,9},{8,6},{9,7},{10,... | collective-permute-start | bytes 688136 | tf_op jit(solution)/shard_map/ppermute | solution.py:407
  71.9 6.7 %collective-permute-start.21 = (bf16[928,128]{1,0:T(8,128)(2,1)S(1)}, bf16[928,128]{1,0:T(8,128)(2,1)S(1)}, u32[]{:S(2)}, u32[]{:S(2)}) collective-permute-start(bf16[928,128]{1,0:T(8,128)(2,1)S(1)} %pack.1.refs_0_), channel_id=1, source_target_pairs={{0,14},{1,15},{2,4},{3,5},{4,2},{5,3},{6,8},{7,9},{8,6},{9,7},{10,... | collective-permute-start | bytes 712712 | tf_op jit(solution)/shard_map/ppermute | solution.py:407
  73.4 5.2 %collective-permute-start.17 = (bf16[928,128]{1,0:T(8,128)(2,1)S(1)}, bf16[928,128]{1,0:T(8,128)(2,1)S(1)}, u32[]{:S(2)}, u32[]{:S(2)}) collective-permute-start(bf16[928,128]{1,0:T(8,128)(2,1)S(1)} %pack.1.refs_0_), channel_id=1, source_target_pairs={{0,2},{1,3},{2,0},{3,1},{4,6},{5,7},{6,4},{7,5},{8,10},{9,11},{10,... | collective-permute-start | bytes 712712 | tf_op jit(solution)/shard_map/ppermute | solution.py:407
  78.6 9.5 %collective-permute-start.22 = (bf16[928,128]{1,0:T(8,128)(2,1)S(1)}, bf16[928,128]{1,0:T(8,128)(2,1)S(1)}, u32[]{:S(2)}, u32[]{:S(2)}) collective-permute-start(bf16[928,128]{1,0:T(8,128)(2,1)S(1)} %collective-permute-done.21.refs_1_), channel_id=1, source_target_pairs={{0,2},{1,3},{2,0},{3,1},{4,6},{5,7},{6,4},{7,5},{8,10},{9,11},{10,... | collective-permute-start | bytes 712712 | tf_op jit(solution)/shard_map/ppermute | solution.py:407
  78.6 11.2 %collective-permute-start.18 = (bf16[928,128]{1,0:T(8,128)(2,1)S(1)}, bf16[928,128]{1,0:T(8,128)(2,1)S(1)}, u32[]{:S(2)}, u32[]{:S(2)}) collective-permute-start(bf16[928,128]{1,0:T(8,128)(2,1)S(1)} %collective-permute-done.17.refs_2_), channel_id=1, source_target_pairs={{0,14},{1,15},{2,4},{3,5},{4,2},{5,3},{6,8},{7,9},{8,6},{9,7},{10,... | collective-permute-start | bytes 712712 | tf_op jit(solution)/shard_map/ppermute | solution.py:407
  79.6 17.2 %collective-permute-start.31 = (bf16[928,128]{1,0:T(8,128)(2,1)S(1)}, bf16[928,128]{1,0:T(8,128)(2,1)S(1)}, u32[]{:S(2)}, u32[]{:S(2)}) collective-permute-start(bf16[928,128]{1,0:T(8,128)(2,1)S(1)} %pack.1.refs_0_), channel_id=1, source_target_pairs={{0,1},{1,0},{2,3},{3,2},{4,5},{5,4},{6,7},{7,6},{8,9},{9,8},{10,11... | collective-permute-start | bytes 712712 | tf_op jit(solution)/shard_map/ppermute | solution.py:407
  88.1 8.8 %collective-permute-start.32 = (bf16[928,128]{1,0:T(8,128)(2,1)S(1)}, bf16[928,128]{1,0:T(8,128)(2,1)S(1)}, u32[]{:S(2)}, u32[]{:S(2)}) collective-permute-start(bf16[928,128]{1,0:T(8,128)(2,1)S(1)} %collective-permute-done.21.refs_1_), channel_id=1, source_target_pairs={{0,1},{1,0},{2,3},{3,2},{4,5},{5,4},{6,7},{7,6},{8,9},{9,8},{10,11... | collective-permute-start | bytes 712712 | tf_op jit(solution)/shard_map/ppermute | solution.py:407
  88.1 9.3 %collective-permute-start.23 = (bf16[928,128]{1,0:T(8,128)(2,1)S(1)}, bf16[928,128]{1,0:T(8,128)(2,1)S(1)}, u32[]{:S(2)}, u32[]{:S(2)}) collective-permute-start(bf16[928,128]{1,0:T(8,128)(2,1)S(1)} %collective-permute-done.22.refs_1_), channel_id=1, source_target_pairs={{0,14},{1,15},{2,4},{3,5},{4,2},{5,3},{6,8},{7,9},{8,6},{9,7},{10,... | collective-permute-start | bytes 712712 | tf_op jit(solution)/shard_map/ppermute | solution.py:407
  89.8 10.5 %collective-permute-start.19 = (bf16[928,128]{1,0:T(8,128)(2,1)S(1)}, bf16[928,128]{1,0:T(8,128)(2,1)S(1)}, u32[]{:S(2)}, u32[]{:S(2)}) collective-permute-start(bf16[928,128]{1,0:T(8,128)(2,1)S(1)} %collective-permute-done.18.refs_0_), channel_id=1, source_target_pairs={{0,2},{1,3},{2,0},{3,1},{4,6},{5,7},{6,4},{7,5},{8,10},{9,11},{10,... | collective-permute-start | bytes 712712 | tf_op jit(solution)/shard_map/ppermute | solution.py:407
  90.7 11.3 %collective-permute-start.33 = (bf16[928,128]{1,0:T(8,128)(2,1)S(1)}, bf16[928,128]{1,0:T(8,128)(2,1)S(1)}, u32[]{:S(2)}, u32[]{:S(2)}) collective-permute-start(bf16[928,128]{1,0:T(8,128)(2,1)S(1)} %collective-permute-done.17.refs_2_), channel_id=1, source_target_pairs={{0,1},{1,0},{2,3},{3,2},{4,5},{5,4},{6,7},{7,6},{8,9},{9,8},{10,11... | collective-permute-start | bytes 712712 | tf_op jit(solution)/shard_map/ppermute | solution.py:407
  96.8 6.0 %collective-permute-start.30 = (bf16[928,128]{1,0:T(8,128)(2,1)S(1)}, bf16[928,128]{1,0:T(8,128)(2,1)S(1)}, u32[]{:S(2)}, u32[]{:S(2)}) collective-permute-start(bf16[928,128]{1,0:T(8,128)(2,1)S(1)} %collective-permute-done.22.refs_1_), channel_id=1, source_target_pairs={{0,1},{1,0},{2,3},{3,2},{4,5},{5,4},{6,7},{7,6},{8,9},{9,8},{10,11... | collective-permute-start | bytes 712712 | tf_op jit(solution)/shard_map/ppermute | solution.py:407
  96.8 14.8 %collective-permute-start.29 = (bf16[928,128]{1,0:T(8,128)(2,1)S(1)}, bf16[928,128]{1,0:T(8,128)(2,1)S(1)}, u32[]{:S(2)}, u32[]{:S(2)}) collective-permute-start(bf16[928,128]{1,0:T(8,128)(2,1)S(1)} %collective-permute-done.18.refs_0_), channel_id=1, source_target_pairs={{0,1},{1,0},{2,3},{3,2},{4,5},{5,4},{6,7},{7,6},{8,9},{9,8},{10,11... | collective-permute-start | bytes 712712 | tf_op jit(solution)/shard_map/ppermute | solution.py:407
  97.4 16.0 %collective-permute-start.27 = (bf16[928,128]{1,0:T(8,128)(2,1)S(1)}, bf16[928,128]{1,0:T(8,128)(2,1)S(1)}, u32[]{:S(2)}, u32[]{:S(2)}) collective-permute-start(bf16[928,128]{1,0:T(8,128)(2,1)S(1)} %collective-permute-done.23.refs_0_), channel_id=1, source_target_pairs={{0,1},{1,0},{2,3},{3,2},{4,5},{5,4},{6,7},{7,6},{8,9},{9,8},{10,11... | collective-permute-start | bytes 712712 | tf_op jit(solution)/shard_map/ppermute | solution.py:407
  100.2 13.1 %collective-permute-start.28 = (bf16[928,128]{1,0:T(8,128)(2,1)S(1)}, bf16[928,128]{1,0:T(8,128)(2,1)S(1)}, u32[]{:S(2)}, u32[]{:S(2)}) collective-permute-start(bf16[928,128]{1,0:T(8,128)(2,1)S(1)} %collective-permute-done.19.refs_1_), channel_id=1, source_target_pairs={{0,1},{1,0},{2,3},{3,2},{4,5},{5,4},{6,7},{7,6},{8,9},{9,8},{10,11... | collective-permute-start | bytes 712712 | tf_op jit(solution)/shard_map/ppermute | solution.py:407
  102.0 4.9 %collective-permute-start.24 = (bf16[464,128]{1,0:T(8,128)(2,1)S(1)}, bf16[464,128]{1,0:T(8,128)(2,1)S(1)}, u32[]{:S(2)}, u32[]{:S(2)}) collective-permute-start(bf16[464,128]{1,0:T(8,128)(2,1)S(1)} %slice.17), channel_id=1, source_target_pairs={{0,2},{1,3},{2,0},{3,1},{4,6},{5,7},{6,4},{7,5},{8,10},{9,11},{10,... | collective-permute-start | bytes 356360 | tf_op jit(solution)/shard_map/ppermute | solution.py:407
  102.8 5.7 %collective-permute-start.20 = (bf16[464,128]{1,0:T(8,128)(2,1)S(1)}, bf16[464,128]{1,0:T(8,128)(2,1)S(1)}, u32[]{:S(2)}, u32[]{:S(2)}) collective-permute-start(bf16[464,128]{1,0:T(8,128)(2,1)S(1)} %slice.16), channel_id=1, source_target_pairs={{0,14},{1,15},{2,4},{3,5},{4,2},{5,3},{6,8},{7,9},{8,6},{9,7},{10,... | collective-permute-start | bytes 356360 | tf_op jit(solution)/shard_map/ppermute | solution.py:407
  106.9 8.3 %collective-permute-start.26 = (bf16[464,128]{1,0:T(8,128)(2,1)S(1)}, bf16[464,128]{1,0:T(8,128)(2,1)S(1)}, u32[]{:S(2)}, u32[]{:S(2)}) collective-permute-start(bf16[464,128]{1,0:T(8,128)(2,1)S(1)} %collective-permute-done.24.refs_1_), channel_id=1, source_target_pairs={{0,1},{1,0},{2,3},{3,2},{4,5},{5,4},{6,7},{7,6},{8,9},{9,8},{10,11... | collective-permute-start | bytes 356360 | tf_op jit(solution)/shard_map/ppermute | solution.py:407
  108.5 6.6 %collective-permute-start.25 = (bf16[464,128]{1,0:T(8,128)(2,1)S(1)}, bf16[464,128]{1,0:T(8,128)(2,1)S(1)}, u32[]{:S(2)}, u32[]{:S(2)}) collective-permute-start(bf16[464,128]{1,0:T(8,128)(2,1)S(1)} %collective-permute-done.20.refs_0_), channel_id=1, source_target_pairs={{0,1},{1,0},{2,3},{3,2},{4,5},{5,4},{6,7},{7,6},{8,9},{9,8},{10,11... | collective-permute-start | bytes 356360 | tf_op jit(solution)/shard_map/ppermute | solution.py:407

commit v3 on v2

--- a/solution.py
+++ b/solution.py
@@ -220,7 +220,7 @@
 def project_kernel(
     place_ref, mine_ref, theirs_ref, own_hbm, other_hbm, sign_ref, turn_ref, gather_ref, *refs
 ):
-    o_refs, (own, other, sems) = refs[: CHIPS + 1], refs[CHIPS + 1 :]
+    o_refs, (own, other, sems) = refs[: 2 * CHIPS - 1], refs[2 * CHIPS - 1 :]
     core, chip, way = place_ref[1], place_ref[2], place_ref[5]
 
     def column(step):
@@ -256,7 +256,7 @@
             @pl.when(step == n)
             def _(n=n):
                 for half in range(2):
-                    o_ref, row = (o_refs[half], 0) if n == 0 else (o_refs[n + 1], half * ROWS)
+                    o_ref, row = (o_refs[2 * n + half], 0) if n < CHIPS - 1 else (o_refs[2 * n], half * ROWS)
                     for b in range(SUB):
                         piece = blocks[half * SUB + b]
                         o_ref[row + b * TOKENS : row + (b + 1) * TOKENS, :] = piece.astype(o_ref.dtype)
@@ -264,13 +264,12 @@
 
 def project(place, mine, theirs, own, other, signs, turn, gatherer):
     half = jax.ShapeDtypeStruct((ROWS, BLOCK), jnp.bfloat16)
-    both = jax.ShapeDtypeStruct((2 * ROWS, BLOCK), jnp.bfloat16)
     full = jax.ShapeDtypeStruct((2 * ROWS, BLOCK), jnp.float32)
     return pl.pallas_call(
         project_kernel,
-        out_shape=(half,) * 2 + (both,) * (CHIPS - 2) + (full,),
+        out_shape=(half,) * (2 * CHIPS - 2) + (full,),
         in_specs=[SMEM, VMEM, VMEM, HBM, HBM, VMEM, VMEM, VMEM],
-        out_specs=(VMEM,) * (CHIPS + 1),
+        out_specs=(VMEM,) * (2 * CHIPS - 1),
         scratch_shapes=[
             pltpu.VMEM((CHIPS, WIDTH, SHARE), jnp.bfloat16),
             pltpu.VMEM((CHIPS, WIDTH, SHARE), jnp.bfloat16),
@@ -284,17 +283,16 @@
     )(place, mine, theirs, own, other, signs, turn, gatherer)
 
 
-def pack_kernel(own, one, two, out, square):
-    for half in range(2):
+def pack_kernel(own, one0, two0, one1, two1, out0, out1, square):
+    for half, (one, two, out) in enumerate(((one0, two0, out0), (one1, two1, out1))):
         lane = lax.broadcasted_iota(jnp.int32, (TOKENS, BLOCK), 1)
         columns = jnp.zeros((TOKENS, BLOCK), jnp.float32)
         for b in range(SUB):
-            rows = slice(half * ROWS + b * TOKENS, half * ROWS + (b + 1) * TOKENS)
+            rows = slice(b * TOKENS, (b + 1) * TOKENS)
             came = one[rows, :].astype(jnp.float32) + two[rows, :].astype(jnp.float32)
-            summed = (own[rows, :] + came) * (1.0 / math.sqrt(BLOCK))
+            summed = (own[half * ROWS + b * TOKENS : half * ROWS + (b + 1) * TOKENS, :] + came) * (1.0 / math.sqrt(BLOCK))
             scale = jnp.max(jnp.abs(summed), axis=-1, keepdims=True) + 1e-06
-            to = half * MSG + b * TOKENS
-            out[to : to + TOKENS, :] = (summed / scale).astype(jnp.bfloat16)
+            out[rows, :] = (summed / scale).astype(jnp.bfloat16)
             columns = jnp.where(lane == b, scale, columns)
         square[...] = jnp.zeros((2 * BLOCK, BLOCK), jnp.float32)
         square[:TOKENS, :] = columns
@@ -303,20 +301,21 @@
         )
         upper = turned.astype(jnp.bfloat16).astype(jnp.float32)
         tail = jnp.concatenate([upper, turned - upper, jnp.zeros((8, BLOCK), jnp.float32)], 0)
-        out[half * MSG + ROWS : (half + 1) * MSG, :] = tail.astype(jnp.bfloat16)
-
-
-def pack(own, one, two):
+        out[ROWS:, :] = tail.astype(jnp.bfloat16)
+
+
+def pack(own, first, second):
+    shape = jax.ShapeDtypeStruct((MSG, BLOCK), jnp.bfloat16)
     return pl.pallas_call(
         pack_kernel,
-        out_shape=jax.ShapeDtypeStruct((2 * MSG, BLOCK), jnp.bfloat16),
-        in_specs=[VMEM] * 3,
-        out_specs=VMEM,
+        out_shape=(shape, shape),
+        in_specs=[VMEM] * 5,
+        out_specs=(VMEM, VMEM),
         scratch_shapes=[pltpu.VMEM((2 * BLOCK, BLOCK), jnp.float32)],
         compiler_params=pltpu.CompilerParams(vmem_limit_bytes=8 << 20),
         cost_estimate=pl.CostEstimate(flops=1 << 20, bytes_accessed=1 << 20, transcendentals=0),
         name="pack",
-    )(own, one, two)
+    )(own, *first, *second)
 
 
 def assemble_kernel(places, fresh, last, index_ref, *refs):
@@ -446,43 +445,51 @@
         came_a = send(for_b, WAY_B)
         return came_a, came_b
 
-    came_a, came_b = exchange(parts[0], parts[1])
-    for_a, for_b = parts[2], parts[3]
-    for_a = lax.dynamic_update_slice(for_a, add(came_a, for_a[ROWS:]), (ROWS, 0))
-    for_b = lax.dynamic_update_slice(for_b, add(came_b, for_b[:ROWS]), (0, 0))
-    came_a, came_b = exchange(for_a, for_b)
-    came_a, came_b = exchange(add(came_a, parts[4]), add(came_b, parts[5]))
-    came_a, came_b = exchange(add(came_a, parts[6]), add(came_b, parts[7]))
-    packed = pack(parts[8], came_a, came_b)
-
-    stages = [[(packed, 0, None)]]
-    came_a = came_b = packed
-    for hop in range(1, 5):
-        if hop < 4:
-            came_a, came_b = exchange(came_a, came_b)
-            stages.append([(came_a, -hop, None), (came_b, hop, None)])
-        else:
-            came_a, came_b = exchange(came_a[:MSG], came_b[MSG:])
-            stages.append([(came_a, hop, 1), (came_b, hop, 0)])
-    swapped_stages = []
-    for stage in stages:
-        swapped_stages.append([(send(array, PAIR), *rest) for array, *rest in stage])
-
-    def gather(hops, before, last=False):
+    def part(distance, way, half):
+        return parts[half if distance == 4 else 2 + 4 * (3 - distance) + 2 * way + half]
+
+    came = {}
+    for step, (distance, half) in enumerate(((4, 0), (3, 0), (3, 1), (2, 1), (2, 0), (1, 0), (1, 1))):
+        for_a, for_b = part(distance, 0, half), part(distance, 1, 1 - half)
+        if step >= 2:
+            came_a, came_b = lax.optimization_barrier(came[step - 2])
+            for_a, for_b = add(came_a, for_a), add(came_b, for_b)
+        came[step] = exchange(for_a, for_b)
+    packed = pack(parts[14], (came[6][0], came[5][1]), (came[5][0], came[6][1]))
+
+    steps, place_of = [], []
+    sends = [((packed[0], 0), (packed[1], 1)), ((packed[1], 1), (packed[0], 0))]
+    for step in range(7):
+        (for_a, half_a), (for_b, half_b) = sends[step]
+        for_a, for_b = lax.optimization_barrier((for_a, for_b))
+        came_a, came_b = exchange(for_a, for_b)
+        sends.append(((came_a, half_b), (came_b, half_a)))
+        hop = step // 2 + 1
+        steps.append((came_a, came_b))
+        place_of.append(((-hop, half_b), (hop, half_a)))
+    steps.insert(0, tuple(packed))
+    place_of.insert(0, ((0, 0), (0, 1)))
+    swapped = []
+    for pieces in steps:
+        joined = jnp.concatenate(pieces, 0)
+        swapped.append(send(joined, PAIR))
+
+    def gather(which, before, last=False):
         arrays, places = [], []
-        for swap, source in ((False, stages), (True, swapped_stages)):
-            for hop in hops:
-                for array, offset, half in source[hop]:
-                    for h in (0, 1) if half is None else (half,):
-                        row = h * MSG if half is None else 0
-                        places.append((len(arrays), row, swap, offset, h))
-                    arrays.append(array)
+        for step in which:
+            for piece, spot in zip(steps[step], place_of[step]):
+                places.append((len(arrays), 0, False, *spot))
+                arrays.append(piece)
+        for step in which:
+            for row, spot in zip((0, MSG), place_of[step]):
+                places.append((len(arrays), row, True, *spot))
+            arrays.append(swapped[step])
         return assemble(place, arrays, tuple(places), before, last)
 
-    result = gather((0, 1), None)
-    result = gather((2,), result)
-    result = gather((3,), result)
-    payload, scales = gather((4,), result, True)
+    result = gather((0, 1, 2), None)
+    result = gather((3, 4), result)
+    result = gather((5, 6), result)
+    payload, scales = gather((7,), result, True)
     return payload, scales.T
 
 

time: 119 us -> 117 us (0.983)
  waiting for transfers between devices: 39.1 us -> 33.7 us
  starting transfers between devices: 53.7 us -> 57 us
    ppermute x28 -> x39, waiting for transfers between devices: 30.1 us -> 24.8 us  [send(): return lax.ppermute(x, 'tp', pairs)]
    ppermute x28 -> x39, starting transfers between devices: 46.6 us -> 50 us  [send(): return lax.ppermute(x, 'tp', pairs)]
  transfers between devices with their start and end apart: 34 -> 45, of which waited for: 15 -> 23; matrix products, arithmetic and copies ran while one was open for 1% -> 1% of each run, Pallas kernels for 8% -> 8%
where the time goes in v3:
time: 117 us; the launch traced here: 115 us
  starting transfers between devices  57 us (49%)
  waiting for transfers between devices  33.7 us (29%)
  Pallas kernels  21 us (18%)
  other arithmetic  1.35 us (1%)
  local copies, waits for them, and re-layouts  1.17 us (1%)
    ppermute x39, starting transfers between devices, send(): return lax.ppermute(x, 'tp', pairs)  50 us
    ppermute x39, waiting for transfers between devices, send(): return lax.ppermute(x, 'tp', pairs)  24.8 us
    pallas_call x1, Pallas kernels, project(): pl.pallas_call(project_kernel, out_shape=(half,) * (2 * CHIPS - 2) + (ful...  9.75 us
    ppermute x6, waiting for transfers between devices, spread_out(): came = [lax.ppermute(x, ('ctx', 'tp'), way) for way in pairs]  8.94 us
    pallas_call x4, Pallas kernels, assemble(): pl.pallas_call(functools.partial(assemble_kernel, places, fresh, last), o...  7.48 us
    ppermute x6, starting transfers between devices, spread_out(): came = [lax.ppermute(x, ('ctx', 'tp'), way) for way in pairs]  7.06 us
    pallas_call x1, Pallas kernels, attention(): pl.pallas_call(attention_kernel, out_shape=jax.ShapeDtypeStruct((TOKENS,...  3.55 us
  transfers between devices with their start and end apart: 45, of which 23 were waited for; matrix products, arithmetic and copies ran while one was open for 1% of the time, Pallas kernels for 8%

profile of v3, /device:TPU:1, one launch (start us, length us, event | category | flops | bytes accessed | tf_op | source)
XLA Modules:
  0.0 115.5 jit_solution(16060830182420275977)
XLA Ops:
  0.6 3.3 %collective-permute-start.8 = (bf16[512,8192]{1,0:T(8,128)(2,1)}, bf16[512,8192]{1,0:T(8,128)(2,1)}, u32[]{:S(2)}, u32[]{:S(2)}) collective-permute-start(bf16[512,8192]{1,0:T(8,128)(2,1)} %own_hbm.1), channel_id=1, source_target_pairs={{0,1},{1,0},{2,3},{3,2},{4,5},{5,4},{6,7},{7,6},{8,9},{9,8},{10,11... | collective-permute-start | bytes 25165832 | tf_op jit(solution)/shard_map/ppermute | solution.py:406
  3.9 0.9 constant_dynamic-update-slice_fusion.6
  4.8 1.3 %collective-permute-start.2 = (bf16[224,128]{1,0:T(8,128)(2,1)S(1)}, bf16[224,128]{1,0:T(8,128)(2,1)S(1)}, u32[]{:S(2)}, u32[]{:S(2)}) collective-permute-start(bf16[224,128]{1,0:T(8,128)(2,1)S(1)} %get-tuple-element.101), channel_id=1, source_target_pairs={{0,32},{1,129},{2,34},{3,131},{4,36},{5,133},{6,38},{7,135},{8,40}... | collective-permute-start | bytes 172040 | tf_op jit(solution)/shard_map/ppermute | solution.py:420
  6.1 0.8 collective-permute-start.1
  6.9 0.7 collective-permute-start
  7.5 2.2 %collective-permute-done.2 = bf16[224,128]{1,0:T(8,128)(2,1)S(1)} collective-permute-done((bf16[224,128]{1,0:T(8,128)(2,1)S(1)}, bf16[224,128]{1,0:T(8,128)(2,1)S(1)}, u32[]{:S(2)}, u32[]{:S(2)}) %collective-permute-start.2) | collective-permute-done | bytes 57376 | tf_op jit(solution)/shard_map/ppermute | solution.py:420
  9.7 1.4 %collective-permute-done = bf16[224,128]{1,0:T(8,128)(2,1)S(1)} collective-permute-done((bf16[224,128]{1,0:T(8,128)(2,1)S(1)}, bf16[224,128]{1,0:T(8,128)(2,1)S(1)}, u32[]{:S(2)}, u32[]{:S(2)}) %collective-permute-start) | collective-permute-done | bytes 57376 | tf_op jit(solution)/shard_map/ppermute | solution.py:420
  11.1 2.8 %collective-permute-start.5 = (bf16[896,128]{1,0:T(8,128)(2,1)S(1)}, bf16[896,128]{1,0:T(8,128)(2,1)S(1)}, u32[]{:S(2)}, u32[]{:S(2)}) collective-permute-start(bf16[896,128]{1,0:T(8,128)(2,1)S(1)} %pad_maximum_fusion.8), channel_id=1, source_target_pairs={{0,128},{1,33},{2,130},{3,35},{4,132},{5,37},{6,134},{7,39},{8,136... | collective-permute-start | bytes 688136 | tf_op jit(solution)/shard_map/ppermute | solution.py:420
  13.9 0.9 collective-permute-start.4
  14.8 0.6 collective-permute-start.3
  15.5 5.4 %collective-permute-done.3 = bf16[896,128]{1,0:T(8,128)(2,1)S(1)} collective-permute-done((bf16[896,128]{1,0:T(8,128)(2,1)S(1)}, bf16[896,128]{1,0:T(8,128)(2,1)S(1)}, u32[]{:S(2)}, u32[]{:S(2)}) %collective-permute-start.3) | collective-permute-done | bytes 229408 | tf_op jit(solution)/shard_map/ppermute | solution.py:420
  21.0 3.5 %collective-permute-start.6 = (bf16[3584,128]{1,0:T(8,128)(2,1)S(1)}, bf16[3584,128]{1,0:T(8,128)(2,1)S(1)}, u32[]{:S(2)}, u32[]{:S(2)}) collective-permute-start(bf16[3584,128]{1,0:T(8,128)(2,1)S(1)} %constant_dynamic-update-slice_fusion.held_ref), channel_id=1, source_target_pairs={{0,1},{1,0},{2,3},{3,2},{4,5},{5,4},{6,7},{7,6},{8,9},{9,8},{10,11... | collective-permute-start | bytes 2752520 | tf_op jit(solution)/shard_map/ppermute | solution.py:406
  24.7 2.0 %collective-permute-done.6.swapped_ref = bf16[3584,128]{1,0:T(8,128)(2,1)S(1)} collective-permute-done((bf16[3584,128]{1,0:T(8,128)(2,1)S(1)}, bf16[3584,128]{1,0:T(8,128)(2,1)S(1)}, u32[]{:S(2)}, u32[]{:S(2)}) %collective-permute-start.6) | collective-permute-done | bytes 917536 | tf_op jit(solution)/shard_map/ppermute | solution.py:406
  26.7 0.9 copy-done.3
  27.6 3.6 %attend.1.mine_ref = bf16[224,512]{1,0:T(8,128)(2,1)S(1)} custom-call(s32[6]{0:T(128)S(1)} %stack.27.place_ref.index_ref, bf16[224,512]{1,0:T(8,128)(2,1)S(1)} %copy-done.3, bf16[3584,128]{1,0:T(8,128)(2,1)S(1)} %constant_dynamic-update-slice_fusion.held_ref, bf16[3584,128]{1,0:T(8,128)(2,1)S(1)} %collective-permute-done.6.swapped_ref), custom_call_target="tpu_custom_call" | custom-call | flops 1644167168 | bytes 3145728 | tf_op jit(solution)/shard_map/attend/pallas_call | solution.py:200
  31.2 0.5 collective-permute-start.7
  31.6 1.1 collective-permute-done.7.theirs_ref
  32.8 9.7 %project.1 = (bf16[448,128]{1,0:T(8,128)(2,1)S(1)}, bf16[448,128]{1,0:T(8,128)(2,1)S(1)}, bf16[448,128]{1,0:T(8,128)(2,1)S(1)}, bf16[448,128]{1,0:T(8,128)(2,1)S...) custom-call(s32[6]{0:T(128)S(1)} %stack.27.place_ref.index_ref, ...), custom_call_target="tpu_custom_call" | custom-call | flops 2348810240 | bytes 10485760 | tf_op jit(solution)/shard_map/project/pallas_call | solution.py:268
  42.5 5.7 %collective-permute-start.9 = (bf16[448,128]{1,0:T(8,128)(2,1)S(1)}, bf16[448,128]{1,0:T(8,128)(2,1)S(1)}, u32[]{:S(2)}, u32[]{:S(2)}) collective-permute-start(bf16[448,128]{1,0:T(8,128)(2,1)S(1)} %get-tuple-element.52), channel_id=1, source_target_pairs={{0,14},{1,15},{2,4},{3,5},{4,2},{5,3},{6,8},{7,9},{8,6},{9,7},{10,... | collective-permute-start | bytes 344072 | tf_op jit(solution)/shard_map/ppermute | solution.py:406
  48.2 1.5 %collective-permute-start.16 = (bf16[448,128]{1,0:T(8,128)(2,1)S(1)}, bf16[448,128]{1,0:T(8,128)(2,1)S(1)}, u32[]{:S(2)}, u32[]{:S(2)}) collective-permute-start(bf16[448,128]{1,0:T(8,128)(2,1)S(1)} %get-tuple-element.64), channel_id=1, source_target_pairs={{0,14},{1,15},{2,4},{3,5},{4,2},{5,3},{6,8},{7,9},{8,6},{9,7},{10,... | collective-permute-start | bytes 344072 | tf_op jit(solution)/shard_map/ppermute | solution.py:406
  49.6 0.7 collective-permute-start.17
  50.4 1.0 collective-permute-done.9
  51.3 0.9 collective-permute-done.10
  52.3 0.4 collective-permute-start.12
  52.7 1.3 %collective-permute-start.11 = (bf16[448,128]{1,0:T(8,128)(2,1)S(1)}, bf16[448,128]{1,0:T(8,128)(2,1)S(1)}, u32[]{:S(2)}, u32[]{:S(2)}) collective-permute-start(bf16[448,128]{1,0:T(8,128)(2,1)S(1)} %add_convert_fusion.9), channel_id=1, source_target_pairs={{0,14},{1,15},{2,4},{3,5},{4,2},{5,3},{6,8},{7,9},{8,6},{9,7},{10,... | collective-permute-start | bytes 344072 | tf_op jit(solution)/shard_map/ppermute | solution.py:406
  54.0 0.8 collective-permute-done.17
  55.0 1.5 %collective-permute-start.18 = (bf16[448,128]{1,0:T(8,128)(2,1)S(1)}, bf16[448,128]{1,0:T(8,128)(2,1)S(1)}, u32[]{:S(2)}, u32[]{:S(2)}) collective-permute-start(bf16[448,128]{1,0:T(8,128)(2,1)S(1)} %add_convert_fusion.4), channel_id=1, source_target_pairs={{0,14},{1,15},{2,4},{3,5},{4,2},{5,3},{6,8},{7,9},{8,6},{9,7},{10,... | collective-permute-start | bytes 344072 | tf_op jit(solution)/shard_map/ppermute | solution.py:406
  56.7 0.9 collective-permute-done.11
  58.0 1.3 %collective-permute-start.13 = (bf16[448,128]{1,0:T(8,128)(2,1)S(1)}, bf16[448,128]{1,0:T(8,128)(2,1)S(1)}, u32[]{:S(2)}, u32[]{:S(2)}) collective-permute-start(bf16[448,128]{1,0:T(8,128)(2,1)S(1)} %add_convert_fusion.7), channel_id=1, source_target_pairs={{0,14},{1,15},{2,4},{3,5},{4,2},{5,3},{6,8},{7,9},{8,6},{9,7},{10,... | collective-permute-start | bytes 344072 | tf_op jit(solution)/shard_map/ppermute | solution.py:406
  59.3 0.4 collective-permute-done.19
  59.7 1.4 %collective-permute-done.18 = bf16[448,128]{1,0:T(8,128)(2,1)S(1)} collective-permute-done((bf16[448,128]{1,0:T(8,128)(2,1)S(1)}, bf16[448,128]{1,0:T(8,128)(2,1)S(1)}, u32[]{:S(2)}, u32[]{:S(2)}) %collective-permute-start.18) | collective-permute-done | bytes 114720 | tf_op jit(solution)/shard_map/ppermute | solution.py:406
  61.1 1.0 collective-permute-start.21
  62.2 0.7 collective-permute-done.14
  62.9 1.0 collective-permute-done.13
  64.0 0.4 collective-permute-start.22
  64.4 1.3 %collective-permute-start.15 = (bf16[448,128]{1,0:T(8,128)(2,1)S(1)}, bf16[448,128]{1,0:T(8,128)(2,1)S(1)}, u32[]{:S(2)}, u32[]{:S(2)}) collective-permute-start(bf16[448,128]{1,0:T(8,128)(2,1)S(1)} %add_convert_fusion.5), channel_id=1, source_target_pairs={{0,14},{1,15},{2,4},{3,5},{4,2},{5,3},{6,8},{7,9},{8,6},{9,7},{10,... | collective-permute-start | bytes 344072 | tf_op jit(solution)/shard_map/ppermute | solution.py:406
  66.0 1.1 collective-permute-done.20.two0
  67.2 1.2 %collective-permute-done.22.two1 = bf16[448,128]{1,0:T(8,128)(2,1)S(1)} collective-permute-done((bf16[448,128]{1,0:T(8,128)(2,1)S(1)}, bf16[448,128]{1,0:T(8,128)(2,1)S(1)}, u32[]{:S(2)}, u32[]{:S(2)}) %collective-permute-start.22) | collective-permute-done | bytes 114720 | tf_op jit(solution)/shard_map/ppermute | solution.py:406
  68.3 1.5 %collective-permute-done.15.one0 = bf16[448,128]{1,0:T(8,128)(2,1)S(1)} collective-permute-done((bf16[448,128]{1,0:T(8,128)(2,1)S(1)}, bf16[448,128]{1,0:T(8,128)(2,1)S(1)}, u32[]{:S(2)}, u32[]{:S(2)}) %collective-permute-start.15) | collective-permute-done | bytes 114720 | tf_op jit(solution)/shard_map/ppermute | solution.py:406
  70.1 1.3 %collective-permute-start.23 = (bf16[464,128]{1,0:T(8,128)(2,1)S(1)}, bf16[464,128]{1,0:T(8,128)(2,1)S(1)}, u32[]{:S(2)}, u32[]{:S(2)}) collective-permute-start(bf16[464,128]{1,0:T(8,128)(2,1)S(1)} %get-tuple-element.87.refs_1_), channel_id=1, source_target_pairs={{0,14},{1,15},{2,4},{3,5},{4,2},{5,3},{6,8},{7,9},{8,6},{9,7},{10,... | collective-permute-start | bytes 356360 | tf_op jit(solution)/shard_map/ppermute | solution.py:406
  71.7 1.5 %collective-permute-start.32 = (bf16[464,128]{1,0:T(8,128)(2,1)S(1)}, bf16[464,128]{1,0:T(8,128)(2,1)S(1)}, u32[]{:S(2)}, u32[]{:S(2)}) collective-permute-start(bf16[464,128]{1,0:T(8,128)(2,1)S(1)} %get-tuple-element.77), channel_id=1, source_target_pairs={{0,14},{1,15},{2,4},{3,5},{4,2},{5,3},{6,8},{7,9},{8,6},{9,7},{10,... | collective-permute-start | bytes 356360 | tf_op jit(solution)/shard_map/ppermute | solution.py:406
  73.1 0.6 collective-permute-start.33
  73.7 2.0 %collective-permute-done.23.refs_2_ = bf16[464,128]{1,0:T(8,128)(2,1)S(1)} collective-permute-done((bf16[464,128]{1,0:T(8,128)(2,1)S(1)}, bf16[464,128]{1,0:T(8,128)(2,1)S(1)}, u32[]{:S(2)}, u32[]{:S(2)}) %collective-permute-start.23) | collective-permute-done | bytes 118816 | tf_op jit(solution)/shard_map/ppermute | solution.py:406
  75.8 1.4 %collective-permute-start.25 = (bf16[464,128]{1,0:T(8,128)(2,1)S(1)}, bf16[464,128]{1,0:T(8,128)(2,1)S(1)}, u32[]{:S(2)}, u32[]{:S(2)}) collective-permute-start(bf16[464,128]{1,0:T(8,128)(2,1)S(1)} %collective-permute-done.24.refs_3_), channel_id=1, source_target_pairs={{0,14},{1,15},{2,4},{3,5},{4,2},{5,3},{6,8},{7,9},{8,6},{9,7},{10,... | collective-permute-start | bytes 356360 | tf_op jit(solution)/shard_map/ppermute | solution.py:406
  77.1 7.3 %collective-permute-start.42 = (bf16[928,128]{1,0:T(8,128)(2,1)S(1)}, bf16[928,128]{1,0:T(8,128)(2,1)S(1)}, u32[]{:S(2)}, u32[]{:S(2)}) collective-permute-start(bf16[928,128]{1,0:T(8,128)(2,1)S(1)} %pad_maximum_fusion.5), channel_id=1, source_target_pairs={{0,1},{1,0},{2,3},{3,2},{4,5},{5,4},{6,7},{7,6},{8,9},{9,8},{10,11... | collective-permute-start | bytes 712712 | tf_op jit(solution)/shard_map/ppermute | solution.py:406
  84.5 1.4 %collective-permute-start.34 = (bf16[464,128]{1,0:T(8,128)(2,1)S(1)}, bf16[464,128]{1,0:T(8,128)(2,1)S(1)}, u32[]{:S(2)}, u32[]{:S(2)}) collective-permute-start(bf16[464,128]{1,0:T(8,128)(2,1)S(1)} %collective-permute-done.33.refs_5_), channel_id=1, source_target_pairs={{0,14},{1,15},{2,4},{3,5},{4,2},{5,3},{6,8},{7,9},{8,6},{9,7},{10,... | collective-permute-start | bytes 356360 | tf_op jit(solution)/shard_map/ppermute | solution.py:406
  85.8 1.1 collective-permute-start.35
  87.0 1.4 %collective-permute-start.27 = (bf16[464,128]{1,0:T(8,128)(2,1)S(1)}, bf16[464,128]{1,0:T(8,128)(2,1)S(1)}, u32[]{:S(2)}, u32[]{:S(2)}) collective-permute-start(bf16[464,128]{1,0:T(8,128)(2,1)S(1)} %collective-permute-done.26.refs_1_), channel_id=1, source_target_pairs={{0,14},{1,15},{2,4},{3,5},{4,2},{5,3},{6,8},{7,9},{8,6},{9,7},{10,... | collective-permute-start | bytes 356360 | tf_op jit(solution)/shard_map/ppermute | solution.py:406
  88.5 1.8 %collective-permute-done.34.refs_2_ = bf16[464,128]{1,0:T(8,128)(2,1)S(1)} collective-permute-done((bf16[464,128]{1,0:T(8,128)(2,1)S(1)}, bf16[464,128]{1,0:T(8,128)(2,1)S(1)}, u32[]{:S(2)}, u32[]{:S(2)}) %collective-permute-start.34) | collective-permute-done | bytes 118816 | tf_op jit(solution)/shard_map/ppermute | solution.py:406
  90.3 0.4 collective-permute-done.35.refs_3_
  90.6 1.4 %collective-permute-start.36 = (bf16[464,128]{1,0:T(8,128)(2,1)S(1)}, bf16[464,128]{1,0:T(8,128)(2,1)S(1)}, u32[]{:S(2)}, u32[]{:S(2)}) collective-permute-start(bf16[464,128]{1,0:T(8,128)(2,1)S(1)} %collective-permute-done.35.refs_3_), channel_id=1, source_target_pairs={{0,14},{1,15},{2,4},{3,5},{4,2},{5,3},{6,8},{7,9},{8,6},{9,7},{10,... | collective-permute-start | bytes 356360 | tf_op jit(solution)/shard_map/ppermute | solution.py:406
  92.1 1.4 %collective-permute-start.28 = (bf16[464,128]{1,0:T(8,128)(2,1)S(1)}, bf16[464,128]{1,0:T(8,128)(2,1)S(1)}, u32[]{:S(2)}, u32[]{:S(2)}) collective-permute-start(bf16[464,128]{1,0:T(8,128)(2,1)S(1)} %collective-permute-done.25.refs_0_), channel_id=1, source_target_pairs={{0,2},{1,3},{2,0},{3,1},{4,6},{5,7},{6,4},{7,5},{8,10},{9,11},{10,... | collective-permute-start | bytes 356360 | tf_op jit(solution)/shard_map/ppermute | solution.py:406
  93.5 2.5 %collective-permute-start.44 = (bf16[928,128]{1,0:T(8,128)(2,1)S(1)}, bf16[928,128]{1,0:T(8,128)(2,1)S(1)}, u32[]{:S(2)}, u32[]{:S(2)}) collective-permute-start(bf16[928,128]{1,0:T(8,128)(2,1)S(1)} %pad_maximum_fusion.7), channel_id=1, source_target_pairs={{0,1},{1,0},{2,3},{3,2},{4,5},{5,4},{6,7},{7,6},{8,9},{9,8},{10,11... | collective-permute-start | bytes 712712 | tf_op jit(solution)/shard_map/ppermute | solution.py:406
  96.0 2.0 %collective-permute-done.28.refs_1_ = bf16[464,128]{1,0:T(8,128)(2,1)S(1)} collective-permute-done((bf16[464,128]{1,0:T(8,128)(2,1)S(1)}, bf16[464,128]{1,0:T(8,128)(2,1)S(1)}, u32[]{:S(2)}, u32[]{:S(2)}) %collective-permute-start.28) | collective-permute-done | bytes 118816 | tf_op jit(solution)/shard_map/ppermute | solution.py:406
  98.0 2.2 %collective-permute-start.43 = (bf16[928,128]{1,0:T(8,128)(2,1)S(1)}, bf16[928,128]{1,0:T(8,128)(2,1)S(1)}, u32[]{:S(2)}, u32[]{:S(2)}) collective-permute-start(bf16[928,128]{1,0:T(8,128)(2,1)S(1)} %pad_maximum_fusion.6), channel_id=1, source_target_pairs={{0,1},{1,0},{2,3},{3,2},{4,5},{5,4},{6,7},{7,6},{8,9},{9,8},{10,11... | collective-permute-start | bytes 712712 | tf_op jit(solution)/shard_map/ppermute | solution.py:406
  100.2 1.3 %collective-permute-start.29 = (bf16[464,128]{1,0:T(8,128)(2,1)S(1)}, bf16[464,128]{1,0:T(8,128)(2,1)S(1)}, u32[]{:S(2)}, u32[]{:S(2)}) collective-permute-start(bf16[464,128]{1,0:T(8,128)(2,1)S(1)} %collective-permute-done.28.refs_1_), channel_id=1, source_target_pairs={{0,14},{1,15},{2,4},{3,5},{4,2},{5,3},{6,8},{7,9},{8,6},{9,7},{10,... | collective-permute-start | bytes 356360 | tf_op jit(solution)/shard_map/ppermute | solution.py:406
  101.6 0.4 collective-permute-start.41
  102.2 4.0 %collective-permute-done.29.refs_0_ = bf16[464,128]{1,0:T(8,128)(2,1)S(1)} collective-permute-done((bf16[464,128]{1,0:T(8,128)(2,1)S(1)}, bf16[464,128]{1,0:T(8,128)(2,1)S(1)}, u32[]{:S(2)}, u32[]{:S(2)}) %collective-permute-start.29) | collective-permute-done | bytes 118816 | tf_op jit(solution)/shard_map/ppermute | solution.py:406
  106.2 0.9 collective-permute-start.39
  107.2 0.5 collective-permute-start.31
  107.7 2.0 %assemble.4 = (bf16[224,8192]{1,0:T(8,128)(2,1)}, f32[8,2,4,256]{3,2,1,0:T(4,128)S(1)}) custom-call(s32[6]{0:T(128)S(1)} %stack.27.place_ref.index_ref, bf16[464,128]{1,0:T(8,128)(2,1)S(1)} %get-tuple-element.77, bf16[464,128]{1,0:T(8,128)(2,1)S(1)} %get-tuple-element.87.refs_1_, bf16[464,128]{1,0:T(8,128)(2,1)S(1)} %collective-permute-done.23.refs_2_, ...), custom_call_target="tpu_custom_call" | custom-call | flops 1048576 | bytes 4194304 | tf_op jit(solution)/shard_map/assemble/pallas_call | solution.py:383
  109.7 1.7 %assemble.5 = (bf16[224,8192]{1,0:T(8,128)(2,1)}, f32[8,2,4,256]{3,2,1,0:T(4,128)S(1)}) custom-call(s32[6]{0:T(128)S(1)} %stack.27.place_ref.index_ref, bf16[464,128]{1,0:T(8,128)(2,1)S(1)} %collective-permute-done.25.refs_0_, bf16[464,128]{1,0:T(8,128)(2,1)S(1)} %collective-permute-done.26.refs_1_, ...), custom_call_target="tpu_custom_call", output_to_operand_aliasing={{0}: (7, {})} | custom-call | flops 1048576 | bytes 4194304 | tf_op jit(solution)/shard_map/assemble/pallas_call | solution.py:383
  111.5 1.7 %assemble.6 = (bf16[224,8192]{1,0:T(8,128)(2,1)}, f32[8,2,4,256]{3,2,1,0:T(4,128)S(1)}) custom-call(s32[6]{0:T(128)S(1)} %stack.27.place_ref.index_ref, bf16[464,128]{1,0:T(8,128)(2,1)S(1)} %collective-permute-done.27.refs_0_, bf16[464,128]{1,0:T(8,128)(2,1)S(1)} %collective-permute-done.28.refs_1_, ...), custom_call_target="tpu_custom_call", output_to_operand_aliasing={{0}: (7, {})} | custom-call | flops 1048576 | bytes 4194304 | tf_op jit(solution)/shard_map/assemble/pallas_call | solution.py:383
  113.2 2.1 %assemble.7 = (bf16[224,8192]{1,0:T(8,128)(2,1)}, f32[64,224]{1,0:T(8,128)}) custom-call(s32[6]{0:T(128)S(1)} %stack.27.place_ref.index_ref, bf16[464,128]{1,0:T(8,128)(2,1)S(1)} %collective-permute-done.29.refs_0_, bf16[464,128]{1,0:T(8,128)(2,1)S(1)} %collective-permute-done.30.refs_1_, ...), custom_call_target="tpu_custom_call", output_to_operand_aliasing={{0}: (4, {})} | custom-call | flops 1048576 | bytes 4194304 | tf_op jit(solution)/shard_map/assemble/pallas_call | solution.py:383
  (68 shorter events, 2.8 us)
Async XLA Ops:
  0.6 32.1 %collective-permute-start.8 = (bf16[512,8192]{1,0:T(8,128)(2,1)}, bf16[512,8192]{1,0:T(8,128)(2,1)}, u32[]{:S(2)}, u32[]{:S(2)}) collective-permute-start(bf16[512,8192]{1,0:T(8,128)(2,1)} %own_hbm.1), channel_id=1, source_target_pairs={{0,1},{1,0},{2,3},{3,2},{4,5},{5,4},{6,7},{7,6},{8,9},{9,8},{10,11... | collective-permute-start | bytes 25165832 | tf_op jit(solution)/shard_map/ppermute | solution.py:406
  4.8 4.9 %collective-permute-start.2 = (bf16[224,128]{1,0:T(8,128)(2,1)S(1)}, bf16[224,128]{1,0:T(8,128)(2,1)S(1)}, u32[]{:S(2)}, u32[]{:S(2)}) collective-permute-start(bf16[224,128]{1,0:T(8,128)(2,1)S(1)} %get-tuple-element.101), channel_id=1, source_target_pairs={{0,32},{1,129},{2,34},{3,131},{4,36},{5,133},{6,38},{7,135},{8,40}... | collective-permute-start | bytes 172040 | tf_op jit(solution)/shard_map/ppermute | solution.py:420
  6.1 3.6 %collective-permute-start.1 = (bf16[224,128]{1,0:T(8,128)(2,1)S(1)}, bf16[224,128]{1,0:T(8,128)(2,1)S(1)}, u32[]{:S(2)}, u32[]{:S(2)}) collective-permute-start(bf16[224,128]{1,0:T(8,128)(2,1)S(1)} %get-tuple-element.101), channel_id=1, source_target_pairs={{0,48},{1,193},{2,50},{3,195},{4,52},{5,197},{6,54},{7,199},{8,56}... | collective-permute-start | bytes 172040 | tf_op jit(solution)/shard_map/ppermute | solution.py:420
  6.9 4.2 %collective-permute-start = (bf16[224,128]{1,0:T(8,128)(2,1)S(1)}, bf16[224,128]{1,0:T(8,128)(2,1)S(1)}, u32[]{:S(2)}, u32[]{:S(2)}) collective-permute-start(bf16[224,128]{1,0:T(8,128)(2,1)S(1)} %get-tuple-element.101), channel_id=1, source_target_pairs={{0,16},{1,65},{2,18},{3,67},{4,20},{5,69},{6,22},{7,71},{8,24},{9,... | collective-permute-start | bytes 172040 | tf_op jit(solution)/shard_map/ppermute | solution.py:420
  11.1 9.9 %collective-permute-start.5 = (bf16[896,128]{1,0:T(8,128)(2,1)S(1)}, bf16[896,128]{1,0:T(8,128)(2,1)S(1)}, u32[]{:S(2)}, u32[]{:S(2)}) collective-permute-start(bf16[896,128]{1,0:T(8,128)(2,1)S(1)} %pad_maximum_fusion.8), channel_id=1, source_target_pairs={{0,128},{1,33},{2,130},{3,35},{4,132},{5,37},{6,134},{7,39},{8,136... | collective-permute-start | bytes 688136 | tf_op jit(solution)/shard_map/ppermute | solution.py:420
  13.9 7.0 %collective-permute-start.4 = (bf16[896,128]{1,0:T(8,128)(2,1)S(1)}, bf16[896,128]{1,0:T(8,128)(2,1)S(1)}, u32[]{:S(2)}, u32[]{:S(2)}) collective-permute-start(bf16[896,128]{1,0:T(8,128)(2,1)S(1)} %pad_maximum_fusion.8), channel_id=1, source_target_pairs={{0,192},{1,49},{2,194},{3,51},{4,196},{5,53},{6,198},{7,55},{8,200... | collective-permute-start | bytes 688136 | tf_op jit(solution)/shard_map/ppermute | solution.py:420
  14.8 6.1 %collective-permute-start.3 = (bf16[896,128]{1,0:T(8,128)(2,1)S(1)}, bf16[896,128]{1,0:T(8,128)(2,1)S(1)}, u32[]{:S(2)}, u32[]{:S(2)}) collective-permute-start(bf16[896,128]{1,0:T(8,128)(2,1)S(1)} %pad_maximum_fusion.8), channel_id=1, source_target_pairs={{0,64},{1,17},{2,66},{3,19},{4,68},{5,21},{6,70},{7,23},{8,72},{9,... | collective-permute-start | bytes 688136 | tf_op jit(solution)/shard_map/ppermute | solution.py:420
  15.5 17.3 %copy-start = (bf16[512,128]{1,0:T(8,128)(2,1)S(1)}, bf16[512,128]{1,0:T(8,128)(2,1)}, u32[]{:S(2)}) copy-start(bf16[512,128]{1,0:T(8,128)(2,1)} %constant.26.clone.gather_ref) | copy-start | bytes 393220
  15.5 17.3 %copy-start.1 = (bf16[256,256]{1,0:T(8,128)(2,1)S(1)}, bf16[256,256]{1,0:T(8,128)(2,1)}, u32[]{:S(2)}) copy-start(bf16[256,256]{1,0:T(8,128)(2,1)} %constant.25.clone.turn_ref) | copy-start | bytes 393220
  15.5 17.3 %copy-start.2 = (s32[8192]{0:T(1024)S(1)}, s32[8192]{0:T(1024)}, u32[]{:S(2)}) copy-start(s32[8192]{0:T(1024)} %param.11) | copy-start | bytes 98308
  21.0 5.6 %collective-permute-start.6 = (bf16[3584,128]{1,0:T(8,128)(2,1)S(1)}, bf16[3584,128]{1,0:T(8,128)(2,1)S(1)}, u32[]{:S(2)}, u32[]{:S(2)}) collective-permute-start(bf16[3584,128]{1,0:T(8,128)(2,1)S(1)} %constant_dynamic-update-slice_fusion.held_ref), channel_id=1, source_target_pairs={{0,1},{1,0},{2,3},{3,2},{4,5},{5,4},{6,7},{7,6},{8,9},{9,8},{10,11... | collective-permute-start | bytes 2752520 | tf_op jit(solution)/shard_map/ppermute | solution.py:406
  26.7 0.9 copy-start.3
  31.2 1.6 %collective-permute-start.7 = (bf16[224,512]{1,0:T(8,128)(2,1)S(1)}, bf16[224,512]{1,0:T(8,128)(2,1)S(1)}, u32[]{:S(2)}, u32[]{:S(2)}) collective-permute-start(bf16[224,512]{1,0:T(8,128)(2,1)S(1)} %attend.1.mine_ref), channel_id=1, source_target_pairs={{0,1},{1,0},{2,3},{3,2},{4,5},{5,4},{6,7},{7,6},{8,9},{9,8},{10,11... | collective-permute-start | bytes 688136 | tf_op jit(solution)/shard_map/ppermute | solution.py:406
  42.5 8.8 %collective-permute-start.9 = (bf16[448,128]{1,0:T(8,128)(2,1)S(1)}, bf16[448,128]{1,0:T(8,128)(2,1)S(1)}, u32[]{:S(2)}, u32[]{:S(2)}) collective-permute-start(bf16[448,128]{1,0:T(8,128)(2,1)S(1)} %get-tuple-element.52), channel_id=1, source_target_pairs={{0,14},{1,15},{2,4},{3,5},{4,2},{5,3},{6,8},{7,9},{8,6},{9,7},{10,... | collective-permute-start | bytes 344072 | tf_op jit(solution)/shard_map/ppermute | solution.py:406
  48.2 4.0 %collective-permute-start.10 = (bf16[448,128]{1,0:T(8,128)(2,1)S(1)}, bf16[448,128]{1,0:T(8,128)(2,1)S(1)}, u32[]{:S(2)}, u32[]{:S(2)}) collective-permute-start(bf16[448,128]{1,0:T(8,128)(2,1)S(1)} %get-tuple-element.53), channel_id=1, source_target_pairs={{0,2},{1,3},{2,0},{3,1},{4,6},{5,7},{6,4},{7,5},{8,10},{9,11},{10,... | collective-permute-start | bytes 344072 | tf_op jit(solution)/shard_map/ppermute | solution.py:406
  48.2 5.8 %collective-permute-start.16 = (bf16[448,128]{1,0:T(8,128)(2,1)S(1)}, bf16[448,128]{1,0:T(8,128)(2,1)S(1)}, u32[]{:S(2)}, u32[]{:S(2)}) collective-permute-start(bf16[448,128]{1,0:T(8,128)(2,1)S(1)} %get-tuple-element.64), channel_id=1, source_target_pairs={{0,14},{1,15},{2,4},{3,5},{4,2},{5,3},{6,8},{7,9},{8,6},{9,7},{10,... | collective-permute-start | bytes 344072 | tf_op jit(solution)/shard_map/ppermute | solution.py:406
  49.6 5.2 %collective-permute-start.17 = (bf16[448,128]{1,0:T(8,128)(2,1)S(1)}, bf16[448,128]{1,0:T(8,128)(2,1)S(1)}, u32[]{:S(2)}, u32[]{:S(2)}) collective-permute-start(bf16[448,128]{1,0:T(8,128)(2,1)S(1)} %get-tuple-element.65), channel_id=1, source_target_pairs={{0,2},{1,3},{2,0},{3,1},{4,6},{5,7},{6,4},{7,5},{8,10},{9,11},{10,... | collective-permute-start | bytes 344072 | tf_op jit(solution)/shard_map/ppermute | solution.py:406
  52.3 4.5 %collective-permute-start.12 = (bf16[448,128]{1,0:T(8,128)(2,1)S(1)}, bf16[448,128]{1,0:T(8,128)(2,1)S(1)}, u32[]{:S(2)}, u32[]{:S(2)}) collective-permute-start(bf16[448,128]{1,0:T(8,128)(2,1)S(1)} %add_convert_fusion.8), channel_id=1, source_target_pairs={{0,2},{1,3},{2,0},{3,1},{4,6},{5,7},{6,4},{7,5},{8,10},{9,11},{10,... | collective-permute-start | bytes 344072 | tf_op jit(solution)/shard_map/ppermute | solution.py:406
  52.7 4.9 %collective-permute-start.11 = (bf16[448,128]{1,0:T(8,128)(2,1)S(1)}, bf16[448,128]{1,0:T(8,128)(2,1)S(1)}, u32[]{:S(2)}, u32[]{:S(2)}) collective-permute-start(bf16[448,128]{1,0:T(8,128)(2,1)S(1)} %add_convert_fusion.9), channel_id=1, source_target_pairs={{0,14},{1,15},{2,4},{3,5},{4,2},{5,3},{6,8},{7,9},{8,6},{9,7},{10,... | collective-permute-start | bytes 344072 | tf_op jit(solution)/shard_map/ppermute | solution.py:406
  54.8 4.9 %collective-permute-start.19 = (bf16[448,128]{1,0:T(8,128)(2,1)S(1)}, bf16[448,128]{1,0:T(8,128)(2,1)S(1)}, u32[]{:S(2)}, u32[]{:S(2)}) collective-permute-start(bf16[448,128]{1,0:T(8,128)(2,1)S(1)} %add_convert_fusion.3), channel_id=1, source_target_pairs={{0,2},{1,3},{2,0},{3,1},{4,6},{5,7},{6,4},{7,5},{8,10},{9,11},{10,... | collective-permute-start | bytes 344072 | tf_op jit(solution)/shard_map/ppermute | solution.py:406
  55.0 6.1 %collective-permute-start.18 = (bf16[448,128]{1,0:T(8,128)(2,1)S(1)}, bf16[448,128]{1,0:T(8,128)(2,1)S(1)}, u32[]{:S(2)}, u32[]{:S(2)}) collective-permute-start(bf16[448,128]{1,0:T(8,128)(2,1)S(1)} %add_convert_fusion.4), channel_id=1, source_target_pairs={{0,14},{1,15},{2,4},{3,5},{4,2},{5,3},{6,8},{7,9},{8,6},{9,7},{10,... | collective-permute-start | bytes 344072 | tf_op jit(solution)/shard_map/ppermute | solution.py:406
  57.6 5.2 %collective-permute-start.14 = (bf16[448,128]{1,0:T(8,128)(2,1)S(1)}, bf16[448,128]{1,0:T(8,128)(2,1)S(1)}, u32[]{:S(2)}, u32[]{:S(2)}) collective-permute-start(bf16[448,128]{1,0:T(8,128)(2,1)S(1)} %add_convert_fusion.6), channel_id=1, source_target_pairs={{0,2},{1,3},{2,0},{3,1},{4,6},{5,7},{6,4},{7,5},{8,10},{9,11},{10,... | collective-permute-start | bytes 344072 | tf_op jit(solution)/shard_map/ppermute | solution.py:406
  58.0 5.9 %collective-permute-start.13 = (bf16[448,128]{1,0:T(8,128)(2,1)S(1)}, bf16[448,128]{1,0:T(8,128)(2,1)S(1)}, u32[]{:S(2)}, u32[]{:S(2)}) collective-permute-start(bf16[448,128]{1,0:T(8,128)(2,1)S(1)} %add_convert_fusion.7), channel_id=1, source_target_pairs={{0,14},{1,15},{2,4},{3,5},{4,2},{5,3},{6,8},{7,9},{8,6},{9,7},{10,... | collective-permute-start | bytes 344072 | tf_op jit(solution)/shard_map/ppermute | solution.py:406
  61.1 4.9 %collective-permute-start.21 = (bf16[448,128]{1,0:T(8,128)(2,1)S(1)}, bf16[448,128]{1,0:T(8,128)(2,1)S(1)}, u32[]{:S(2)}, u32[]{:S(2)}) collective-permute-start(bf16[448,128]{1,0:T(8,128)(2,1)S(1)} %add_convert_fusion.1), channel_id=1, source_target_pairs={{0,14},{1,15},{2,4},{3,5},{4,2},{5,3},{6,8},{7,9},{8,6},{9,7},{10,... | collective-permute-start | bytes 344072 | tf_op jit(solution)/shard_map/ppermute | solution.py:406
  62.1 5.0 %collective-permute-start.20 = (bf16[448,128]{1,0:T(8,128)(2,1)S(1)}, bf16[448,128]{1,0:T(8,128)(2,1)S(1)}, u32[]{:S(2)}, u32[]{:S(2)}) collective-permute-start(bf16[448,128]{1,0:T(8,128)(2,1)S(1)} %add_convert_fusion.2), channel_id=1, source_target_pairs={{0,2},{1,3},{2,0},{3,1},{4,6},{5,7},{6,4},{7,5},{8,10},{9,11},{10,... | collective-permute-start | bytes 344072 | tf_op jit(solution)/shard_map/ppermute | solution.py:406
  64.0 4.4 %collective-permute-start.22 = (bf16[448,128]{1,0:T(8,128)(2,1)S(1)}, bf16[448,128]{1,0:T(8,128)(2,1)S(1)}, u32[]{:S(2)}, u32[]{:S(2)}) collective-permute-start(bf16[448,128]{1,0:T(8,128)(2,1)S(1)} %add_convert_fusion), channel_id=1, source_target_pairs={{0,2},{1,3},{2,0},{3,1},{4,6},{5,7},{6,4},{7,5},{8,10},{9,11},{10,... | collective-permute-start | bytes 344072 | tf_op jit(solution)/shard_map/ppermute | solution.py:406
  64.4 5.5 %collective-permute-start.15 = (bf16[448,128]{1,0:T(8,128)(2,1)S(1)}, bf16[448,128]{1,0:T(8,128)(2,1)S(1)}, u32[]{:S(2)}, u32[]{:S(2)}) collective-permute-start(bf16[448,128]{1,0:T(8,128)(2,1)S(1)} %add_convert_fusion.5), channel_id=1, source_target_pairs={{0,14},{1,15},{2,4},{3,5},{4,2},{5,3},{6,8},{7,9},{8,6},{9,7},{10,... | collective-permute-start | bytes 344072 | tf_op jit(solution)/shard_map/ppermute | solution.py:406
  70.1 5.6 %collective-permute-start.23 = (bf16[464,128]{1,0:T(8,128)(2,1)S(1)}, bf16[464,128]{1,0:T(8,128)(2,1)S(1)}, u32[]{:S(2)}, u32[]{:S(2)}) collective-permute-start(bf16[464,128]{1,0:T(8,128)(2,1)S(1)} %get-tuple-element.87.refs_1_), channel_id=1, source_target_pairs={{0,14},{1,15},{2,4},{3,5},{4,2},{5,3},{6,8},{7,9},{8,6},{9,7},{10,... | collective-permute-start | bytes 356360 | tf_op jit(solution)/shard_map/ppermute | solution.py:406
  71.4 4.3 %collective-permute-start.24 = (bf16[464,128]{1,0:T(8,128)(2,1)S(1)}, bf16[464,128]{1,0:T(8,128)(2,1)S(1)}, u32[]{:S(2)}, u32[]{:S(2)}) collective-permute-start(bf16[464,128]{1,0:T(8,128)(2,1)S(1)} %get-tuple-element.77), channel_id=1, source_target_pairs={{0,2},{1,3},{2,0},{3,1},{4,6},{5,7},{6,4},{7,5},{8,10},{9,11},{10,... | collective-permute-start | bytes 356360 | tf_op jit(solution)/shard_map/ppermute | solution.py:406
  71.7 12.8 %collective-permute-start.32 = (bf16[464,128]{1,0:T(8,128)(2,1)S(1)}, bf16[464,128]{1,0:T(8,128)(2,1)S(1)}, u32[]{:S(2)}, u32[]{:S(2)}) collective-permute-start(bf16[464,128]{1,0:T(8,128)(2,1)S(1)} %get-tuple-element.77), channel_id=1, source_target_pairs={{0,14},{1,15},{2,4},{3,5},{4,2},{5,3},{6,8},{7,9},{8,6},{9,7},{10,... | collective-permute-start | bytes 356360 | tf_op jit(solution)/shard_map/ppermute | solution.py:406
  73.1 11.3 %collective-permute-start.33 = (bf16[464,128]{1,0:T(8,128)(2,1)S(1)}, bf16[464,128]{1,0:T(8,128)(2,1)S(1)}, u32[]{:S(2)}, u32[]{:S(2)}) collective-permute-start(bf16[464,128]{1,0:T(8,128)(2,1)S(1)} %get-tuple-element.87.refs_1_), channel_id=1, source_target_pairs={{0,2},{1,3},{2,0},{3,1},{4,6},{5,7},{6,4},{7,5},{8,10},{9,11},{10,... | collective-permute-start | bytes 356360 | tf_op jit(solution)/shard_map/ppermute | solution.py:406
  75.8 11.2 %collective-permute-start.25 = (bf16[464,128]{1,0:T(8,128)(2,1)S(1)}, bf16[464,128]{1,0:T(8,128)(2,1)S(1)}, u32[]{:S(2)}, u32[]{:S(2)}) collective-permute-start(bf16[464,128]{1,0:T(8,128)(2,1)S(1)} %collective-permute-done.24.refs_3_), channel_id=1, source_target_pairs={{0,14},{1,15},{2,4},{3,5},{4,2},{5,3},{6,8},{7,9},{8,6},{9,7},{10,... | collective-permute-start | bytes 356360 | tf_op jit(solution)/shard_map/ppermute | solution.py:406
  77.1 9.9 %collective-permute-start.26 = (bf16[464,128]{1,0:T(8,128)(2,1)S(1)}, bf16[464,128]{1,0:T(8,128)(2,1)S(1)}, u32[]{:S(2)}, u32[]{:S(2)}) collective-permute-start(bf16[464,128]{1,0:T(8,128)(2,1)S(1)} %collective-permute-done.23.refs_2_), channel_id=1, source_target_pairs={{0,2},{1,3},{2,0},{3,1},{4,6},{5,7},{6,4},{7,5},{8,10},{9,11},{10,... | collective-permute-start | bytes 356360 | tf_op jit(solution)/shard_map/ppermute | solution.py:406
  77.1 24.4 %collective-permute-start.42 = (bf16[928,128]{1,0:T(8,128)(2,1)S(1)}, bf16[928,128]{1,0:T(8,128)(2,1)S(1)}, u32[]{:S(2)}, u32[]{:S(2)}) collective-permute-start(bf16[928,128]{1,0:T(8,128)(2,1)S(1)} %pad_maximum_fusion.5), channel_id=1, source_target_pairs={{0,1},{1,0},{2,3},{3,2},{4,5},{5,4},{6,7},{7,6},{8,9},{9,8},{10,11... | collective-permute-start | bytes 712712 | tf_op jit(solution)/shard_map/ppermute | solution.py:406
  84.5 5.8 %collective-permute-start.34 = (bf16[464,128]{1,0:T(8,128)(2,1)S(1)}, bf16[464,128]{1,0:T(8,128)(2,1)S(1)}, u32[]{:S(2)}, u32[]{:S(2)}) collective-permute-start(bf16[464,128]{1,0:T(8,128)(2,1)S(1)} %collective-permute-done.33.refs_5_), channel_id=1, source_target_pairs={{0,14},{1,15},{2,4},{3,5},{4,2},{5,3},{6,8},{7,9},{8,6},{9,7},{10,... | collective-permute-start | bytes 356360 | tf_op jit(solution)/shard_map/ppermute | solution.py:406
  85.8 4.8 %collective-permute-start.35 = (bf16[464,128]{1,0:T(8,128)(2,1)S(1)}, bf16[464,128]{1,0:T(8,128)(2,1)S(1)}, u32[]{:S(2)}, u32[]{:S(2)}) collective-permute-start(bf16[464,128]{1,0:T(8,128)(2,1)S(1)} %collective-permute-done.32.refs_4_), channel_id=1, source_target_pairs={{0,2},{1,3},{2,0},{3,1},{4,6},{5,7},{6,4},{7,5},{8,10},{9,11},{10,... | collective-permute-start | bytes 356360 | tf_op jit(solution)/shard_map/ppermute | solution.py:406
  87.0 6.5 %collective-permute-start.27 = (bf16[464,128]{1,0:T(8,128)(2,1)S(1)}, bf16[464,128]{1,0:T(8,128)(2,1)S(1)}, u32[]{:S(2)}, u32[]{:S(2)}) collective-permute-start(bf16[464,128]{1,0:T(8,128)(2,1)S(1)} %collective-permute-done.26.refs_1_), channel_id=1, source_target_pairs={{0,14},{1,15},{2,4},{3,5},{4,2},{5,3},{6,8},{7,9},{8,6},{9,7},{10,... | collective-permute-start | bytes 356360 | tf_op jit(solution)/shard_map/ppermute | solution.py:406
  90.6 9.6 %collective-permute-start.36 = (bf16[464,128]{1,0:T(8,128)(2,1)S(1)}, bf16[464,128]{1,0:T(8,128)(2,1)S(1)}, u32[]{:S(2)}, u32[]{:S(2)}) collective-permute-start(bf16[464,128]{1,0:T(8,128)(2,1)S(1)} %collective-permute-done.35.refs_3_), channel_id=1, source_target_pairs={{0,14},{1,15},{2,4},{3,5},{4,2},{5,3},{6,8},{7,9},{8,6},{9,7},{10,... | collective-permute-start | bytes 356360 | tf_op jit(solution)/shard_map/ppermute | solution.py:406
  92.0 9.5 %collective-permute-start.37 = (bf16[464,128]{1,0:T(8,128)(2,1)S(1)}, bf16[464,128]{1,0:T(8,128)(2,1)S(1)}, u32[]{:S(2)}, u32[]{:S(2)}) collective-permute-start(bf16[464,128]{1,0:T(8,128)(2,1)S(1)} %collective-permute-done.34.refs_2_), channel_id=1, source_target_pairs={{0,2},{1,3},{2,0},{3,1},{4,6},{5,7},{6,4},{7,5},{8,10},{9,11},{10,... | collective-permute-start | bytes 356360 | tf_op jit(solution)/shard_map/ppermute | solution.py:406
  92.1 5.9 %collective-permute-start.28 = (bf16[464,128]{1,0:T(8,128)(2,1)S(1)}, bf16[464,128]{1,0:T(8,128)(2,1)S(1)}, u32[]{:S(2)}, u32[]{:S(2)}) collective-permute-start(bf16[464,128]{1,0:T(8,128)(2,1)S(1)} %collective-permute-done.25.refs_0_), channel_id=1, source_target_pairs={{0,2},{1,3},{2,0},{3,1},{4,6},{5,7},{6,4},{7,5},{8,10},{9,11},{10,... | collective-permute-start | bytes 356360 | tf_op jit(solution)/shard_map/ppermute | solution.py:406
  93.5 8.4 %collective-permute-start.44 = (bf16[928,128]{1,0:T(8,128)(2,1)S(1)}, bf16[928,128]{1,0:T(8,128)(2,1)S(1)}, u32[]{:S(2)}, u32[]{:S(2)}) collective-permute-start(bf16[928,128]{1,0:T(8,128)(2,1)S(1)} %pad_maximum_fusion.7), channel_id=1, source_target_pairs={{0,1},{1,0},{2,3},{3,2},{4,5},{5,4},{6,7},{7,6},{8,9},{9,8},{10,11... | collective-permute-start | bytes 712712 | tf_op jit(solution)/shard_map/ppermute | solution.py:406
  98.0 9.2 %collective-permute-start.43 = (bf16[928,128]{1,0:T(8,128)(2,1)S(1)}, bf16[928,128]{1,0:T(8,128)(2,1)S(1)}, u32[]{:S(2)}, u32[]{:S(2)}) collective-permute-start(bf16[928,128]{1,0:T(8,128)(2,1)S(1)} %pad_maximum_fusion.6), channel_id=1, source_target_pairs={{0,1},{1,0},{2,3},{3,2},{4,5},{5,4},{6,7},{7,6},{8,9},{9,8},{10,11... | collective-permute-start | bytes 712712 | tf_op jit(solution)/shard_map/ppermute | solution.py:406
  100.2 6.0 %collective-permute-start.29 = (bf16[464,128]{1,0:T(8,128)(2,1)S(1)}, bf16[464,128]{1,0:T(8,128)(2,1)S(1)}, u32[]{:S(2)}, u32[]{:S(2)}) collective-permute-start(bf16[464,128]{1,0:T(8,128)(2,1)S(1)} %collective-permute-done.28.refs_1_), channel_id=1, source_target_pairs={{0,14},{1,15},{2,4},{3,5},{4,2},{5,3},{6,8},{7,9},{8,6},{9,7},{10,... | collective-permute-start | bytes 356360 | tf_op jit(solution)/shard_map/ppermute | solution.py:406
  101.5 5.6 %collective-permute-start.30 = (bf16[464,128]{1,0:T(8,128)(2,1)S(1)}, bf16[464,128]{1,0:T(8,128)(2,1)S(1)}, u32[]{:S(2)}, u32[]{:S(2)}) collective-permute-start(bf16[464,128]{1,0:T(8,128)(2,1)S(1)} %collective-permute-done.27.refs_0_), channel_id=1, source_target_pairs={{0,2},{1,3},{2,0},{3,1},{4,6},{5,7},{6,4},{7,5},{8,10},{9,11},{10,... | collective-permute-start | bytes 356360 | tf_op jit(solution)/shard_map/ppermute | solution.py:406
  101.6 8.1 %collective-permute-start.41 = (bf16[928,128]{1,0:T(8,128)(2,1)S(1)}, bf16[928,128]{1,0:T(8,128)(2,1)S(1)}, u32[]{:S(2)}, u32[]{:S(2)}) collective-permute-start(bf16[928,128]{1,0:T(8,128)(2,1)S(1)} %pad_maximum_fusion.4), channel_id=1, source_target_pairs={{0,1},{1,0},{2,3},{3,2},{4,5},{5,4},{6,7},{7,6},{8,9},{9,8},{10,11... | collective-permute-start | bytes 712712 | tf_op jit(solution)/shard_map/ppermute | solution.py:406
  102.0 7.8 %collective-permute-start.40 = (bf16[928,128]{1,0:T(8,128)(2,1)S(1)}, bf16[928,128]{1,0:T(8,128)(2,1)S(1)}, u32[]{:S(2)}, u32[]{:S(2)}) collective-permute-start(bf16[928,128]{1,0:T(8,128)(2,1)S(1)} %pad_maximum_fusion.3), channel_id=1, source_target_pairs={{0,1},{1,0},{2,3},{3,2},{4,5},{5,4},{6,7},{7,6},{8,9},{9,8},{10,11... | collective-permute-start | bytes 712712 | tf_op jit(solution)/shard_map/ppermute | solution.py:406
  106.2 5.2 %collective-permute-start.39 = (bf16[928,128]{1,0:T(8,128)(2,1)S(1)}, bf16[928,128]{1,0:T(8,128)(2,1)S(1)}, u32[]{:S(2)}, u32[]{:S(2)}) collective-permute-start(bf16[928,128]{1,0:T(8,128)(2,1)S(1)} %pad_maximum_fusion.2), channel_id=1, source_target_pairs={{0,1},{1,0},{2,3},{3,2},{4,5},{5,4},{6,7},{7,6},{8,9},{9,8},{10,11... | collective-permute-start | bytes 712712 | tf_op jit(solution)/shard_map/ppermute | solution.py:406
  107.1 4.4 %collective-permute-start.38 = (bf16[928,128]{1,0:T(8,128)(2,1)S(1)}, bf16[928,128]{1,0:T(8,128)(2,1)S(1)}, u32[]{:S(2)}, u32[]{:S(2)}) collective-permute-start(bf16[928,128]{1,0:T(8,128)(2,1)S(1)} %pad_maximum_fusion.1), channel_id=1, source_target_pairs={{0,1},{1,0},{2,3},{3,2},{4,5},{5,4},{6,7},{7,6},{8,9},{9,8},{10,11... | collective-permute-start | bytes 712712 | tf_op jit(solution)/shard_map/ppermute | solution.py:406
  107.2 6.0 %collective-permute-start.31 = (bf16[928,128]{1,0:T(8,128)(2,1)S(1)}, bf16[928,128]{1,0:T(8,128)(2,1)S(1)}, u32[]{:S(2)}, u32[]{:S(2)}) collective-permute-start(bf16[928,128]{1,0:T(8,128)(2,1)S(1)} %pad_maximum_fusion), channel_id=1, source_target_pairs={{0,1},{1,0},{2,3},{3,2},{4,5},{5,4},{6,7},{7,6},{8,9},{9,8},{10,11... | collective-permute-start | bytes 712712 | tf_op jit(solution)/shard_map/ppermute | solution.py:406

commit v4 on v3

--- a/solution.py
+++ b/solution.py
@@ -474,22 +474,22 @@
         joined = jnp.concatenate(pieces, 0)
         swapped.append(send(joined, PAIR))
 
-    def gather(which, before, last=False):
+    def gather(mine, theirs, before, last=False):
         arrays, places = [], []
-        for step in which:
+        for step in mine:
             for piece, spot in zip(steps[step], place_of[step]):
                 places.append((len(arrays), 0, False, *spot))
                 arrays.append(piece)
-        for step in which:
+        for step in theirs:
             for row, spot in zip((0, MSG), place_of[step]):
                 places.append((len(arrays), row, True, *spot))
             arrays.append(swapped[step])
         return assemble(place, arrays, tuple(places), before, last)
 
-    result = gather((0, 1, 2), None)
-    result = gather((3, 4), result)
-    result = gather((5, 6), result)
-    payload, scales = gather((7,), result, True)
+    result = gather((0, 1, 2), (0, 1, 2), None)
+    result = gather((3, 4), (3, 4), result)
+    result = gather((5, 6, 7), (5, 6), result)
+    payload, scales = gather((), (7,), result, True)
     return payload, scales.T
 
 

time: 117 us -> 117 us (level)
  no operation moved by 1% of the time
where the time goes in v4:
time: 117 us; the launch traced here: 115 us
  starting transfers between devices  57 us (49%)
  waiting for transfers between devices  33.7 us (29%)
  Pallas kernels  21 us (18%)
  other arithmetic  1.35 us (1%)
  local copies, waits for them, and re-layouts  1.17 us (1%)
    ppermute x39, starting transfers between devices, send(): return lax.ppermute(x, 'tp', pairs)  50 us
    ppermute x39, waiting for transfers between devices, send(): return lax.ppermute(x, 'tp', pairs)  24.8 us
    pallas_call x1, Pallas kernels, project(): pl.pallas_call(project_kernel, out_shape=(half,) * (2 * CHIPS - 2) + (ful...  9.75 us
    ppermute x6, waiting for transfers between devices, spread_out(): came = [lax.ppermute(x, ('ctx', 'tp'), way) for way in pairs]  8.94 us
    pallas_call x4, Pallas kernels, assemble(): pl.pallas_call(functools.partial(assemble_kernel, places, fresh, last), o...  7.48 us
    ppermute x6, starting transfers between devices, spread_out(): came = [lax.ppermute(x, ('ctx', 'tp'), way) for way in pairs]  7.06 us
    pallas_call x1, Pallas kernels, attention(): pl.pallas_call(attention_kernel, out_shape=jax.ShapeDtypeStruct((TOKENS,...  3.55 us
  transfers between devices with their start and end apart: 45, of which 23 were waited for; matrix products, arithmetic and copies ran while one was open for 1% of the time, Pallas kernels for 8%

profile of v4, /device:TPU:1, one launch (start us, length us, event | category | flops | bytes accessed | tf_op | source)
XLA Modules:
  0.0 115.5 jit_solution(9088176012762539225)
XLA Ops:
  0.6 3.3 %collective-permute-start.8 = (bf16[512,8192]{1,0:T(8,128)(2,1)}, bf16[512,8192]{1,0:T(8,128)(2,1)}, u32[]{:S(2)}, u32[]{:S(2)}) collective-permute-start(bf16[512,8192]{1,0:T(8,128)(2,1)} %own_hbm.1), channel_id=1, source_target_pairs={{0,1},{1,0},{2,3},{3,2},{4,5},{5,4},{6,7},{7,6},{8,9},{9,8},{10,11... | collective-permute-start | bytes 25165832 | tf_op jit(solution)/shard_map/ppermute | solution.py:406
  3.9 0.9 constant_dynamic-update-slice_fusion.6
  4.8 1.3 %collective-permute-start.2 = (bf16[224,128]{1,0:T(8,128)(2,1)S(1)}, bf16[224,128]{1,0:T(8,128)(2,1)S(1)}, u32[]{:S(2)}, u32[]{:S(2)}) collective-permute-start(bf16[224,128]{1,0:T(8,128)(2,1)S(1)} %get-tuple-element.101), channel_id=1, source_target_pairs={{0,32},{1,129},{2,34},{3,131},{4,36},{5,133},{6,38},{7,135},{8,40}... | collective-permute-start | bytes 172040 | tf_op jit(solution)/shard_map/ppermute | solution.py:420
  6.1 0.8 collective-permute-start.1
  6.9 0.7 collective-permute-start
  7.5 2.2 %collective-permute-done.2 = bf16[224,128]{1,0:T(8,128)(2,1)S(1)} collective-permute-done((bf16[224,128]{1,0:T(8,128)(2,1)S(1)}, bf16[224,128]{1,0:T(8,128)(2,1)S(1)}, u32[]{:S(2)}, u32[]{:S(2)}) %collective-permute-start.2) | collective-permute-done | bytes 57376 | tf_op jit(solution)/shard_map/ppermute | solution.py:420
  9.7 1.4 %collective-permute-done = bf16[224,128]{1,0:T(8,128)(2,1)S(1)} collective-permute-done((bf16[224,128]{1,0:T(8,128)(2,1)S(1)}, bf16[224,128]{1,0:T(8,128)(2,1)S(1)}, u32[]{:S(2)}, u32[]{:S(2)}) %collective-permute-start) | collective-permute-done | bytes 57376 | tf_op jit(solution)/shard_map/ppermute | solution.py:420
  11.1 2.8 %collective-permute-start.5 = (bf16[896,128]{1,0:T(8,128)(2,1)S(1)}, bf16[896,128]{1,0:T(8,128)(2,1)S(1)}, u32[]{:S(2)}, u32[]{:S(2)}) collective-permute-start(bf16[896,128]{1,0:T(8,128)(2,1)S(1)} %pad_maximum_fusion.8), channel_id=1, source_target_pairs={{0,128},{1,33},{2,130},{3,35},{4,132},{5,37},{6,134},{7,39},{8,136... | collective-permute-start | bytes 688136 | tf_op jit(solution)/shard_map/ppermute | solution.py:420
  13.9 0.9 collective-permute-start.4
  14.8 0.6 collective-permute-start.3
  15.5 5.4 %collective-permute-done.3 = bf16[896,128]{1,0:T(8,128)(2,1)S(1)} collective-permute-done((bf16[896,128]{1,0:T(8,128)(2,1)S(1)}, bf16[896,128]{1,0:T(8,128)(2,1)S(1)}, u32[]{:S(2)}, u32[]{:S(2)}) %collective-permute-start.3) | collective-permute-done | bytes 229408 | tf_op jit(solution)/shard_map/ppermute | solution.py:420
  21.0 3.5 %collective-permute-start.6 = (bf16[3584,128]{1,0:T(8,128)(2,1)S(1)}, bf16[3584,128]{1,0:T(8,128)(2,1)S(1)}, u32[]{:S(2)}, u32[]{:S(2)}) collective-permute-start(bf16[3584,128]{1,0:T(8,128)(2,1)S(1)} %constant_dynamic-update-slice_fusion.held_ref), channel_id=1, source_target_pairs={{0,1},{1,0},{2,3},{3,2},{4,5},{5,4},{6,7},{7,6},{8,9},{9,8},{10,11... | collective-permute-start | bytes 2752520 | tf_op jit(solution)/shard_map/ppermute | solution.py:406
  24.7 2.0 %collective-permute-done.6.swapped_ref = bf16[3584,128]{1,0:T(8,128)(2,1)S(1)} collective-permute-done((bf16[3584,128]{1,0:T(8,128)(2,1)S(1)}, bf16[3584,128]{1,0:T(8,128)(2,1)S(1)}, u32[]{:S(2)}, u32[]{:S(2)}) %collective-permute-start.6) | collective-permute-done | bytes 917536 | tf_op jit(solution)/shard_map/ppermute | solution.py:406
  26.7 0.9 copy-done.3
  27.6 3.6 %attend.1.mine_ref = bf16[224,512]{1,0:T(8,128)(2,1)S(1)} custom-call(s32[6]{0:T(128)S(1)} %stack.27.place_ref.index_ref, bf16[224,512]{1,0:T(8,128)(2,1)S(1)} %copy-done.3, bf16[3584,128]{1,0:T(8,128)(2,1)S(1)} %constant_dynamic-update-slice_fusion.held_ref, bf16[3584,128]{1,0:T(8,128)(2,1)S(1)} %collective-permute-done.6.swapped_ref), custom_call_target="tpu_custom_call" | custom-call | flops 1644167168 | bytes 3145728 | tf_op jit(solution)/shard_map/attend/pallas_call | solution.py:200
  31.2 0.5 collective-permute-start.7
  31.6 1.1 collective-permute-done.7.theirs_ref
  32.8 9.7 %project.1 = (bf16[448,128]{1,0:T(8,128)(2,1)S(1)}, bf16[448,128]{1,0:T(8,128)(2,1)S(1)}, bf16[448,128]{1,0:T(8,128)(2,1)S(1)}, bf16[448,128]{1,0:T(8,128)(2,1)S...) custom-call(s32[6]{0:T(128)S(1)} %stack.27.place_ref.index_ref, ...), custom_call_target="tpu_custom_call" | custom-call | flops 2348810240 | bytes 10485760 | tf_op jit(solution)/shard_map/project/pallas_call | solution.py:268
  42.5 5.7 %collective-permute-start.9 = (bf16[448,128]{1,0:T(8,128)(2,1)S(1)}, bf16[448,128]{1,0:T(8,128)(2,1)S(1)}, u32[]{:S(2)}, u32[]{:S(2)}) collective-permute-start(bf16[448,128]{1,0:T(8,128)(2,1)S(1)} %get-tuple-element.52), channel_id=1, source_target_pairs={{0,14},{1,15},{2,4},{3,5},{4,2},{5,3},{6,8},{7,9},{8,6},{9,7},{10,... | collective-permute-start | bytes 344072 | tf_op jit(solution)/shard_map/ppermute | solution.py:406
  48.2 1.5 %collective-permute-start.16 = (bf16[448,128]{1,0:T(8,128)(2,1)S(1)}, bf16[448,128]{1,0:T(8,128)(2,1)S(1)}, u32[]{:S(2)}, u32[]{:S(2)}) collective-permute-start(bf16[448,128]{1,0:T(8,128)(2,1)S(1)} %get-tuple-element.64), channel_id=1, source_target_pairs={{0,14},{1,15},{2,4},{3,5},{4,2},{5,3},{6,8},{7,9},{8,6},{9,7},{10,... | collective-permute-start | bytes 344072 | tf_op jit(solution)/shard_map/ppermute | solution.py:406
  49.6 0.7 collective-permute-start.17
  50.4 1.0 collective-permute-done.9
  51.3 0.9 collective-permute-done.10
  52.3 0.4 collective-permute-start.12
  52.7 1.3 %collective-permute-start.11 = (bf16[448,128]{1,0:T(8,128)(2,1)S(1)}, bf16[448,128]{1,0:T(8,128)(2,1)S(1)}, u32[]{:S(2)}, u32[]{:S(2)}) collective-permute-start(bf16[448,128]{1,0:T(8,128)(2,1)S(1)} %add_convert_fusion.9), channel_id=1, source_target_pairs={{0,14},{1,15},{2,4},{3,5},{4,2},{5,3},{6,8},{7,9},{8,6},{9,7},{10,... | collective-permute-start | bytes 344072 | tf_op jit(solution)/shard_map/ppermute | solution.py:406
  54.0 0.8 collective-permute-done.17
  55.0 1.5 %collective-permute-start.18 = (bf16[448,128]{1,0:T(8,128)(2,1)S(1)}, bf16[448,128]{1,0:T(8,128)(2,1)S(1)}, u32[]{:S(2)}, u32[]{:S(2)}) collective-permute-start(bf16[448,128]{1,0:T(8,128)(2,1)S(1)} %add_convert_fusion.4), channel_id=1, source_target_pairs={{0,14},{1,15},{2,4},{3,5},{4,2},{5,3},{6,8},{7,9},{8,6},{9,7},{10,... | collective-permute-start | bytes 344072 | tf_op jit(solution)/shard_map/ppermute | solution.py:406
  56.7 0.9 collective-permute-done.11
  58.0 1.3 %collective-permute-start.13 = (bf16[448,128]{1,0:T(8,128)(2,1)S(1)}, bf16[448,128]{1,0:T(8,128)(2,1)S(1)}, u32[]{:S(2)}, u32[]{:S(2)}) collective-permute-start(bf16[448,128]{1,0:T(8,128)(2,1)S(1)} %add_convert_fusion.7), channel_id=1, source_target_pairs={{0,14},{1,15},{2,4},{3,5},{4,2},{5,3},{6,8},{7,9},{8,6},{9,7},{10,... | collective-permute-start | bytes 344072 | tf_op jit(solution)/shard_map/ppermute | solution.py:406
  59.3 0.4 collective-permute-done.19
  59.7 1.4 %collective-permute-done.18 = bf16[448,128]{1,0:T(8,128)(2,1)S(1)} collective-permute-done((bf16[448,128]{1,0:T(8,128)(2,1)S(1)}, bf16[448,128]{1,0:T(8,128)(2,1)S(1)}, u32[]{:S(2)}, u32[]{:S(2)}) %collective-permute-start.18) | collective-permute-done | bytes 114720 | tf_op jit(solution)/shard_map/ppermute | solution.py:406
  61.1 1.0 collective-permute-start.21
  62.2 0.7 collective-permute-done.14
  62.9 1.0 collective-permute-done.13
  64.0 0.4 collective-permute-start.22
  64.4 1.3 %collective-permute-start.15 = (bf16[448,128]{1,0:T(8,128)(2,1)S(1)}, bf16[448,128]{1,0:T(8,128)(2,1)S(1)}, u32[]{:S(2)}, u32[]{:S(2)}) collective-permute-start(bf16[448,128]{1,0:T(8,128)(2,1)S(1)} %add_convert_fusion.5), channel_id=1, source_target_pairs={{0,14},{1,15},{2,4},{3,5},{4,2},{5,3},{6,8},{7,9},{8,6},{9,7},{10,... | collective-permute-start | bytes 344072 | tf_op jit(solution)/shard_map/ppermute | solution.py:406
  66.0 1.1 collective-permute-done.20.two0
  67.2 1.2 %collective-permute-done.22.two1 = bf16[448,128]{1,0:T(8,128)(2,1)S(1)} collective-permute-done((bf16[448,128]{1,0:T(8,128)(2,1)S(1)}, bf16[448,128]{1,0:T(8,128)(2,1)S(1)}, u32[]{:S(2)}, u32[]{:S(2)}) %collective-permute-start.22) | collective-permute-done | bytes 114720 | tf_op jit(solution)/shard_map/ppermute | solution.py:406
  68.3 1.5 %collective-permute-done.15.one0 = bf16[448,128]{1,0:T(8,128)(2,1)S(1)} collective-permute-done((bf16[448,128]{1,0:T(8,128)(2,1)S(1)}, bf16[448,128]{1,0:T(8,128)(2,1)S(1)}, u32[]{:S(2)}, u32[]{:S(2)}) %collective-permute-start.15) | collective-permute-done | bytes 114720 | tf_op jit(solution)/shard_map/ppermute | solution.py:406
  70.1 1.3 %collective-permute-start.23 = (bf16[464,128]{1,0:T(8,128)(2,1)S(1)}, bf16[464,128]{1,0:T(8,128)(2,1)S(1)}, u32[]{:S(2)}, u32[]{:S(2)}) collective-permute-start(bf16[464,128]{1,0:T(8,128)(2,1)S(1)} %get-tuple-element.87.refs_1_), channel_id=1, source_target_pairs={{0,14},{1,15},{2,4},{3,5},{4,2},{5,3},{6,8},{7,9},{8,6},{9,7},{10,... | collective-permute-start | bytes 356360 | tf_op jit(solution)/shard_map/ppermute | solution.py:406
  71.7 1.5 %collective-permute-start.32 = (bf16[464,128]{1,0:T(8,128)(2,1)S(1)}, bf16[464,128]{1,0:T(8,128)(2,1)S(1)}, u32[]{:S(2)}, u32[]{:S(2)}) collective-permute-start(bf16[464,128]{1,0:T(8,128)(2,1)S(1)} %get-tuple-element.77), channel_id=1, source_target_pairs={{0,14},{1,15},{2,4},{3,5},{4,2},{5,3},{6,8},{7,9},{8,6},{9,7},{10,... | collective-permute-start | bytes 356360 | tf_op jit(solution)/shard_map/ppermute | solution.py:406
  73.1 0.6 collective-permute-start.33
  73.7 2.0 %collective-permute-done.23.refs_2_ = bf16[464,128]{1,0:T(8,128)(2,1)S(1)} collective-permute-done((bf16[464,128]{1,0:T(8,128)(2,1)S(1)}, bf16[464,128]{1,0:T(8,128)(2,1)S(1)}, u32[]{:S(2)}, u32[]{:S(2)}) %collective-permute-start.23) | collective-permute-done | bytes 118816 | tf_op jit(solution)/shard_map/ppermute | solution.py:406
  75.8 1.4 %collective-permute-start.25 = (bf16[464,128]{1,0:T(8,128)(2,1)S(1)}, bf16[464,128]{1,0:T(8,128)(2,1)S(1)}, u32[]{:S(2)}, u32[]{:S(2)}) collective-permute-start(bf16[464,128]{1,0:T(8,128)(2,1)S(1)} %collective-permute-done.24.refs_3_), channel_id=1, source_target_pairs={{0,14},{1,15},{2,4},{3,5},{4,2},{5,3},{6,8},{7,9},{8,6},{9,7},{10,... | collective-permute-start | bytes 356360 | tf_op jit(solution)/shard_map/ppermute | solution.py:406
  77.1 7.3 %collective-permute-start.42 = (bf16[928,128]{1,0:T(8,128)(2,1)S(1)}, bf16[928,128]{1,0:T(8,128)(2,1)S(1)}, u32[]{:S(2)}, u32[]{:S(2)}) collective-permute-start(bf16[928,128]{1,0:T(8,128)(2,1)S(1)} %pad_maximum_fusion.5), channel_id=1, source_target_pairs={{0,1},{1,0},{2,3},{3,2},{4,5},{5,4},{6,7},{7,6},{8,9},{9,8},{10,11... | collective-permute-start | bytes 712712 | tf_op jit(solution)/shard_map/ppermute | solution.py:406
  84.5 1.4 %collective-permute-start.34 = (bf16[464,128]{1,0:T(8,128)(2,1)S(1)}, bf16[464,128]{1,0:T(8,128)(2,1)S(1)}, u32[]{:S(2)}, u32[]{:S(2)}) collective-permute-start(bf16[464,128]{1,0:T(8,128)(2,1)S(1)} %collective-permute-done.33.refs_5_), channel_id=1, source_target_pairs={{0,14},{1,15},{2,4},{3,5},{4,2},{5,3},{6,8},{7,9},{8,6},{9,7},{10,... | collective-permute-start | bytes 356360 | tf_op jit(solution)/shard_map/ppermute | solution.py:406
  85.8 1.1 collective-permute-start.35
  87.0 1.4 %collective-permute-start.27 = (bf16[464,128]{1,0:T(8,128)(2,1)S(1)}, bf16[464,128]{1,0:T(8,128)(2,1)S(1)}, u32[]{:S(2)}, u32[]{:S(2)}) collective-permute-start(bf16[464,128]{1,0:T(8,128)(2,1)S(1)} %collective-permute-done.26.refs_1_), channel_id=1, source_target_pairs={{0,14},{1,15},{2,4},{3,5},{4,2},{5,3},{6,8},{7,9},{8,6},{9,7},{10,... | collective-permute-start | bytes 356360 | tf_op jit(solution)/shard_map/ppermute | solution.py:406
  88.5 1.8 %collective-permute-done.34.refs_2_ = bf16[464,128]{1,0:T(8,128)(2,1)S(1)} collective-permute-done((bf16[464,128]{1,0:T(8,128)(2,1)S(1)}, bf16[464,128]{1,0:T(8,128)(2,1)S(1)}, u32[]{:S(2)}, u32[]{:S(2)}) %collective-permute-start.34) | collective-permute-done | bytes 118816 | tf_op jit(solution)/shard_map/ppermute | solution.py:406
  90.3 0.4 collective-permute-done.35.refs_3_
  90.6 1.4 %collective-permute-start.36 = (bf16[464,128]{1,0:T(8,128)(2,1)S(1)}, bf16[464,128]{1,0:T(8,128)(2,1)S(1)}, u32[]{:S(2)}, u32[]{:S(2)}) collective-permute-start(bf16[464,128]{1,0:T(8,128)(2,1)S(1)} %collective-permute-done.35.refs_3_), channel_id=1, source_target_pairs={{0,14},{1,15},{2,4},{3,5},{4,2},{5,3},{6,8},{7,9},{8,6},{9,7},{10,... | collective-permute-start | bytes 356360 | tf_op jit(solution)/shard_map/ppermute | solution.py:406
  92.1 1.4 %collective-permute-start.28 = (bf16[464,128]{1,0:T(8,128)(2,1)S(1)}, bf16[464,128]{1,0:T(8,128)(2,1)S(1)}, u32[]{:S(2)}, u32[]{:S(2)}) collective-permute-start(bf16[464,128]{1,0:T(8,128)(2,1)S(1)} %collective-permute-done.25.refs_0_), channel_id=1, source_target_pairs={{0,2},{1,3},{2,0},{3,1},{4,6},{5,7},{6,4},{7,5},{8,10},{9,11},{10,... | collective-permute-start | bytes 356360 | tf_op jit(solution)/shard_map/ppermute | solution.py:406
  93.5 2.5 %collective-permute-start.44 = (bf16[928,128]{1,0:T(8,128)(2,1)S(1)}, bf16[928,128]{1,0:T(8,128)(2,1)S(1)}, u32[]{:S(2)}, u32[]{:S(2)}) collective-permute-start(bf16[928,128]{1,0:T(8,128)(2,1)S(1)} %pad_maximum_fusion.7), channel_id=1, source_target_pairs={{0,1},{1,0},{2,3},{3,2},{4,5},{5,4},{6,7},{7,6},{8,9},{9,8},{10,11... | collective-permute-start | bytes 712712 | tf_op jit(solution)/shard_map/ppermute | solution.py:406
  96.0 2.0 %collective-permute-done.28.refs_1_ = bf16[464,128]{1,0:T(8,128)(2,1)S(1)} collective-permute-done((bf16[464,128]{1,0:T(8,128)(2,1)S(1)}, bf16[464,128]{1,0:T(8,128)(2,1)S(1)}, u32[]{:S(2)}, u32[]{:S(2)}) %collective-permute-start.28) | collective-permute-done | bytes 118816 | tf_op jit(solution)/shard_map/ppermute | solution.py:406
  98.0 2.2 %collective-permute-start.43 = (bf16[928,128]{1,0:T(8,128)(2,1)S(1)}, bf16[928,128]{1,0:T(8,128)(2,1)S(1)}, u32[]{:S(2)}, u32[]{:S(2)}) collective-permute-start(bf16[928,128]{1,0:T(8,128)(2,1)S(1)} %pad_maximum_fusion.6), channel_id=1, source_target_pairs={{0,1},{1,0},{2,3},{3,2},{4,5},{5,4},{6,7},{7,6},{8,9},{9,8},{10,11... | collective-permute-start | bytes 712712 | tf_op jit(solution)/shard_map/ppermute | solution.py:406
  100.2 1.3 %collective-permute-start.29 = (bf16[464,128]{1,0:T(8,128)(2,1)S(1)}, bf16[464,128]{1,0:T(8,128)(2,1)S(1)}, u32[]{:S(2)}, u32[]{:S(2)}) collective-permute-start(bf16[464,128]{1,0:T(8,128)(2,1)S(1)} %collective-permute-done.28.refs_1_), channel_id=1, source_target_pairs={{0,14},{1,15},{2,4},{3,5},{4,2},{5,3},{6,8},{7,9},{8,6},{9,7},{10,... | collective-permute-start | bytes 356360 | tf_op jit(solution)/shard_map/ppermute | solution.py:406
  101.6 0.4 collective-permute-start.41
  102.2 4.0 %collective-permute-done.29.refs_4_ = bf16[464,128]{1,0:T(8,128)(2,1)S(1)} collective-permute-done((bf16[464,128]{1,0:T(8,128)(2,1)S(1)}, bf16[464,128]{1,0:T(8,128)(2,1)S(1)}, u32[]{:S(2)}, u32[]{:S(2)}) %collective-permute-start.29) | collective-permute-done | bytes 118816 | tf_op jit(solution)/shard_map/ppermute | solution.py:406
  106.2 0.9 collective-permute-start.39
  107.2 0.5 collective-permute-start.31
  107.7 2.0 %assemble.4 = (bf16[224,8192]{1,0:T(8,128)(2,1)}, f32[8,2,4,256]{3,2,1,0:T(4,128)S(1)}) custom-call(s32[6]{0:T(128)S(1)} %stack.27.place_ref.index_ref, bf16[464,128]{1,0:T(8,128)(2,1)S(1)} %get-tuple-element.77, bf16[464,128]{1,0:T(8,128)(2,1)S(1)} %get-tuple-element.87.refs_1_, bf16[464,128]{1,0:T(8,128)(2,1)S(1)} %collective-permute-done.23.refs_2_, ...), custom_call_target="tpu_custom_call" | custom-call | flops 1048576 | bytes 4194304 | tf_op jit(solution)/shard_map/assemble/pallas_call | solution.py:383
  109.7 1.7 %assemble.5 = (bf16[224,8192]{1,0:T(8,128)(2,1)}, f32[8,2,4,256]{3,2,1,0:T(4,128)S(1)}) custom-call(s32[6]{0:T(128)S(1)} %stack.27.place_ref.index_ref, bf16[464,128]{1,0:T(8,128)(2,1)S(1)} %collective-permute-done.25.refs_0_, bf16[464,128]{1,0:T(8,128)(2,1)S(1)} %collective-permute-done.26.refs_1_, ...), custom_call_target="tpu_custom_call", output_to_operand_aliasing={{0}: (7, {})} | custom-call | flops 1048576 | bytes 4194304 | tf_op jit(solution)/shard_map/assemble/pallas_call | solution.py:383
  111.5 1.9 %assemble.6 = (bf16[224,8192]{1,0:T(8,128)(2,1)}, f32[8,2,4,256]{3,2,1,0:T(4,128)S(1)}) custom-call(s32[6]{0:T(128)S(1)} %stack.27.place_ref.index_ref, bf16[464,128]{1,0:T(8,128)(2,1)S(1)} %collective-permute-done.27.refs_0_, bf16[464,128]{1,0:T(8,128)(2,1)S(1)} %collective-permute-done.28.refs_1_, ...), custom_call_target="tpu_custom_call", output_to_operand_aliasing={{0}: (9, {})} | custom-call | flops 1048576 | bytes 4194304 | tf_op jit(solution)/shard_map/assemble/pallas_call | solution.py:383
  113.4 1.9 %assemble.7 = (bf16[224,8192]{1,0:T(8,128)(2,1)}, f32[64,224]{1,0:T(8,128)}) custom-call(s32[6]{0:T(128)S(1)} %stack.27.place_ref.index_ref, bf16[928,128]{1,0:T(8,128)(2,1)S(1)} %collective-permute-done.31.refs_0_, bf16[224,8192]{1,0:T(8,128)(2,1)} %get-tuple-element.96.refs_1_, ...), custom_call_target="tpu_custom_call", output_to_operand_aliasing={{0}: (2, {})} | custom-call | flops 1048576 | bytes 4194304 | tf_op jit(solution)/shard_map/assemble/pallas_call | solution.py:383
  (68 shorter events, 2.8 us)
Async XLA Ops:
  0.6 32.1 %collective-permute-start.8 = (bf16[512,8192]{1,0:T(8,128)(2,1)}, bf16[512,8192]{1,0:T(8,128)(2,1)}, u32[]{:S(2)}, u32[]{:S(2)}) collective-permute-start(bf16[512,8192]{1,0:T(8,128)(2,1)} %own_hbm.1), channel_id=1, source_target_pairs={{0,1},{1,0},{2,3},{3,2},{4,5},{5,4},{6,7},{7,6},{8,9},{9,8},{10,11... | collective-permute-start | bytes 25165832 | tf_op jit(solution)/shard_map/ppermute | solution.py:406
  4.8 4.9 %collective-permute-start.2 = (bf16[224,128]{1,0:T(8,128)(2,1)S(1)}, bf16[224,128]{1,0:T(8,128)(2,1)S(1)}, u32[]{:S(2)}, u32[]{:S(2)}) collective-permute-start(bf16[224,128]{1,0:T(8,128)(2,1)S(1)} %get-tuple-element.101), channel_id=1, source_target_pairs={{0,32},{1,129},{2,34},{3,131},{4,36},{5,133},{6,38},{7,135},{8,40}... | collective-permute-start | bytes 172040 | tf_op jit(solution)/shard_map/ppermute | solution.py:420
  6.1 3.6 %collective-permute-start.1 = (bf16[224,128]{1,0:T(8,128)(2,1)S(1)}, bf16[224,128]{1,0:T(8,128)(2,1)S(1)}, u32[]{:S(2)}, u32[]{:S(2)}) collective-permute-start(bf16[224,128]{1,0:T(8,128)(2,1)S(1)} %get-tuple-element.101), channel_id=1, source_target_pairs={{0,48},{1,193},{2,50},{3,195},{4,52},{5,197},{6,54},{7,199},{8,56}... | collective-permute-start | bytes 172040 | tf_op jit(solution)/shard_map/ppermute | solution.py:420
  6.9 4.2 %collective-permute-start = (bf16[224,128]{1,0:T(8,128)(2,1)S(1)}, bf16[224,128]{1,0:T(8,128)(2,1)S(1)}, u32[]{:S(2)}, u32[]{:S(2)}) collective-permute-start(bf16[224,128]{1,0:T(8,128)(2,1)S(1)} %get-tuple-element.101), channel_id=1, source_target_pairs={{0,16},{1,65},{2,18},{3,67},{4,20},{5,69},{6,22},{7,71},{8,24},{9,... | collective-permute-start | bytes 172040 | tf_op jit(solution)/shard_map/ppermute | solution.py:420
  11.1 9.9 %collective-permute-start.5 = (bf16[896,128]{1,0:T(8,128)(2,1)S(1)}, bf16[896,128]{1,0:T(8,128)(2,1)S(1)}, u32[]{:S(2)}, u32[]{:S(2)}) collective-permute-start(bf16[896,128]{1,0:T(8,128)(2,1)S(1)} %pad_maximum_fusion.8), channel_id=1, source_target_pairs={{0,128},{1,33},{2,130},{3,35},{4,132},{5,37},{6,134},{7,39},{8,136... | collective-permute-start | bytes 688136 | tf_op jit(solution)/shard_map/ppermute | solution.py:420
  13.9 7.0 %collective-permute-start.4 = (bf16[896,128]{1,0:T(8,128)(2,1)S(1)}, bf16[896,128]{1,0:T(8,128)(2,1)S(1)}, u32[]{:S(2)}, u32[]{:S(2)}) collective-permute-start(bf16[896,128]{1,0:T(8,128)(2,1)S(1)} %pad_maximum_fusion.8), channel_id=1, source_target_pairs={{0,192},{1,49},{2,194},{3,51},{4,196},{5,53},{6,198},{7,55},{8,200... | collective-permute-start | bytes 688136 | tf_op jit(solution)/shard_map/ppermute | solution.py:420
  14.8 6.1 %collective-permute-start.3 = (bf16[896,128]{1,0:T(8,128)(2,1)S(1)}, bf16[896,128]{1,0:T(8,128)(2,1)S(1)}, u32[]{:S(2)}, u32[]{:S(2)}) collective-permute-start(bf16[896,128]{1,0:T(8,128)(2,1)S(1)} %pad_maximum_fusion.8), channel_id=1, source_target_pairs={{0,64},{1,17},{2,66},{3,19},{4,68},{5,21},{6,70},{7,23},{8,72},{9,... | collective-permute-start | bytes 688136 | tf_op jit(solution)/shard_map/ppermute | solution.py:420
  15.5 17.3 %copy-start = (bf16[512,128]{1,0:T(8,128)(2,1)S(1)}, bf16[512,128]{1,0:T(8,128)(2,1)}, u32[]{:S(2)}) copy-start(bf16[512,128]{1,0:T(8,128)(2,1)} %constant.26.clone.gather_ref) | copy-start | bytes 393220
  15.5 17.3 %copy-start.1 = (bf16[256,256]{1,0:T(8,128)(2,1)S(1)}, bf16[256,256]{1,0:T(8,128)(2,1)}, u32[]{:S(2)}) copy-start(bf16[256,256]{1,0:T(8,128)(2,1)} %constant.25.clone.turn_ref) | copy-start | bytes 393220
  15.5 17.3 %copy-start.2 = (s32[8192]{0:T(1024)S(1)}, s32[8192]{0:T(1024)}, u32[]{:S(2)}) copy-start(s32[8192]{0:T(1024)} %param.11) | copy-start | bytes 98308
  21.0 5.6 %collective-permute-start.6 = (bf16[3584,128]{1,0:T(8,128)(2,1)S(1)}, bf16[3584,128]{1,0:T(8,128)(2,1)S(1)}, u32[]{:S(2)}, u32[]{:S(2)}) collective-permute-start(bf16[3584,128]{1,0:T(8,128)(2,1)S(1)} %constant_dynamic-update-slice_fusion.held_ref), channel_id=1, source_target_pairs={{0,1},{1,0},{2,3},{3,2},{4,5},{5,4},{6,7},{7,6},{8,9},{9,8},{10,11... | collective-permute-start | bytes 2752520 | tf_op jit(solution)/shard_map/ppermute | solution.py:406
  26.7 0.9 copy-start.3
  31.2 1.6 %collective-permute-start.7 = (bf16[224,512]{1,0:T(8,128)(2,1)S(1)}, bf16[224,512]{1,0:T(8,128)(2,1)S(1)}, u32[]{:S(2)}, u32[]{:S(2)}) collective-permute-start(bf16[224,512]{1,0:T(8,128)(2,1)S(1)} %attend.1.mine_ref), channel_id=1, source_target_pairs={{0,1},{1,0},{2,3},{3,2},{4,5},{5,4},{6,7},{7,6},{8,9},{9,8},{10,11... | collective-permute-start | bytes 688136 | tf_op jit(solution)/shard_map/ppermute | solution.py:406
  42.5 8.8 %collective-permute-start.9 = (bf16[448,128]{1,0:T(8,128)(2,1)S(1)}, bf16[448,128]{1,0:T(8,128)(2,1)S(1)}, u32[]{:S(2)}, u32[]{:S(2)}) collective-permute-start(bf16[448,128]{1,0:T(8,128)(2,1)S(1)} %get-tuple-element.52), channel_id=1, source_target_pairs={{0,14},{1,15},{2,4},{3,5},{4,2},{5,3},{6,8},{7,9},{8,6},{9,7},{10,... | collective-permute-start | bytes 344072 | tf_op jit(solution)/shard_map/ppermute | solution.py:406
  48.2 4.0 %collective-permute-start.10 = (bf16[448,128]{1,0:T(8,128)(2,1)S(1)}, bf16[448,128]{1,0:T(8,128)(2,1)S(1)}, u32[]{:S(2)}, u32[]{:S(2)}) collective-permute-start(bf16[448,128]{1,0:T(8,128)(2,1)S(1)} %get-tuple-element.53), channel_id=1, source_target_pairs={{0,2},{1,3},{2,0},{3,1},{4,6},{5,7},{6,4},{7,5},{8,10},{9,11},{10,... | collective-permute-start | bytes 344072 | tf_op jit(solution)/shard_map/ppermute | solution.py:406
  48.2 5.8 %collective-permute-start.16 = (bf16[448,128]{1,0:T(8,128)(2,1)S(1)}, bf16[448,128]{1,0:T(8,128)(2,1)S(1)}, u32[]{:S(2)}, u32[]{:S(2)}) collective-permute-start(bf16[448,128]{1,0:T(8,128)(2,1)S(1)} %get-tuple-element.64), channel_id=1, source_target_pairs={{0,14},{1,15},{2,4},{3,5},{4,2},{5,3},{6,8},{7,9},{8,6},{9,7},{10,... | collective-permute-start | bytes 344072 | tf_op jit(solution)/shard_map/ppermute | solution.py:406
  49.6 5.2 %collective-permute-start.17 = (bf16[448,128]{1,0:T(8,128)(2,1)S(1)}, bf16[448,128]{1,0:T(8,128)(2,1)S(1)}, u32[]{:S(2)}, u32[]{:S(2)}) collective-permute-start(bf16[448,128]{1,0:T(8,128)(2,1)S(1)} %get-tuple-element.65), channel_id=1, source_target_pairs={{0,2},{1,3},{2,0},{3,1},{4,6},{5,7},{6,4},{7,5},{8,10},{9,11},{10,... | collective-permute-start | bytes 344072 | tf_op jit(solution)/shard_map/ppermute | solution.py:406
  52.3 4.5 %collective-permute-start.12 = (bf16[448,128]{1,0:T(8,128)(2,1)S(1)}, bf16[448,128]{1,0:T(8,128)(2,1)S(1)}, u32[]{:S(2)}, u32[]{:S(2)}) collective-permute-start(bf16[448,128]{1,0:T(8,128)(2,1)S(1)} %add_convert_fusion.8), channel_id=1, source_target_pairs={{0,2},{1,3},{2,0},{3,1},{4,6},{5,7},{6,4},{7,5},{8,10},{9,11},{10,... | collective-permute-start | bytes 344072 | tf_op jit(solution)/shard_map/ppermute | solution.py:406
  52.7 4.9 %collective-permute-start.11 = (bf16[448,128]{1,0:T(8,128)(2,1)S(1)}, bf16[448,128]{1,0:T(8,128)(2,1)S(1)}, u32[]{:S(2)}, u32[]{:S(2)}) collective-permute-start(bf16[448,128]{1,0:T(8,128)(2,1)S(1)} %add_convert_fusion.9), channel_id=1, source_target_pairs={{0,14},{1,15},{2,4},{3,5},{4,2},{5,3},{6,8},{7,9},{8,6},{9,7},{10,... | collective-permute-start | bytes 344072 | tf_op jit(solution)/shard_map/ppermute | solution.py:406
  54.8 4.9 %collective-permute-start.19 = (bf16[448,128]{1,0:T(8,128)(2,1)S(1)}, bf16[448,128]{1,0:T(8,128)(2,1)S(1)}, u32[]{:S(2)}, u32[]{:S(2)}) collective-permute-start(bf16[448,128]{1,0:T(8,128)(2,1)S(1)} %add_convert_fusion.3), channel_id=1, source_target_pairs={{0,2},{1,3},{2,0},{3,1},{4,6},{5,7},{6,4},{7,5},{8,10},{9,11},{10,... | collective-permute-start | bytes 344072 | tf_op jit(solution)/shard_map/ppermute | solution.py:406
  55.0 6.1 %collective-permute-start.18 = (bf16[448,128]{1,0:T(8,128)(2,1)S(1)}, bf16[448,128]{1,0:T(8,128)(2,1)S(1)}, u32[]{:S(2)}, u32[]{:S(2)}) collective-permute-start(bf16[448,128]{1,0:T(8,128)(2,1)S(1)} %add_convert_fusion.4), channel_id=1, source_target_pairs={{0,14},{1,15},{2,4},{3,5},{4,2},{5,3},{6,8},{7,9},{8,6},{9,7},{10,... | collective-permute-start | bytes 344072 | tf_op jit(solution)/shard_map/ppermute | solution.py:406
  57.6 5.2 %collective-permute-start.14 = (bf16[448,128]{1,0:T(8,128)(2,1)S(1)}, bf16[448,128]{1,0:T(8,128)(2,1)S(1)}, u32[]{:S(2)}, u32[]{:S(2)}) collective-permute-start(bf16[448,128]{1,0:T(8,128)(2,1)S(1)} %add_convert_fusion.6), channel_id=1, source_target_pairs={{0,2},{1,3},{2,0},{3,1},{4,6},{5,7},{6,4},{7,5},{8,10},{9,11},{10,... | collective-permute-start | bytes 344072 | tf_op jit(solution)/shard_map/ppermute | solution.py:406
  58.0 5.9 %collective-permute-start.13 = (bf16[448,128]{1,0:T(8,128)(2,1)S(1)}, bf16[448,128]{1,0:T(8,128)(2,1)S(1)}, u32[]{:S(2)}, u32[]{:S(2)}) collective-permute-start(bf16[448,128]{1,0:T(8,128)(2,1)S(1)} %add_convert_fusion.7), channel_id=1, source_target_pairs={{0,14},{1,15},{2,4},{3,5},{4,2},{5,3},{6,8},{7,9},{8,6},{9,7},{10,... | collective-permute-start | bytes 344072 | tf_op jit(solution)/shard_map/ppermute | solution.py:406
  61.1 4.9 %collective-permute-start.21 = (bf16[448,128]{1,0:T(8,128)(2,1)S(1)}, bf16[448,128]{1,0:T(8,128)(2,1)S(1)}, u32[]{:S(2)}, u32[]{:S(2)}) collective-permute-start(bf16[448,128]{1,0:T(8,128)(2,1)S(1)} %add_convert_fusion.1), channel_id=1, source_target_pairs={{0,14},{1,15},{2,4},{3,5},{4,2},{5,3},{6,8},{7,9},{8,6},{9,7},{10,... | collective-permute-start | bytes 344072 | tf_op jit(solution)/shard_map/ppermute | solution.py:406
  62.1 5.0 %collective-permute-start.20 = (bf16[448,128]{1,0:T(8,128)(2,1)S(1)}, bf16[448,128]{1,0:T(8,128)(2,1)S(1)}, u32[]{:S(2)}, u32[]{:S(2)}) collective-permute-start(bf16[448,128]{1,0:T(8,128)(2,1)S(1)} %add_convert_fusion.2), channel_id=1, source_target_pairs={{0,2},{1,3},{2,0},{3,1},{4,6},{5,7},{6,4},{7,5},{8,10},{9,11},{10,... | collective-permute-start | bytes 344072 | tf_op jit(solution)/shard_map/ppermute | solution.py:406
  64.0 4.4 %collective-permute-start.22 = (bf16[448,128]{1,0:T(8,128)(2,1)S(1)}, bf16[448,128]{1,0:T(8,128)(2,1)S(1)}, u32[]{:S(2)}, u32[]{:S(2)}) collective-permute-start(bf16[448,128]{1,0:T(8,128)(2,1)S(1)} %add_convert_fusion), channel_id=1, source_target_pairs={{0,2},{1,3},{2,0},{3,1},{4,6},{5,7},{6,4},{7,5},{8,10},{9,11},{10,... | collective-permute-start | bytes 344072 | tf_op jit(solution)/shard_map/ppermute | solution.py:406
  64.4 5.5 %collective-permute-start.15 = (bf16[448,128]{1,0:T(8,128)(2,1)S(1)}, bf16[448,128]{1,0:T(8,128)(2,1)S(1)}, u32[]{:S(2)}, u32[]{:S(2)}) collective-permute-start(bf16[448,128]{1,0:T(8,128)(2,1)S(1)} %add_convert_fusion.5), channel_id=1, source_target_pairs={{0,14},{1,15},{2,4},{3,5},{4,2},{5,3},{6,8},{7,9},{8,6},{9,7},{10,... | collective-permute-start | bytes 344072 | tf_op jit(solution)/shard_map/ppermute | solution.py:406
  70.1 5.6 %collective-permute-start.23 = (bf16[464,128]{1,0:T(8,128)(2,1)S(1)}, bf16[464,128]{1,0:T(8,128)(2,1)S(1)}, u32[]{:S(2)}, u32[]{:S(2)}) collective-permute-start(bf16[464,128]{1,0:T(8,128)(2,1)S(1)} %get-tuple-element.87.refs_1_), channel_id=1, source_target_pairs={{0,14},{1,15},{2,4},{3,5},{4,2},{5,3},{6,8},{7,9},{8,6},{9,7},{10,... | collective-permute-start | bytes 356360 | tf_op jit(solution)/shard_map/ppermute | solution.py:406
  71.4 4.3 %collective-permute-start.24 = (bf16[464,128]{1,0:T(8,128)(2,1)S(1)}, bf16[464,128]{1,0:T(8,128)(2,1)S(1)}, u32[]{:S(2)}, u32[]{:S(2)}) collective-permute-start(bf16[464,128]{1,0:T(8,128)(2,1)S(1)} %get-tuple-element.77), channel_id=1, source_target_pairs={{0,2},{1,3},{2,0},{3,1},{4,6},{5,7},{6,4},{7,5},{8,10},{9,11},{10,... | collective-permute-start | bytes 356360 | tf_op jit(solution)/shard_map/ppermute | solution.py:406
  71.7 12.8 %collective-permute-start.32 = (bf16[464,128]{1,0:T(8,128)(2,1)S(1)}, bf16[464,128]{1,0:T(8,128)(2,1)S(1)}, u32[]{:S(2)}, u32[]{:S(2)}) collective-permute-start(bf16[464,128]{1,0:T(8,128)(2,1)S(1)} %get-tuple-element.77), channel_id=1, source_target_pairs={{0,14},{1,15},{2,4},{3,5},{4,2},{5,3},{6,8},{7,9},{8,6},{9,7},{10,... | collective-permute-start | bytes 356360 | tf_op jit(solution)/shard_map/ppermute | solution.py:406
  73.1 11.3 %collective-permute-start.33 = (bf16[464,128]{1,0:T(8,128)(2,1)S(1)}, bf16[464,128]{1,0:T(8,128)(2,1)S(1)}, u32[]{:S(2)}, u32[]{:S(2)}) collective-permute-start(bf16[464,128]{1,0:T(8,128)(2,1)S(1)} %get-tuple-element.87.refs_1_), channel_id=1, source_target_pairs={{0,2},{1,3},{2,0},{3,1},{4,6},{5,7},{6,4},{7,5},{8,10},{9,11},{10,... | collective-permute-start | bytes 356360 | tf_op jit(solution)/shard_map/ppermute | solution.py:406
  75.8 11.2 %collective-permute-start.25 = (bf16[464,128]{1,0:T(8,128)(2,1)S(1)}, bf16[464,128]{1,0:T(8,128)(2,1)S(1)}, u32[]{:S(2)}, u32[]{:S(2)}) collective-permute-start(bf16[464,128]{1,0:T(8,128)(2,1)S(1)} %collective-permute-done.24.refs_3_), channel_id=1, source_target_pairs={{0,14},{1,15},{2,4},{3,5},{4,2},{5,3},{6,8},{7,9},{8,6},{9,7},{10,... | collective-permute-start | bytes 356360 | tf_op jit(solution)/shard_map/ppermute | solution.py:406
  77.1 9.9 %collective-permute-start.26 = (bf16[464,128]{1,0:T(8,128)(2,1)S(1)}, bf16[464,128]{1,0:T(8,128)(2,1)S(1)}, u32[]{:S(2)}, u32[]{:S(2)}) collective-permute-start(bf16[464,128]{1,0:T(8,128)(2,1)S(1)} %collective-permute-done.23.refs_2_), channel_id=1, source_target_pairs={{0,2},{1,3},{2,0},{3,1},{4,6},{5,7},{6,4},{7,5},{8,10},{9,11},{10,... | collective-permute-start | bytes 356360 | tf_op jit(solution)/shard_map/ppermute | solution.py:406
  77.1 24.4 %collective-permute-start.42 = (bf16[928,128]{1,0:T(8,128)(2,1)S(1)}, bf16[928,128]{1,0:T(8,128)(2,1)S(1)}, u32[]{:S(2)}, u32[]{:S(2)}) collective-permute-start(bf16[928,128]{1,0:T(8,128)(2,1)S(1)} %pad_maximum_fusion.5), channel_id=1, source_target_pairs={{0,1},{1,0},{2,3},{3,2},{4,5},{5,4},{6,7},{7,6},{8,9},{9,8},{10,11... | collective-permute-start | bytes 712712 | tf_op jit(solution)/shard_map/ppermute | solution.py:406
  84.5 5.8 %collective-permute-start.34 = (bf16[464,128]{1,0:T(8,128)(2,1)S(1)}, bf16[464,128]{1,0:T(8,128)(2,1)S(1)}, u32[]{:S(2)}, u32[]{:S(2)}) collective-permute-start(bf16[464,128]{1,0:T(8,128)(2,1)S(1)} %collective-permute-done.33.refs_5_), channel_id=1, source_target_pairs={{0,14},{1,15},{2,4},{3,5},{4,2},{5,3},{6,8},{7,9},{8,6},{9,7},{10,... | collective-permute-start | bytes 356360 | tf_op jit(solution)/shard_map/ppermute | solution.py:406
  85.8 4.8 %collective-permute-start.35 = (bf16[464,128]{1,0:T(8,128)(2,1)S(1)}, bf16[464,128]{1,0:T(8,128)(2,1)S(1)}, u32[]{:S(2)}, u32[]{:S(2)}) collective-permute-start(bf16[464,128]{1,0:T(8,128)(2,1)S(1)} %collective-permute-done.32.refs_4_), channel_id=1, source_target_pairs={{0,2},{1,3},{2,0},{3,1},{4,6},{5,7},{6,4},{7,5},{8,10},{9,11},{10,... | collective-permute-start | bytes 356360 | tf_op jit(solution)/shard_map/ppermute | solution.py:406
  87.0 6.5 %collective-permute-start.27 = (bf16[464,128]{1,0:T(8,128)(2,1)S(1)}, bf16[464,128]{1,0:T(8,128)(2,1)S(1)}, u32[]{:S(2)}, u32[]{:S(2)}) collective-permute-start(bf16[464,128]{1,0:T(8,128)(2,1)S(1)} %collective-permute-done.26.refs_1_), channel_id=1, source_target_pairs={{0,14},{1,15},{2,4},{3,5},{4,2},{5,3},{6,8},{7,9},{8,6},{9,7},{10,... | collective-permute-start | bytes 356360 | tf_op jit(solution)/shard_map/ppermute | solution.py:406
  90.6 9.6 %collective-permute-start.36 = (bf16[464,128]{1,0:T(8,128)(2,1)S(1)}, bf16[464,128]{1,0:T(8,128)(2,1)S(1)}, u32[]{:S(2)}, u32[]{:S(2)}) collective-permute-start(bf16[464,128]{1,0:T(8,128)(2,1)S(1)} %collective-permute-done.35.refs_3_), channel_id=1, source_target_pairs={{0,14},{1,15},{2,4},{3,5},{4,2},{5,3},{6,8},{7,9},{8,6},{9,7},{10,... | collective-permute-start | bytes 356360 | tf_op jit(solution)/shard_map/ppermute | solution.py:406
  92.0 9.5 %collective-permute-start.37 = (bf16[464,128]{1,0:T(8,128)(2,1)S(1)}, bf16[464,128]{1,0:T(8,128)(2,1)S(1)}, u32[]{:S(2)}, u32[]{:S(2)}) collective-permute-start(bf16[464,128]{1,0:T(8,128)(2,1)S(1)} %collective-permute-done.34.refs_2_), channel_id=1, source_target_pairs={{0,2},{1,3},{2,0},{3,1},{4,6},{5,7},{6,4},{7,5},{8,10},{9,11},{10,... | collective-permute-start | bytes 356360 | tf_op jit(solution)/shard_map/ppermute | solution.py:406
  92.1 5.9 %collective-permute-start.28 = (bf16[464,128]{1,0:T(8,128)(2,1)S(1)}, bf16[464,128]{1,0:T(8,128)(2,1)S(1)}, u32[]{:S(2)}, u32[]{:S(2)}) collective-permute-start(bf16[464,128]{1,0:T(8,128)(2,1)S(1)} %collective-permute-done.25.refs_0_), channel_id=1, source_target_pairs={{0,2},{1,3},{2,0},{3,1},{4,6},{5,7},{6,4},{7,5},{8,10},{9,11},{10,... | collective-permute-start | bytes 356360 | tf_op jit(solution)/shard_map/ppermute | solution.py:406
  93.5 8.4 %collective-permute-start.44 = (bf16[928,128]{1,0:T(8,128)(2,1)S(1)}, bf16[928,128]{1,0:T(8,128)(2,1)S(1)}, u32[]{:S(2)}, u32[]{:S(2)}) collective-permute-start(bf16[928,128]{1,0:T(8,128)(2,1)S(1)} %pad_maximum_fusion.7), channel_id=1, source_target_pairs={{0,1},{1,0},{2,3},{3,2},{4,5},{5,4},{6,7},{7,6},{8,9},{9,8},{10,11... | collective-permute-start | bytes 712712 | tf_op jit(solution)/shard_map/ppermute | solution.py:406
  98.0 9.2 %collective-permute-start.43 = (bf16[928,128]{1,0:T(8,128)(2,1)S(1)}, bf16[928,128]{1,0:T(8,128)(2,1)S(1)}, u32[]{:S(2)}, u32[]{:S(2)}) collective-permute-start(bf16[928,128]{1,0:T(8,128)(2,1)S(1)} %pad_maximum_fusion.6), channel_id=1, source_target_pairs={{0,1},{1,0},{2,3},{3,2},{4,5},{5,4},{6,7},{7,6},{8,9},{9,8},{10,11... | collective-permute-start | bytes 712712 | tf_op jit(solution)/shard_map/ppermute | solution.py:406
  100.2 6.0 %collective-permute-start.29 = (bf16[464,128]{1,0:T(8,128)(2,1)S(1)}, bf16[464,128]{1,0:T(8,128)(2,1)S(1)}, u32[]{:S(2)}, u32[]{:S(2)}) collective-permute-start(bf16[464,128]{1,0:T(8,128)(2,1)S(1)} %collective-permute-done.28.refs_1_), channel_id=1, source_target_pairs={{0,14},{1,15},{2,4},{3,5},{4,2},{5,3},{6,8},{7,9},{8,6},{9,7},{10,... | collective-permute-start | bytes 356360 | tf_op jit(solution)/shard_map/ppermute | solution.py:406
  101.5 5.6 %collective-permute-start.30 = (bf16[464,128]{1,0:T(8,128)(2,1)S(1)}, bf16[464,128]{1,0:T(8,128)(2,1)S(1)}, u32[]{:S(2)}, u32[]{:S(2)}) collective-permute-start(bf16[464,128]{1,0:T(8,128)(2,1)S(1)} %collective-permute-done.27.refs_0_), channel_id=1, source_target_pairs={{0,2},{1,3},{2,0},{3,1},{4,6},{5,7},{6,4},{7,5},{8,10},{9,11},{10,... | collective-permute-start | bytes 356360 | tf_op jit(solution)/shard_map/ppermute | solution.py:406
  101.6 8.1 %collective-permute-start.41 = (bf16[928,128]{1,0:T(8,128)(2,1)S(1)}, bf16[928,128]{1,0:T(8,128)(2,1)S(1)}, u32[]{:S(2)}, u32[]{:S(2)}) collective-permute-start(bf16[928,128]{1,0:T(8,128)(2,1)S(1)} %pad_maximum_fusion.4), channel_id=1, source_target_pairs={{0,1},{1,0},{2,3},{3,2},{4,5},{5,4},{6,7},{7,6},{8,9},{9,8},{10,11... | collective-permute-start | bytes 712712 | tf_op jit(solution)/shard_map/ppermute | solution.py:406
  102.0 7.8 %collective-permute-start.40 = (bf16[928,128]{1,0:T(8,128)(2,1)S(1)}, bf16[928,128]{1,0:T(8,128)(2,1)S(1)}, u32[]{:S(2)}, u32[]{:S(2)}) collective-permute-start(bf16[928,128]{1,0:T(8,128)(2,1)S(1)} %pad_maximum_fusion.3), channel_id=1, source_target_pairs={{0,1},{1,0},{2,3},{3,2},{4,5},{5,4},{6,7},{7,6},{8,9},{9,8},{10,11... | collective-permute-start | bytes 712712 | tf_op jit(solution)/shard_map/ppermute | solution.py:406
  106.2 5.2 %collective-permute-start.39 = (bf16[928,128]{1,0:T(8,128)(2,1)S(1)}, bf16[928,128]{1,0:T(8,128)(2,1)S(1)}, u32[]{:S(2)}, u32[]{:S(2)}) collective-permute-start(bf16[928,128]{1,0:T(8,128)(2,1)S(1)} %pad_maximum_fusion.2), channel_id=1, source_target_pairs={{0,1},{1,0},{2,3},{3,2},{4,5},{5,4},{6,7},{7,6},{8,9},{9,8},{10,11... | collective-permute-start | bytes 712712 | tf_op jit(solution)/shard_map/ppermute | solution.py:406
  107.1 4.4 %collective-permute-start.38 = (bf16[928,128]{1,0:T(8,128)(2,1)S(1)}, bf16[928,128]{1,0:T(8,128)(2,1)S(1)}, u32[]{:S(2)}, u32[]{:S(2)}) collective-permute-start(bf16[928,128]{1,0:T(8,128)(2,1)S(1)} %pad_maximum_fusion.1), channel_id=1, source_target_pairs={{0,1},{1,0},{2,3},{3,2},{4,5},{5,4},{6,7},{7,6},{8,9},{9,8},{10,11... | collective-permute-start | bytes 712712 | tf_op jit(solution)/shard_map/ppermute | solution.py:406
  107.2 6.1 %collective-permute-start.31 = (bf16[928,128]{1,0:T(8,128)(2,1)S(1)}, bf16[928,128]{1,0:T(8,128)(2,1)S(1)}, u32[]{:S(2)}, u32[]{:S(2)}) collective-permute-start(bf16[928,128]{1,0:T(8,128)(2,1)S(1)} %pad_maximum_fusion), channel_id=1, source_target_pairs={{0,1},{1,0},{2,3},{3,2},{4,5},{5,4},{6,7},{7,6},{8,9},{9,8},{10,11... | collective-permute-start | bytes 712712 | tf_op jit(solution)/shard_map/ppermute | solution.py:406
